TPU v7x, 256 devices: a whole 4x4x8 slice. The times are simulated.
256 devices in a mesh: col: 32 (over x, y, core), row: 8 (over z).
Axes of the slice: x: 4, y: 4, z: 8, core: 2. Of those that a mesh axis runs over, the one named last changes fastest.
Arguments:
- weights: float32 [4096, 53248], P('row', 'col'), may hold values from -6 to 6
- factor: float32 [6, 512, 53248], P(None, 'row', 'col'), as said below
- diag_inverse: float32 [6, 4, 128, 128], replicated
- prune_mask: int32 [6, 32, 4], P(None, 'row'), may hold values 0 or 1
- panel_start: int32 [6], replicated, may hold values from 0 to 52736, as said below
Outputs:
- pruned: float32 [4096, 53248], P('row', 'col')
Inputs may be any that keep to these rules, and one draw needn't show every extreme that they name: `panel_start`: strictly increasing; each a multiple of 128; each panel lies within one block of 1664 columns, and no two panels in the same block. `factor`: row j of panel k is zero left of column panel_start[k] + j and positive on it.
All inputs are finite; a program needn't handle non-finite values. No bound on the sum of `prune_mask` on one device may be relied on, other than what follows from the above.
Results may differ from a plain program's by a relative error of at most 0.0001.
Values sent between devices are 32-bit elements; how exact they have to be, the bound alone decides.
No kernel may reach another device: no remote copies, remote signals or barrier semaphores. Data moves between devices by JAX's collectives and lax.ppermute only.
A program may use at most 192 MiB of HBM per device.

v0:
```python
import jax
import jax.numpy as jnp
from jax import lax
from jax.sharding import Mesh
from jax.sharding import PartitionSpec as P

TILE = 128
PANEL_TILES = 4
PW = 512
P_SIZE = 6
COL = ("col_0", "col_1", "col_2")


def cut_along(value, dim, devices):
    dims = value.shape
    tiles = value.reshape(*dims[:dim], devices, dims[dim] // devices, *dims[dim + 1 :])
    return jnp.moveaxis(tiles, dim, 0)


def sent_and_summed(value, axis, dim):
    tiles = cut_along(value, dim, lax.axis_size(axis))
    arrived = lax.all_to_all(tiles, axis, split_axis=0, concat_axis=0, tiled=True)
    return arrived.sum(axis=0)


def summed_rows(value, axes, dim):
    far, near = axes
    own = sent_and_summed(cut_along(value, dim, lax.axis_size(far)), near, dim + 1)
    return jnp.sum(lax.all_to_all(own, far, 0, 0, tiled=True), axis=0)


def filled_up(lines, devices):
    spare = -lines.shape[0] % devices
    if not spare:
        return lines
    return jnp.concatenate([lines, jnp.zeros((spare, *lines.shape[1:]), lines.dtype)])


def sent_to_all(value, axis):
    devices = lax.axis_size(axis)
    return lax.all_to_all(
        jnp.broadcast_to(value[None], (devices, *value.shape)), axis, 0, 0, tiled=True
    )


def laid_out(tiles, dim):
    dims = list(tiles.shape[1:])
    dims[dim] *= tiles.shape[0]
    return jnp.moveaxis(tiles, 0, dim).reshape(dims)


def gathered_by_axis(value, axes, dim):
    far, near = axes
    leading = sent_to_all(value, far)
    tiles = jnp.swapaxes(sent_to_all(leading, near), 0, 1)
    return laid_out(tiles.reshape(-1, *value.shape), dim)


def nested_sum(value, axes):
    lines = value.reshape(-1, value.shape[-1])
    own = summed_rows(filled_up(lines, lax.axis_size(axes[0]) * lax.axis_size(axes[1])), axes, 0)
    whole = gathered_by_axis(own, axes, 0)
    return whole[: len(lines)].reshape(value.shape)


def panel_errors(wpanel, ublock, dinv, rowmask):
    tiles = []
    for a in range(PANEL_TILES):
        acc = wpanel[:, a * TILE : (a + 1) * TILE]
        for b in range(a):
            acc = acc - jnp.dot(
                tiles[b],
                ublock[b * TILE : (b + 1) * TILE, a * TILE : (a + 1) * TILE],
                precision=lax.Precision.HIGHEST,
            )
        tiles.append(rowmask[:, a : a + 1] * jnp.dot(acc, dinv[a], precision=lax.Precision.HIGHEST))
    return jnp.concatenate(tiles, 1)


def shards(weights, factor, diag_inverse, prune_mask, panel_start):
    width = weights.shape[1]
    myself = lax.axis_index(COL)
    starts = TILE * jnp.arange(PANEL_TILES, dtype=jnp.int32)
    all_rows = lax.all_gather(factor, "row", axis=1, tiled=True)
    for k in range(P_SIZE):
        first = panel_start[k]
        owner = first // width
        shift_col = jnp.clip(first - myself * width, 0, width - PW)
        wpanel = lax.dynamic_slice_in_dim(weights, shift_col, PW, 1)
        rows_k = all_rows[k]
        ublock = lax.dynamic_slice_in_dim(rows_k, shift_col, PW, 1)
        rowmask = jnp.repeat(prune_mask[k].astype(jnp.float32), TILE, axis=0)
        errors = panel_errors(wpanel, ublock, diag_inverse[k], rowmask)
        owned = jnp.where(myself == owner, errors, jnp.zeros_like(errors))
        errors = nested_sum(owned, (("col_0", "col_1"), "col_2"))
        weights = weights - jnp.dot(errors, rows_k, precision=lax.Precision.HIGHEST)
        offset = myself * width + jnp.arange(width, dtype=jnp.int32) - first
        indicator = (
            (offset[None, :] >= starts[:, None]) & (offset[None, :] < starts[:, None] + TILE)
        ).astype(jnp.float32)
        prune = jnp.dot(rowmask, indicator, precision=lax.Precision.HIGHEST)
        weights = weights * (1.0 - prune)
    return weights


def solution(mesh):
    torus = Mesh(
        mesh.devices.reshape(4, 4, 2, mesh.shape["row"]), ("col_0", "col_1", "col_2", "row")
    )
    return jax.shard_map(
        shards,
        mesh=torus,
        in_specs=(P("row", COL), P(None, "row", COL), P(), P(None, "row", None), P()),
        out_specs=P("row", COL),
        check_vma=False,
    )
```

profile of v0, /device:TPU:1, one launch (start us, length us, event | category | flops | bytes accessed | tf_op | source)
XLA Modules:
  0.0 636.3 jit_solution(11401464521342157056)
XLA Ops:
  14.8 205.1 %all-gather.2.cloned.1.call-done = f32[6,512,1664]{2,1,0:T(8,128)} async-done(((f32[6,64,1664]{2,1,0:T(8,128)}), f32[6,512,1664]{2,1,0:T(8,128)}) %all-gather.2.cloned.1.call-update) | async-done | bytes 20447248 | tf_op jit(solution)/shard_map/all_gather | solution.py:84
  219.9 12.4 %fusion.180 = (f32[1,512,1664]{2,1,0:T(8,128)}, f32[1,512,1664]{2,1,0:T(8,128)}, f32[1,512,1664]{2,1,0:T(8,128)}, f32[1,512,1664]{2,1,0:T(8,128)}, f32[1,512,1664]{2,1,0:T(8,128)S(1)}, /*index=5*/f32[1,512,1664]{2,1,0:T(8,128)S(1)}) fusion(f32[6,512,1664]{2,1,0:T(8,128)} %all-gather.2.cloned.1.call-done), kind=kLoop, calls=%fused_computation.273 | loop fusion | bytes 40894464 | tf_op jit(solution)/shard_map/slice | solution.py:90
  243.0 5.0 all_to_all.120
  248.9 6.5 %all-to-all-start.1 = ((f32[16,16,512]{2,1,0:T(8,128)}), f32[16,16,512]{2,1,0:T(8,128)S(1)}, u32[]{:S(2)}, u32[]{:S(2)}) async-start(f32[16,16,512]{2,1,0:T(8,128)} %reduce_sum.108), calls=%async_computation.1 | async-start | bytes 1048576 | tf_op jit(solution)/shard_map/all_to_all | solution.py:29
  258.4 7.5 %all-to-all-done.1 = f32[16,16,512]{2,1,0:T(8,128)S(1)} async-done(((f32[16,16,512]{2,1,0:T(8,128)}), f32[16,16,512]{2,1,0:T(8,128)S(1)}, u32[]{:S(2)}, u32[]{:S(2)}) %all-to-all-start.1) | async-done | bytes 524320 | tf_op jit(solution)/shard_map/all_to_all | solution.py:29
  266.7 3.7 all-to-all-start.2
  270.5 3.3 fusion.140
  273.8 5.9 all-to-all-done.2
  279.8 7.8 %all_to_all.121 = f32[2,16,16,512]{3,2,1,0:T(8,128)S(1)} all-to-all(f32[2,16,16,512]{3,2,1,0:T(8,128)S(1)} %broadcast_in_dim.38), channel_id=1, replica_groups=mesh['col_0'=4,'col_1'=4,'col_2'=2,'row'=8] {'col_2'}, dimensions={0} | all-to-all | bytes 2097152 | tf_op jit(solution)/shard_map/all_to_all | solution.py:41
  287.8 9.1 %bitcast_multiply_fusion.5 = f32[512,1664]{1,0:T(8,128)S(1)} fusion(f32[1664,512]{0,1:T(8,128)S(1)} %copy-done.8, f32[512,1664]{1,0:T(8,128)} %param.5, f32[512,512]{1,0:T(8,128)S(1)} %bitcast.335, f32[6,512,1664]{2,1,0:T(8,128)} %all-gather.2.cloned.1.call-done), kind=kOutput, calls=%fused_computation.15 | convolution fusion | flops 5237047296 | bytes 14680064 | tf_op jit(solution)/shard_map/dot_general | solution.py:96
  309.2 5.4 all_to_all.122
  316.7 4.2 all-to-all-start.5
  321.2 10.0 %all-to-all-done.5 = f32[16,16,512]{2,1,0:T(8,128)} async-done(((f32[16,16,512]{2,1,0:T(8,128)}), f32[16,16,512]{2,1,0:T(8,128)}, u32[]{:S(2)}, u32[]{:S(2)}) %all-to-all-start.5) | async-done | bytes 524320 | tf_op jit(solution)/shard_map/all_to_all | solution.py:29
  333.1 4.7 all-to-all-start.6
  345.0 3.5 dynamic-slice_bitcast_fusion.2
  349.9 6.4 %all_to_all.123 = f32[2,16,16,512]{3,2,1,0:T(8,128)S(1)} all-to-all(f32[2,16,16,512]{3,2,1,0:T(8,128)S(1)} %broadcast_in_dim.41), channel_id=1, replica_groups=mesh['col_0'=4,'col_1'=4,'col_2'=2,'row'=8] {'col_2'}, dimensions={0} | all-to-all | bytes 2097152 | tf_op jit(solution)/shard_map/all_to_all | solution.py:41
  356.4 8.1 %bitcast_multiply_fusion.4 = f32[512,1664]{1,0:T(8,128)S(1)} fusion(f32[1664,512]{0,1:T(8,128)S(1)} %copy-done.7, f32[512,1664]{1,0:T(8,128)S(1)} %bitcast_multiply_fusion.5, f32[512,512]{1,0:T(8,128)S(1)} %bitcast.331, f32[6,512,1664]{2,1,0:T(8,128)} %all-gather.2.cloned.1.call-done), kind=kOutput, calls=%fused_computation.12 | convolution fusion | flops 5237047296 | bytes 14680064 | tf_op jit(solution)/shard_map/dot_general | solution.py:96
  376.9 4.6 all_to_all.124
  382.3 7.2 %all-to-all-start.9 = ((f32[16,16,512]{2,1,0:T(8,128)}), f32[16,16,512]{2,1,0:T(8,128)S(1)}, u32[]{:S(2)}, u32[]{:S(2)}) async-start(f32[16,16,512]{2,1,0:T(8,128)} %reduce_sum.112), calls=%async_computation.9 | async-start | bytes 1048576 | tf_op jit(solution)/shard_map/all_to_all | solution.py:29
  392.3 7.6 %all-to-all-done.9 = f32[16,16,512]{2,1,0:T(8,128)S(1)} async-done(((f32[16,16,512]{2,1,0:T(8,128)}), f32[16,16,512]{2,1,0:T(8,128)S(1)}, u32[]{:S(2)}, u32[]{:S(2)}) %all-to-all-start.9) | async-done | bytes 524320 | tf_op jit(solution)/shard_map/all_to_all | solution.py:29
  400.9 3.7 all-to-all-start.10
  404.6 3.3 fusion.132
  408.0 5.9 all-to-all-done.10
  414.0 7.7 %all_to_all.125 = f32[2,16,16,512]{3,2,1,0:T(8,128)S(1)} all-to-all(f32[2,16,16,512]{3,2,1,0:T(8,128)S(1)} %broadcast_in_dim.44), channel_id=1, replica_groups=mesh['col_0'=4,'col_1'=4,'col_2'=2,'row'=8] {'col_2'}, dimensions={0} | all-to-all | bytes 2097152 | tf_op jit(solution)/shard_map/all_to_all | solution.py:41
  421.7 9.1 %bitcast_multiply_fusion.3 = f32[512,1664]{1,0:T(8,128)S(1)} fusion(f32[1664,512]{0,1:T(8,128)} %fusion.132, f32[512,1664]{1,0:T(8,128)S(1)} %copy-done.3, f32[512,512]{1,0:T(8,128)S(1)} %bitcast.332, f32[6,512,1664]{2,1,0:T(8,128)} %all-gather.2.cloned.1.call-done), kind=kOutput, calls=%fused_computation.9 | convolution fusion | flops 5237047296 | bytes 14680064 | tf_op jit(solution)/shard_map/dot_general | solution.py:96
  443.1 5.4 all_to_all.126
  450.7 4.2 all-to-all-start.13
  455.1 10.0 %all-to-all-done.13 = f32[16,16,512]{2,1,0:T(8,128)} async-done(((f32[16,16,512]{2,1,0:T(8,128)}), f32[16,16,512]{2,1,0:T(8,128)}, u32[]{:S(2)}, u32[]{:S(2)}) %all-to-all-start.13) | async-done | bytes 524320 | tf_op jit(solution)/shard_map/all_to_all | solution.py:29
  467.1 4.3 all-to-all-start.14
  474.8 3.3 fusion.128
  478.1 3.5 dynamic-slice_bitcast_fusion
  482.9 6.8 %all_to_all.127 = f32[2,16,16,512]{3,2,1,0:T(8,128)S(1)} all-to-all(f32[2,16,16,512]{3,2,1,0:T(8,128)S(1)} %broadcast_in_dim.47), channel_id=1, replica_groups=mesh['col_0'=4,'col_1'=4,'col_2'=2,'row'=8] {'col_2'}, dimensions={0} | all-to-all | bytes 2097152 | tf_op jit(solution)/shard_map/all_to_all | solution.py:41
  489.9 8.1 %bitcast_multiply_fusion.2 = f32[512,1664]{1,0:T(8,128)S(1)} fusion(f32[1664,512]{0,1:T(8,128)S(1)} %copy-done.6, f32[512,1664]{1,0:T(8,128)S(1)} %bitcast_multiply_fusion.3, f32[512,512]{1,0:T(8,128)S(1)} %bitcast.333, f32[6,512,1664]{2,1,0:T(8,128)} %all-gather.2.cloned.1.call-done), kind=kOutput, calls=%fused_computation.6 | convolution fusion | flops 5237047296 | bytes 14680064 | tf_op jit(solution)/shard_map/dot_general | solution.py:96
  510.3 4.6 all_to_all.128
  515.8 6.8 %all-to-all-start.17 = ((f32[16,16,512]{2,1,0:T(8,128)}), f32[16,16,512]{2,1,0:T(8,128)S(1)}, u32[]{:S(2)}, u32[]{:S(2)}) async-start(f32[16,16,512]{2,1,0:T(8,128)} %reduce_sum.116), calls=%async_computation.17 | async-start | bytes 1048576 | tf_op jit(solution)/shard_map/all_to_all | solution.py:29
  525.1 7.9 %all-to-all-done.17 = f32[16,16,512]{2,1,0:T(8,128)S(1)} async-done(((f32[16,16,512]{2,1,0:T(8,128)}), f32[16,16,512]{2,1,0:T(8,128)S(1)}, u32[]{:S(2)}, u32[]{:S(2)}) %all-to-all-start.17) | async-done | bytes 524320 | tf_op jit(solution)/shard_map/all_to_all | solution.py:29
  533.9 4.2 all-to-all-start.18
  538.1 3.3 fusion.124
  541.5 5.8 all-to-all-done.18
  548.5 7.6 %all_to_all.129 = f32[2,16,16,512]{3,2,1,0:T(8,128)S(1)} all-to-all(f32[2,16,16,512]{3,2,1,0:T(8,128)S(1)} %broadcast_in_dim.50), channel_id=1, replica_groups=mesh['col_0'=4,'col_1'=4,'col_2'=2,'row'=8] {'col_2'}, dimensions={0} | all-to-all | bytes 2097152 | tf_op jit(solution)/shard_map/all_to_all | solution.py:41
  556.2 9.1 %bitcast_multiply_fusion.1 = f32[512,1664]{1,0:T(8,128)S(1)} fusion(f32[1664,512]{0,1:T(8,128)} %fusion.124, f32[512,1664]{1,0:T(8,128)S(1)} %copy-done.1, f32[512,512]{1,0:T(8,128)S(1)} %bitcast.334, f32[6,512,1664]{2,1,0:T(8,128)} %all-gather.2.cloned.1.call-done), kind=kOutput, calls=%fused_computation.3 | convolution fusion | flops 5237047296 | bytes 14680064 | tf_op jit(solution)/shard_map/dot_general | solution.py:96
  577.7 4.6 all_to_all.130
  582.4 13.4 %all_to_all.131 = f32[16,16,512]{2,1,0:T(8,128)S(1)} all-to-all(f32[16,16,512]{2,1,0:T(8,128)S(1)} %reduce_sum.118), channel_id=1, replica_groups=mesh['col_0'=4,'col_1'=4,'col_2'=2,'row'=8] {'col_0','col_1'}, dimensions={0} | all-to-all | bytes 1048576 | tf_op jit(solution)/shard_map/all_to_all | solution.py:29
  596.6 4.2 all-to-all-start.22
  601.5 3.3 fusion.120
  604.8 5.3 all-to-all-done.22
  611.2 7.7 %all_to_all.132 = f32[2,16,16,512]{3,2,1,0:T(8,128)S(1)} all-to-all(f32[2,16,16,512]{3,2,1,0:T(8,128)S(1)} %broadcast_in_dim.53), channel_id=1, replica_groups=mesh['col_0'=4,'col_1'=4,'col_2'=2,'row'=8] {'col_2'}, dimensions={0} | all-to-all | bytes 2097152 | tf_op jit(solution)/shard_map/all_to_all | solution.py:41
  619.0 10.2 %bitcast_multiply_fusion = f32[512,1664]{1,0:T(8,128)} fusion(f32[1664,512]{0,1:T(8,128)} %fusion.120, f32[512,1664]{1,0:T(8,128)S(1)} %copy-done.5, f32[512,512]{1,0:T(8,128)S(1)} %bitcast.330, f32[6,512,1664]{2,1,0:T(8,128)} %all-gather.2.cloned.1.call-done), kind=kOutput, calls=%fused_computation | convolution fusion | flops 5237047296 | bytes 14680064 | tf_op jit(solution)/shard_map/dot_general | solution.py:96
  (153 shorter events, 105.2 us)
Async XLA Ops:
  6.5 213.4 %all-gather.2.cloned.1.call-start = ((), (), s32[]{:S(2)}) async-start(), calls=%async_computation.24 | async-start | bytes 23003136 | tf_op jit(solution)/shard_map/all_gather | solution.py:84
  248.9 16.9 %all-to-all-start.1 = ((f32[16,16,512]{2,1,0:T(8,128)}), f32[16,16,512]{2,1,0:T(8,128)S(1)}, u32[]{:S(2)}, u32[]{:S(2)}) async-start(f32[16,16,512]{2,1,0:T(8,128)} %reduce_sum.108), calls=%async_computation.1 | async-start | bytes 1048576 | tf_op jit(solution)/shard_map/all_to_all | solution.py:29
  266.7 13.0 %all-to-all-start.2 = ((f32[16,16,512]{2,1,0:T(8,128)}), f32[16,16,512]{2,1,0:T(8,128)S(1)}, u32[]{:S(2)}, u32[]{:S(2)}) async-start(f32[16,16,512]{2,1,0:T(8,128)} %broadcast_in_dim.37), calls=%async_computation.2 | async-start | bytes 1048576 | tf_op jit(solution)/shard_map/all_to_all | solution.py:41
  279.7 8.1 %copy-start.8 = (f32[1664,512]{0,1:T(8,128)S(1)}, f32[1664,512]{0,1:T(8,128)}, u32[]{:S(2)}) copy-start(f32[1664,512]{0,1:T(8,128)} %fusion.140) | copy-start | bytes 10223620
  316.7 14.5 %all-to-all-start.5 = ((f32[16,16,512]{2,1,0:T(8,128)}), f32[16,16,512]{2,1,0:T(8,128)}, u32[]{:S(2)}, u32[]{:S(2)}) async-start(f32[16,16,512]{2,1,0:T(8,128)} %reduce_sum.110), calls=%async_computation.5 | async-start | bytes 1048576 | tf_op jit(solution)/shard_map/all_to_all | solution.py:29
  333.1 15.4 %all-to-all-start.6 = ((f32[16,16,512]{2,1,0:T(8,128)}), f32[16,16,512]{2,1,0:T(8,128)}, u32[]{:S(2)}, u32[]{:S(2)}) async-start(f32[16,16,512]{2,1,0:T(8,128)} %broadcast_in_dim.40), calls=%async_computation.6 | async-start | bytes 1048576 | tf_op jit(solution)/shard_map/all_to_all | solution.py:41
  348.5 7.9 %copy-start.7 = (f32[1664,512]{0,1:T(8,128)S(1)}, f32[1664,512]{0,1:T(8,128)}, u32[]{:S(2)}) copy-start(f32[1664,512]{0,1:T(8,128)} %fusion.136) | copy-start | bytes 10223620
  364.5 11.1 %copy-start.2 = (f32[512,1664]{1,0:T(8,128)}, f32[512,1664]{1,0:T(8,128)S(1)}, u32[]{:S(2)}) copy-start(f32[512,1664]{1,0:T(8,128)S(1)} %bitcast_multiply_fusion.4) | copy-start | bytes 10223620
  382.3 17.6 %all-to-all-start.9 = ((f32[16,16,512]{2,1,0:T(8,128)}), f32[16,16,512]{2,1,0:T(8,128)S(1)}, u32[]{:S(2)}, u32[]{:S(2)}) async-start(f32[16,16,512]{2,1,0:T(8,128)} %reduce_sum.112), calls=%async_computation.9 | async-start | bytes 1048576 | tf_op jit(solution)/shard_map/all_to_all | solution.py:29
  400.9 13.0 %all-to-all-start.10 = ((f32[16,16,512]{2,1,0:T(8,128)}), f32[16,16,512]{2,1,0:T(8,128)S(1)}, u32[]{:S(2)}, u32[]{:S(2)}) async-start(f32[16,16,512]{2,1,0:T(8,128)} %broadcast_in_dim.43), calls=%async_computation.10 | async-start | bytes 1048576 | tf_op jit(solution)/shard_map/all_to_all | solution.py:41
  413.8 7.9 %copy-start.3 = (f32[512,1664]{1,0:T(8,128)S(1)}, f32[512,1664]{1,0:T(8,128)}, u32[]{:S(2)}) copy-start(f32[512,1664]{1,0:T(8,128)} %copy-done.2) | copy-start | bytes 10223620
  450.7 14.5 %all-to-all-start.13 = ((f32[16,16,512]{2,1,0:T(8,128)}), f32[16,16,512]{2,1,0:T(8,128)}, u32[]{:S(2)}, u32[]{:S(2)}) async-start(f32[16,16,512]{2,1,0:T(8,128)} %reduce_sum.114), calls=%async_computation.13 | async-start | bytes 1048576 | tf_op jit(solution)/shard_map/all_to_all | solution.py:29
  467.1 14.5 %all-to-all-start.14 = ((f32[16,16,512]{2,1,0:T(8,128)}), f32[16,16,512]{2,1,0:T(8,128)}, u32[]{:S(2)}, u32[]{:S(2)}) async-start(f32[16,16,512]{2,1,0:T(8,128)} %broadcast_in_dim.46), calls=%async_computation.14 | async-start | bytes 1048576 | tf_op jit(solution)/shard_map/all_to_all | solution.py:41
  481.6 8.3 %copy-start.6 = (f32[1664,512]{0,1:T(8,128)S(1)}, f32[1664,512]{0,1:T(8,128)}, u32[]{:S(2)}) copy-start(f32[1664,512]{0,1:T(8,128)} %fusion.128) | copy-start | bytes 10223620
  498.0 11.1 %copy-start = (f32[512,1664]{1,0:T(8,128)}, f32[512,1664]{1,0:T(8,128)S(1)}, u32[]{:S(2)}) copy-start(f32[512,1664]{1,0:T(8,128)S(1)} %bitcast_multiply_fusion.2) | copy-start | bytes 10223620
  515.8 17.2 %all-to-all-start.17 = ((f32[16,16,512]{2,1,0:T(8,128)}), f32[16,16,512]{2,1,0:T(8,128)S(1)}, u32[]{:S(2)}, u32[]{:S(2)}) async-start(f32[16,16,512]{2,1,0:T(8,128)} %reduce_sum.116), calls=%async_computation.17 | async-start | bytes 1048576 | tf_op jit(solution)/shard_map/all_to_all | solution.py:29
  533.9 13.4 %all-to-all-start.18 = ((f32[16,16,512]{2,1,0:T(8,128)}), f32[16,16,512]{2,1,0:T(8,128)}, u32[]{:S(2)}, u32[]{:S(2)}) async-start(f32[16,16,512]{2,1,0:T(8,128)} %broadcast_in_dim.49), calls=%async_computation.18 | async-start | bytes 1048576 | tf_op jit(solution)/shard_map/all_to_all | solution.py:41
  541.5 14.7 %copy-start.1 = (f32[512,1664]{1,0:T(8,128)S(1)}, f32[512,1664]{1,0:T(8,128)}, u32[]{:S(2)}) copy-start(f32[512,1664]{1,0:T(8,128)} %copy-done) | copy-start | bytes 10223620
  565.3 11.1 %copy-start.4 = (f32[512,1664]{1,0:T(8,128)}, f32[512,1664]{1,0:T(8,128)S(1)}, u32[]{:S(2)}) copy-start(f32[512,1664]{1,0:T(8,128)S(1)} %bitcast_multiply_fusion.1) | copy-start | bytes 10223620
  596.6 13.4 %all-to-all-start.22 = ((f32[16,16,512]{2,1,0:T(8,128)}), f32[16,16,512]{2,1,0:T(8,128)}, u32[]{:S(2)}, u32[]{:S(2)}) async-start(f32[16,16,512]{2,1,0:T(8,128)} %broadcast_in_dim.52), calls=%async_computation.22 | async-start | bytes 1048576 | tf_op jit(solution)/shard_map/all_to_all | solution.py:41
  604.8 14.2 %copy-start.5 = (f32[512,1664]{1,0:T(8,128)S(1)}, f32[512,1664]{1,0:T(8,128)}, u32[]{:S(2)}) copy-start(f32[512,1664]{1,0:T(8,128)} %copy-done.4) | copy-start | bytes 10223620
Sparse Core Ops, SparseCore 0:
  9.1 210.7 all-gather.1
where the time goes:
time: 647 us; the launch traced here: 636 us
  waiting for transfers between devices  272 us (42%)
  matrix products  145 us (22%)
  blocking collectives  86.9 us (13%)
  starting transfers between devices  53.9 us (8%)
  local copies, waits for them, and re-layouts  34.7 us (5%)
  between operations  29.5 us (5%)
  other arithmetic  14.6 us (2%)
    all_gather x1, waiting for transfers between devices, shards(): all_rows = lax.all_gather(factor, 'row', axis=1, tiled=True)  205 us
    dot_general x6, matrix products, shards(): weights = weights - jnp.dot(errors, rows_k, precision=lax.Precision.HIGHEST)  53.7 us
    all_to_all x6, blocking collectives, sent_to_all(): lax.all_to_all(jnp.broadcast_to(value[None], (devices, *value.shape)), ax...  44.1 us
    all_to_all x5, waiting for transfers between devices, summed_rows(): return jnp.sum(lax.all_to_all(own, far, 0, 0, tiled=True), axis=0)  43 us
    dot_general x36, matrix products, panel_errors(): jnp.dot(tiles[b], ublock[b * TILE:(b + 1) * TILE, a * TILE:(a + 1) * TILE...  41.5 us
    dot_general x24, matrix products, panel_errors(): jnp.dot(acc, dinv[a], precision=lax.Precision.HIGHEST)  29.7 us
    all_to_all x6, blocking collectives, sent_and_summed(): lax.all_to_all(tiles, axis, split_axis=0, concat_axis=0, tiled=True)  29.5 us
    all_to_all x5, starting transfers between devices, summed_rows(): return jnp.sum(lax.all_to_all(own, far, 0, 0, tiled=True), axis=0)  29 us
  transfers between devices with their start and end apart: 12, of which 10 were waited for; matrix products, arithmetic and copies ran while one was open for 6% of the time, Pallas kernels for 0%

commit v1 on v0

v1 whole, which is shorter than its diff:
```python
import functools

import jax
import jax.numpy as jnp
import numpy as np
from jax import lax
from jax.experimental import pallas as pl
from jax.experimental.pallas import tpu as pltpu
from jax.sharding import Mesh
from jax.sharding import PartitionSpec as P

TILE = 128
PANEL_TILES = 4
PW = 512
P_SIZE = 6
N_COL = 32
COL = ("col_0", "col_1", "col_2")
HOPS = ((0, 1), (1, 1), (0, 3), (1, 3))
BLOCKS = [(k, m) for k in range(P_SIZE) for m in range(k + 1)]
SLOTS = 6
HALF = SLOTS // 2
MINE = 16
NARROW = 256


def device(x, y, core):
    return (x * 4 + y) * 2 + core


def exchange(stream, stage):
    pairs = []
    for x in range(4):
        for y in range(4):
            for core in range(2):
                axis, bits = HOPS[(stream + stage + 2 * core) % 4]
                there = (x ^ bits, y) if axis == 0 else (x, y ^ bits)
                pairs.append((device(x, y, core), device(*there, core)))
    return pairs


def other_core(value):
    return lax.ppermute(value, "col_2", [(0, 1), (1, 0)])


def spread(streams):
    near = [value[None] for value in streams]
    for stage in range(3):
        near = [
            jnp.concatenate([value, lax.ppermute(value, COL, exchange(i, stage))], 0)
            for i, value in enumerate(near)
        ]
    far = [lax.ppermute(value, COL, exchange(i, 3)) for i, value in enumerate(near)]
    return [
        [near[i], far[i], other_core(near[i]), other_core(far[i])] for i in range(len(streams))
    ]


def all_rows(value):
    height = lax.axis_size("row")
    up = [(z, (z + 1) % height) for z in range(height)]
    down = [(z, (z - 1) % height) for z in range(height)]
    below, above = [value], [value]
    for hop in range(height // 2):
        below.append(lax.ppermute(below[-1], "row", up))
        if hop < height // 2 - 1:
            above.append(lax.ppermute(above[-1], "row", down))
    here = lax.axis_index("row")
    whole = jnp.zeros((value.shape[0], height, *value.shape[1:]), value.dtype)
    for i, part in enumerate(above + below[:0:-1]):
        place = lax.rem(here + i, height)
        whole = lax.dynamic_update_slice_in_dim(whole, part[:, None], place, 1)
    return whole


def sources():
    x, y, own = (lax.axis_index(name) for name in COL)
    steps = []
    for axis in range(2):
        value = np.zeros((2, 2, 16), np.int32)
        for core in range(2):
            for stream in range(2):
                for unit in range(16):
                    for stage in range(4):
                        hop, bits = HOPS[(stream + stage + 2 * core) % 4]
                        if hop == axis and unit >> stage & 1:
                            value[core, stream, unit] ^= bits
        steps.append(jnp.asarray(value))
    rows = []
    for core in (own, 1 - own):
        there_x = x ^ jnp.where(core == 0, steps[0][0], steps[0][1])
        there_y = y ^ jnp.where(core == 0, steps[1][0], steps[1][1])
        rows.append(device(there_x, there_y, core))
    return jnp.stack(rows, 1).astype(jnp.int32).reshape(-1)


def halves(value):
    high = value.astype(jnp.bfloat16)
    low = (value - high.astype(jnp.float32)).astype(jnp.bfloat16)
    return high, low


def product(left, right):
    dot = functools.partial(jnp.dot, preferred_element_type=jnp.float32)
    return dot(left[0], right[0]) + (dot(left[0], right[1]) + dot(left[1], right[0]))


def unit_copies(refs, place, semaphores):
    copies = []
    for stream in range(2):
        group = []
        for part in range(4):
            for unit in range(8):
                number = (stream * 2 + part // 2) * 16 + part % 2 * 8 + unit
                group.append(
                    pltpu.make_async_copy(
                        refs[stream * 4 + part].at[unit],
                        place(stream, number),
                        semaphores.at[number],
                    )
                )
        copies.append(group)
    return copies


def solve_kernel(source, flags, *refs):
    parts, (windows, inverse), outs = refs[:8], refs[8:10], refs[10:12]
    blocks, errors, semaphores = refs[12:]

    def place(stream, number):
        place_of = source[number]
        return blocks.at[pl.ds(stream * HALF, HALF), place_of // 8, :, lax.rem(place_of, 8)]

    copies = unit_copies(parts, place, semaphores)
    for group in copies:
        for copy in group:
            copy.start()
    for copy in copies[0]:
        copy.wait()
    arrived = 1

    def block_at(number):
        return halves(blocks[number // 4, lax.rem(number, 4)].reshape(PW, PW))

    for k in range(P_SIZE):
        base = k * (k + 1) // 2
        if base + k >= 4 * HALF and arrived == 1:
            for copy in copies[1]:
                copy.wait()
            arrived = 2

        def take(m, acc, base=base):
            return acc - product((errors[m, 0], errors[m, 1]), block_at(base + m))

        window = lax.fori_loop(0, k, take, windows[k])
        block = block_at(base + k)
        done = []
        for a in range(PANEL_TILES):
            tile = slice(a * TILE, (a + 1) * TILE)
            acc = window[:, tile]
            if a:
                left = tuple(jnp.concatenate([d[i] for d in done], 1) for i in range(2))
                acc = acc - product(left, tuple(b[: a * TILE, tile] for b in block))
            acc = product(halves(acc), halves(inverse[k, a]))
            acc = jnp.where(flags[k, a] != 0, acc, 0.0)
            done.append(halves(acc))
            column = (k % 3) * PW + a * TILE
            outs[k // 3][:, column : column + TILE] = acc
        for i in range(2):
            errors[k, i] = jnp.concatenate([d[i] for d in done], 1)


def assemble_kernel(source, *refs):
    parts, (out, errors, semaphores) = refs[:8], refs[8:]

    def place(stream, number):
        first = pl.multiple_of(source[number] * MINE, MINE)
        return errors.at[stream, pl.ds(first, MINE)]

    copies = unit_copies(parts, place, semaphores)
    for group in copies:
        for copy in group:
            copy.start()
    for stream, group in enumerate(copies):
        for copy in group:
            copy.wait()
        for k in range(3 * stream, 3 * stream + 3):
            high, low = halves(errors[stream, :, (k % 3) * PW : (k % 3 + 1) * PW])
            out[k, :, :PW] = high
            out[k, :, PW : 2 * PW] = low
            out[k, :, 2 * PW :] = high


def update_kernel(flags, errors, weights, factor, out):
    n = pl.program_id(0)
    out[...] = weights[...]

    def take(k, carry):
        high, low = halves(factor[k])
        rows = jnp.concatenate([high, high, low], 0)
        out[...] = out[...] - jnp.dot(errors[k], rows, preferred_element_type=jnp.float32)
        return carry

    lax.fori_loop(0, P_SIZE, take, 0)
    for part in range(NARROW // TILE):
        tile = n * (NARROW // TILE) + part - flags[0]
        inside = jnp.logical_and(tile >= 0, tile < PANEL_TILES)
        a = jnp.clip(tile, 0, PANEL_TILES - 1)
        columns = slice(part * TILE, (part + 1) * TILE)
        for r in range(4):
            gone = jnp.logical_and(inside, flags[1 + r * PANEL_TILES + a] != 0)

            @pl.when(gone)
            def _(r=r, columns=columns):
                out[r * TILE : (r + 1) * TILE, columns] = jnp.zeros((TILE, TILE), jnp.float32)


def shards(weights, factor, diag_inverse, prune_mask, panel_start):
    rows, width = weights.shape
    slab = factor.shape[1]
    me = lax.axis_index(COL)
    owner = panel_start // width
    mine = owner == me
    shift = jnp.sum(jnp.where(mine, panel_start - me * width, 0))
    panel = jnp.sum(jnp.where(mine, jnp.arange(P_SIZE, dtype=jnp.int32), 0))
    gathered = lax.all_gather(factor, "row", axis=1, tiled=True)

    window = lax.dynamic_slice(factor, (0, 0, shift), (P_SIZE, slab, PW))
    window = window.reshape(P_SIZE, 8, 8, PW)
    turn = lax.rem(panel * (panel + 1) // 2, 4)
    order = lax.rem(jnp.arange(4, dtype=jnp.int32) + 4 - turn, 4)
    order = jnp.minimum(order[:, None] + jnp.array([0, 4], jnp.int32), P_SIZE - 1)
    eighths = jnp.swapaxes(window[order], 1, 2).reshape(N_COL, 16, PW)
    wanted = lax.dynamic_slice(weights, (0, shift), (rows, PW)).reshape(N_COL, MINE, PW)
    arrived = lax.all_to_all(
        jnp.concatenate([eighths, wanted], 1), COL, 0, 0, tiled=True
    ).reshape(4 * N_COL, 8, PW)

    numbers = jnp.minimum(4 * jnp.arange(SLOTS, dtype=jnp.int32) + me // 8, len(BLOCKS) - 1)
    panels = jnp.array([k for k, _ in BLOCKS], jnp.int32)[numbers]
    parts = jnp.array([m // 4 for _, m in BLOCKS], jnp.int32)[numbers]
    picked = all_rows(arrived[owner[panels] * 4 + parts])
    windows = arrived[(owner[:, None] * 4 + jnp.array([2, 3], jnp.int32)).reshape(-1)]
    windows = windows.reshape(P_SIZE, MINE, PW)
    source = sources()
    spread_parts = spread([picked[:HALF], picked[HALF:]])

    own_rows = lax.dynamic_slice(prune_mask, (0, me // 8, 0), (P_SIZE, 1, PANEL_TILES))[:, 0]
    any_spec = pl.BlockSpec(memory_space=pl.ANY)
    vmem = pl.BlockSpec(memory_space=pltpu.VMEM)
    smem = pl.BlockSpec(memory_space=pltpu.SMEM)
    found = pl.pallas_call(
        solve_kernel,
        out_shape=[jax.ShapeDtypeStruct((MINE, 3 * PW), jnp.float32)] * 2,
        in_specs=[smem, smem] + [any_spec] * 8 + [vmem, vmem],
        out_specs=[vmem, vmem],
        scratch_shapes=[
            pltpu.VMEM((SLOTS, 4, 8, 8, 8, PW), jnp.float32),
            pltpu.VMEM((P_SIZE, 2, MINE, PW), jnp.bfloat16),
            pltpu.SemaphoreType.DMA((64,)),
        ],
        compiler_params=pltpu.CompilerParams(vmem_limit_bytes=48 << 20),
        name="solve",
    )(source, own_rows, *spread_parts[0], *spread_parts[1], windows, diag_inverse)

    spread_errors = spread(found)
    pruned = jnp.sum(jnp.where(mine[:, None, None], prune_mask, 0), 0).reshape(-1)
    flags = jnp.concatenate([(shift // TILE)[None], pruned]).astype(jnp.int32)
    split = pl.pallas_call(
        assemble_kernel,
        out_shape=jax.ShapeDtypeStruct((P_SIZE, rows, 3 * PW), jnp.bfloat16),
        in_specs=[smem] + [any_spec] * 8,
        out_specs=vmem,
        scratch_shapes=[
            pltpu.VMEM((2, rows, 3 * PW), jnp.float32),
            pltpu.SemaphoreType.DMA((64,)),
        ],
        compiler_params=pltpu.CompilerParams(vmem_limit_bytes=24 << 20),
        name="assemble",
    )(source, *spread_errors[0], *spread_errors[1])
    steps = pl.cdiv(width, NARROW)
    column = lambda i, *_: (0, i)
    return pl.pallas_call(
        update_kernel,
        out_shape=jax.ShapeDtypeStruct(weights.shape, jnp.float32),
        grid_spec=pltpu.PrefetchScalarGridSpec(
            num_scalar_prefetch=1,
            grid=(steps,),
            in_specs=[
                vmem,
                pl.BlockSpec((rows, NARROW), column),
                pl.BlockSpec((P_SIZE, PW, NARROW), lambda i, *_: (0, 0, i)),
            ],
            out_specs=pl.BlockSpec((rows, NARROW), column),
        ),
        compiler_params=pltpu.CompilerParams(vmem_limit_bytes=40 << 20),
        name="update",
    )(flags, split, weights, gathered)


def solution(mesh):
    torus = Mesh(
        mesh.devices.reshape(4, 4, 2, mesh.shape["row"]), ("col_0", "col_1", "col_2", "row")
    )
    return jax.shard_map(
        shards,
        mesh=torus,
        in_specs=(P("row", COL), P(None, "row", COL), P(), P(None, "row", None), P()),
        out_specs=P("row", COL),
        check_vma=False,
    )
```

time: 647 us -> 300 us (0.46); the launches traced: 636 us -> 299 us
  matrix products: 145 us -> 0 us
  waiting for transfers between devices: 272 us -> 138 us
  blocking collectives: 86.9 us -> 0 us
  Pallas kernels: 0 us -> 50.6 us
  local copies, waits for them, and re-layouts: 34.7 us -> 18 us
  starting transfers between devices: 53.9 us -> 64.7 us
  between operations: 29.5 us -> 19.3 us
    all_gather x1, waiting for transfers between devices: 205 us -> 0.01 us  [shards(): gathered = lax.all_gather(factor, 'row', axis=1, tiled=True)]
    dot_general x72 -> x0, matrix products: 145 us -> none  [the longest x6 53.7 us: shards(): weights = weights - jnp.dot(errors, rows_k, precision=lax.Precision.HIGHEST)]
    ppermute x0 -> x31, waiting for transfers between devices: none -> 111 us  [the longest x12 50.6 us: spread(): lax.ppermute(value, COL, exchange(i, stage))]
    all_to_all x13 -> x0, blocking collectives: 86.9 us -> none  [the longest x6 44.1 us: sent_to_all(): lax.all_to_all(jnp.broadcast_to(value[None], (devices, *value.shape)), ax...]
    ppermute x0 -> x31, starting transfers between devices: none -> 56 us  [the longest x8 29.1 us: other_core(): return lax.ppermute(value, 'col_2', [(0, 1), (1, 0)])]
    pallas_call x0 -> x3, Pallas kernels: none -> 50.6 us  [the longest x1 28.7 us: shards(): pl.pallas_call(update_kernel, out_shape=jax.ShapeDtypeStruct(weights.shap...]
    all_to_all x11 -> x1, starting transfers between devices: 53.9 us -> 8.71 us  [shards(): lax.all_to_all(jnp.concatenate([eighths, wanted], 1), COL, 0, 0, tiled=True)]
    all_to_all x11 -> x1, waiting for transfers between devices: 65.8 us -> 26.2 us  [shards(): lax.all_to_all(jnp.concatenate([eighths, wanted], 1), COL, 0, 0, tiled=True)]
  transfers between devices with their start and end apart: 12 -> 33, of which waited for: 10 -> 17; matrix products, arithmetic and copies ran while one was open for 6% -> 6% of each run, Pallas kernels for 0% -> 7%
where the time goes in v1:
time: 300 us; the launch traced here: 299 us
  waiting for transfers between devices  138 us (46%)
  starting transfers between devices  64.7 us (22%)
  Pallas kernels  50.6 us (17%)
  between operations  19.3 us (6%)
  local copies, waits for them, and re-layouts  18 us (6%)
  other arithmetic  8.75 us (3%)
    ppermute x12, waiting for transfers between devices, spread(): lax.ppermute(value, COL, exchange(i, stage))  50.6 us
    ppermute x4, waiting for transfers between devices, spread(): lax.ppermute(value, COL, exchange(i, 3))  34 us
    ppermute x8, starting transfers between devices, other_core(): return lax.ppermute(value, 'col_2', [(0, 1), (1, 0)])  29.1 us
    pallas_call x1, Pallas kernels, shards(): pl.pallas_call(update_kernel, out_shape=jax.ShapeDtypeStruct(weights.shap...  28.7 us
    all_to_all x1, waiting for transfers between devices, shards(): lax.all_to_all(jnp.concatenate([eighths, wanted], 1), COL, 0, 0, tiled=True)  26.2 us
    pallas_call x1, Pallas kernels, shards(): pl.pallas_call(solve_kernel, out_shape=[jax.ShapeDtypeStruct((MINE, 3 * P...  17.2 us
    ppermute x4, waiting for transfers between devices, all_rows(): below.append(lax.ppermute(below[-1], 'row', up))  14.7 us
    ppermute x3, starting transfers between devices, all_rows(): above.append(lax.ppermute(above[-1], 'row', down))  12.7 us
  transfers between devices with their start and end apart: 33, of which 17 were waited for; matrix products, arithmetic and copies ran while one was open for 6% of the time, Pallas kernels for 7%

profile of v1, /device:TPU:1, one launch (start us, length us, event | category | flops | bytes accessed | tf_op | source)
XLA Modules:
  0.0 299.2 jit_solution(13394172941814160164)
XLA Ops:
  6.5 0.7 all-gather.2.cloned.1.call-update
  7.9 1.4 select_reduce_fusion.1
  12.8 1.5 dynamic-slice_bitcast_fusion
  15.0 1.7 constant_dynamic-slice_fusion
  16.7 1.5 pad_maximum_fusion.2
  18.2 8.7 %all-to-all-start = ((f32[32,32,512]{2,1,0:T(8,128)}), f32[32,32,512]{2,1,0:T(8,128)S(1)}, u32[]{:S(2)}, u32[]{:S(2)}) async-start(f32[32,32,512]{2,1,0:T(8,128)} %pad_maximum_fusion.2), calls=%async_computation | async-start | bytes 4194304 | tf_op jit(solution)/shard_map/all_to_all | solution.py:234
  29.0 26.2 %all-to-all-done = f32[32,32,512]{2,1,0:T(8,128)S(1)} async-done(((f32[32,32,512]{2,1,0:T(8,128)}), f32[32,32,512]{2,1,0:T(8,128)S(1)}, u32[]{:S(2)}, u32[]{:S(2)}) %all-to-all-start) | async-done | bytes 2097184 | tf_op jit(solution)/shard_map/all_to_all | solution.py:234
  55.8 5.7 %collective-permute-start = (f32[6,8,512]{2,1,0:T(8,128)S(1)}, f32[6,8,512]{2,1,0:T(8,128)S(1)}, u32[]{:S(2)}, u32[]{:S(2)}) collective-permute-start(f32[6,8,512]{2,1,0:T(8,128)S(1)} %gather_fusion.4), channel_id=1, source_target_pairs={{0,7},{1,0},{2,1},{3,2},{4,3},{5,4},{6,5},{7,6},{8,15},{9,8},{10,9... | collective-permute-start | bytes 294920 | tf_op jit(solution)/shard_map/ppermute | solution.py:66
  61.6 4.3 %collective-permute-done = f32[6,8,512]{2,1,0:T(8,128)S(1)} collective-permute-done((f32[6,8,512]{2,1,0:T(8,128)S(1)}, f32[6,8,512]{2,1,0:T(8,128)S(1)}, u32[]{:S(2)}, u32[]{:S(2)}) %collective-permute-start) | collective-permute-done | bytes 98336 | tf_op jit(solution)/shard_map/ppermute | solution.py:66
  65.9 3.5 %collective-permute-start.1 = (f32[6,8,512]{2,1,0:T(8,128)S(1)}, f32[6,8,512]{2,1,0:T(8,128)S(1)}, u32[]{:S(2)}, u32[]{:S(2)}) collective-permute-start(f32[6,8,512]{2,1,0:T(8,128)S(1)} %collective-permute-done), channel_id=1, source_target_pairs={{0,7},{1,0},{2,1},{3,2},{4,3},{5,4},{6,5},{7,6},{8,15},{9,8},{10,9... | collective-permute-start | bytes 294920 | tf_op jit(solution)/shard_map/ppermute | solution.py:66
  69.5 4.2 %collective-permute-done.1 = f32[6,8,512]{2,1,0:T(8,128)S(1)} collective-permute-done((f32[6,8,512]{2,1,0:T(8,128)S(1)}, f32[6,8,512]{2,1,0:T(8,128)S(1)}, u32[]{:S(2)}, u32[]{:S(2)}) %collective-permute-start.1) | collective-permute-done | bytes 98336 | tf_op jit(solution)/shard_map/ppermute | solution.py:66
  73.7 3.5 %collective-permute-start.2 = (f32[6,8,512]{2,1,0:T(8,128)S(1)}, f32[6,8,512]{2,1,0:T(8,128)S(1)}, u32[]{:S(2)}, u32[]{:S(2)}) collective-permute-start(f32[6,8,512]{2,1,0:T(8,128)S(1)} %collective-permute-done.1), channel_id=1, source_target_pairs={{0,7},{1,0},{2,1},{3,2},{4,3},{5,4},{6,5},{7,6},{8,15},{9,8},{10,9... | collective-permute-start | bytes 294920 | tf_op jit(solution)/shard_map/ppermute | solution.py:66
  77.2 7.4 %collective-permute-done.5 = f32[6,8,512]{2,1,0:T(8,128)S(1)} collective-permute-done((f32[6,8,512]{2,1,0:T(8,128)S(1)}, f32[6,8,512]{2,1,0:T(8,128)S(1)}, u32[]{:S(2)}, u32[]{:S(2)}) %collective-permute-start.5) | collective-permute-done | bytes 98336 | tf_op jit(solution)/shard_map/ppermute | solution.py:64
  84.7 7.3 %collective-permute-done.6 = f32[6,8,512]{2,1,0:T(8,128)S(1)} collective-permute-done((f32[6,8,512]{2,1,0:T(8,128)S(1)}, f32[6,8,512]{2,1,0:T(8,128)S(1)}, u32[]{:S(2)}, u32[]{:S(2)}) %collective-permute-start.6) | collective-permute-done | bytes 98336 | tf_op jit(solution)/shard_map/ppermute | solution.py:64
  92.1 1.1 collective-permute-start.13
  93.6 6.8 %collective-permute-done.13 = f32[1,3,8,8,512]{4,3,2,1,0:T(8,128)S(1)} collective-permute-done((f32[1,3,8,8,512]{4,3,2,1,0:T(8,128)S(1)}, f32[1,3,8,8,512]{4,3,2,1,0:T(8,128)S(1)}, u32[]{:S(2)}, u32[]{:S(2)}) %collective-permute-start.13) | collective-permute-done | bytes 393248 | tf_op jit(solution)/shard_map/ppermute | solution.py:49
  100.6 0.8 collective-permute-done.7
  101.6 1.8 collective-permute-start.8
  103.3 8.7 %collective-permute-done.14 = f32[2,3,8,8,512]{4,3,2,1,0:T(8,128)S(1)} collective-permute-done((f32[2,3,8,8,512]{4,3,2,1,0:T(8,128)S(1)}, f32[2,3,8,8,512]{4,3,2,1,0:T(8,128)S(1)}, u32[]{:S(2)}, u32[]{:S(2)}) %collective-permute-start.14) | collective-permute-done | bytes 786464 | tf_op jit(solution)/shard_map/ppermute | solution.py:49
  112.1 1.7 collective-permute-start.15
  114.2 0.7 collective-permute-start.9
  114.9 21.4 %collective-permute-done.15 = f32[4,3,8,8,512]{4,3,2,1,0:T(8,128)S(1)} collective-permute-done((f32[4,3,8,8,512]{4,3,2,1,0:T(8,128)S(1)}, f32[4,3,8,8,512]{4,3,2,1,0:T(8,128)S(1)}, u32[]{:S(2)}, u32[]{:S(2)}) %collective-permute-start.15) | collective-permute-done | bytes 1572896 | tf_op jit(solution)/shard_map/ppermute | solution.py:49
  136.4 2.1 pad_maximum_fusion.1.refs_4_
  139.1 1.8 collective-permute-start.10
  141.0 8.2 %collective-permute-start.17 = (f32[8,3,8,8,512]{4,3,2,1,0:T(8,128)}, f32[8,3,8,8,512]{4,3,2,1,0:T(8,128)}, u32[]{:S(2)}, u32[]{:S(2)}) collective-permute-start(f32[8,3,8,8,512]{4,3,2,1,0:T(8,128)} %pad_maximum_fusion.1.refs_4_), channel_id=1, source_target_pairs={{0,8},{8,0},{1,9},{9,1},{2,10},{10,2},{3,11},{11,3},{4,12},{12,4},... | collective-permute-start | bytes 9437192 | tf_op jit(solution)/shard_map/ppermute | solution.py:42
  149.2 30.1 %collective-permute-done.16.refs_5_ = f32[8,3,8,8,512]{4,3,2,1,0:T(8,128)} collective-permute-done((f32[8,3,8,8,512]{4,3,2,1,0:T(8,128)}, f32[8,3,8,8,512]{4,3,2,1,0:T(8,128)}, u32[]{:S(2)}, u32[]{:S(2)}) %collective-permute-start.16) | collective-permute-done | bytes 3145760 | tf_op jit(solution)/shard_map/ppermute | solution.py:52
  179.4 8.2 %collective-permute-start.12 = (f32[8,3,8,8,512]{4,3,2,1,0:T(8,128)}, f32[8,3,8,8,512]{4,3,2,1,0:T(8,128)}, u32[]{:S(2)}, u32[]{:S(2)}) collective-permute-start(f32[8,3,8,8,512]{4,3,2,1,0:T(8,128)} %collective-permute-done.10.refs_1_), channel_id=1, source_target_pairs={{0,8},{8,0},{1,9},{9,1},{2,10},{10,2},{3,11},{11,3},{4,12},{12,4},... | collective-permute-start | bytes 9437192 | tf_op jit(solution)/shard_map/ppermute | solution.py:42
  188.0 2.2 gather_fusion.5
  190.3 3.0 collective-permute-done.12.refs_3_
  193.3 1.4 copy-done.3
  194.7 17.2 %solve.1 = (f32[16,1536]{1,0:T(8,128)S(1)}, f32[16,1536]{1,0:T(8,128)S(1)}) custom-call(s32[64]{0:T(128)S(1)} %reshape.308.source, s32[6,4]{1,0:T(8,128)S(1)} %copy.39.flags, f32[8,3,8,8,512]{4,3,2,1,0:T(8,128)S(1)} %pad_maximum_fusion.refs_0_, f32[8,3,8,8,512]{4,3,2,1,0:T(8,128)} %collective-permute-done.10.refs_1_, ...), custom_call_target="tpu_custom_call" | custom-call | tf_op jit(solution)/shard_map/solve/pallas_call | solution.py:251
  212.1 5.0 %collective-permute-done.25 = f32[1,16,1536]{2,1,0:T(8,128)S(1)} collective-permute-done((f32[1,16,1536]{2,1,0:T(8,128)S(1)}, f32[1,16,1536]{2,1,0:T(8,128)S(1)}, u32[]{:S(2)}, u32[]{:S(2)}) %collective-permute-start.25) | collective-permute-done | bytes 98336 | tf_op jit(solution)/shard_map/ppermute | solution.py:49
  217.2 2.6 collective-permute-start.20
  219.8 2.2 collective-permute-done.26
  222.2 1.2 collective-permute-done.20
  223.4 1.5 collective-permute-start.21
  225.0 4.1 %collective-permute-done.27 = f32[4,16,1536]{2,1,0:T(8,128)S(1)} collective-permute-done((f32[4,16,1536]{2,1,0:T(8,128)S(1)}, f32[4,16,1536]{2,1,0:T(8,128)S(1)}, u32[]{:S(2)}, u32[]{:S(2)}) %collective-permute-start.27) | collective-permute-done | bytes 393248 | tf_op jit(solution)/shard_map/ppermute | solution.py:49
  229.1 0.9 pad_maximum_fusion.8.refs_4_
  230.7 0.9 pad_maximum_fusion.7.refs_0_
  231.6 1.0 collective-permute-start.22
  232.7 6.2 %collective-permute-start.29 = (f32[8,16,1536]{2,1,0:T(8,128)}, f32[8,16,1536]{2,1,0:T(8,128)}, u32[]{:S(2)}, u32[]{:S(2)}) collective-permute-start(f32[8,16,1536]{2,1,0:T(8,128)} %pad_maximum_fusion.8.refs_4_), channel_id=1, source_target_pairs={{0,8},{8,0},{1,9},{9,1},{2,10},{10,2},{3,11},{11,3},{4,12},{12,4},... | collective-permute-start | bytes 2359304 | tf_op jit(solution)/shard_map/ppermute | solution.py:42
  238.9 3.8 %collective-permute-done.28.refs_5_ = f32[8,16,1536]{2,1,0:T(8,128)} collective-permute-done((f32[8,16,1536]{2,1,0:T(8,128)}, f32[8,16,1536]{2,1,0:T(8,128)}, u32[]{:S(2)}, u32[]{:S(2)}) %collective-permute-start.28) | collective-permute-done | bytes 786464 | tf_op jit(solution)/shard_map/ppermute | solution.py:52
  242.7 3.6 %collective-permute-start.30 = (f32[8,16,1536]{2,1,0:T(8,128)}, f32[8,16,1536]{2,1,0:T(8,128)}, u32[]{:S(2)}, u32[]{:S(2)}) collective-permute-start(f32[8,16,1536]{2,1,0:T(8,128)} %collective-permute-done.28.refs_5_), channel_id=1, source_target_pairs={{0,8},{8,0},{1,9},{9,1},{2,10},{10,2},{3,11},{11,3},{4,12},{12,4},... | collective-permute-start | bytes 2359304 | tf_op jit(solution)/shard_map/ppermute | solution.py:42
  246.3 2.8 collective-permute-start.24
  251.5 4.8 %assemble.1.errors = bf16[6,512,1536]{2,1,0:T(8,128)(2,1)S(1)} custom-call(s32[64]{0:T(128)S(1)} %reshape.308.source, f32[8,16,1536]{2,1,0:T(8,128)} %pad_maximum_fusion.7.refs_0_, f32[8,16,1536]{2,1,0:T(8,128)} %collective-permute-done.22.refs_1_, f32[8,16,1536]{2,1,0:T(8,128)} %collective-permute-done.23.refs_2_, ...), custom_call_target="tpu_custom_call" | custom-call | tf_op jit(solution)/shard_map/assemble/pallas_call | solution.py:268
  256.3 3.7 %copy-done = bf16[6,512,1536]{2,1,0:T(8,128)(2,1)} copy-done((bf16[6,512,1536]{2,1,0:T(8,128)(2,1)}, bf16[6,512,1536]{2,1,0:T(8,128)(2,1)S(1)}, u32[]{:S(2)}) %copy-start) | copy-done | bytes 9437208
  260.0 3.7 %copy-done.1 = bf16[6,512,1536]{2,1,0:T(8,128)(2,1)S(1)} copy-done((bf16[6,512,1536]{2,1,0:T(8,128)(2,1)S(1)}, bf16[6,512,1536]{2,1,0:T(8,128)(2,1)}, u32[]{:S(2)}) %copy-start.1) | copy-done | bytes 9437208
  263.6 28.7 %update.1 = f32[512,1664]{1,0:T(8,128)} custom-call(s32[17]{0:T(128)S(1)} %pad_add_fusion.1.flags, bf16[6,512,1536]{2,1,0:T(8,128)(2,1)S(1)} %copy-done.1, f32[512,1664]{1,0:T(8,128)S(1)} %copy-done.2, f32[6,512,1664]{2,1,0:T(8,128)} %all-gather.2.cloned.1.call-done.factor), custom_call_target="tpu_custom_call" | custom-call | tf_op jit(solution)/shard_map/update/pallas_call | solution.py:282
  (106 shorter events, 8.0 us)
Async XLA Ops:
  6.5 253.4 %all-gather.2.cloned.1.call-start = ((), (), s32[]{:S(2)}) async-start(), calls=%async_computation.1 | async-start | bytes 23003136 | tf_op jit(solution)/shard_map/all_gather | solution.py:225
  18.2 8.8 %copy-start.5 = (s32[21]{0:T(128)S(1)}, s32[21]{0:T(128)}, u32[]{:S(2)}) copy-start(s32[21]{0:T(128)} %constant.129.clone) | copy-start | bytes 256
  18.2 10.1 %copy-start.4 = (s32[21]{0:T(128)S(1)}, s32[21]{0:T(128)}, u32[]{:S(2)}) copy-start(s32[21]{0:T(128)} %constant.130.clone) | copy-start | bytes 256
  18.2 37.1 %all-to-all-start = ((f32[32,32,512]{2,1,0:T(8,128)}), f32[32,32,512]{2,1,0:T(8,128)S(1)}, u32[]{:S(2)}, u32[]{:S(2)}) async-start(f32[32,32,512]{2,1,0:T(8,128)} %pad_maximum_fusion.2), calls=%async_computation | async-start | bytes 4194304 | tf_op jit(solution)/shard_map/all_to_all | solution.py:234
  55.3 46.3 %copy-start.6 = (f32[32,32,512]{2,1,0:T(8,128)}, f32[32,32,512]{2,1,0:T(8,128)S(1)}, u32[]{:S(2)}) copy-start(f32[32,32,512]{2,1,0:T(8,128)S(1)} %all-to-all-done) | copy-start | bytes 6291460
  55.8 10.1 %collective-permute-start = (f32[6,8,512]{2,1,0:T(8,128)S(1)}, f32[6,8,512]{2,1,0:T(8,128)S(1)}, u32[]{:S(2)}, u32[]{:S(2)}) collective-permute-start(f32[6,8,512]{2,1,0:T(8,128)S(1)} %gather_fusion.4), channel_id=1, source_target_pairs={{0,7},{1,0},{2,1},{3,2},{4,3},{5,4},{6,5},{7,6},{8,15},{9,8},{10,9... | collective-permute-start | bytes 294920 | tf_op jit(solution)/shard_map/ppermute | solution.py:66
  61.5 8.0 %collective-permute-start.3 = (f32[6,8,512]{2,1,0:T(8,128)S(1)}, f32[6,8,512]{2,1,0:T(8,128)S(1)}, u32[]{:S(2)}, u32[]{:S(2)}) collective-permute-start(f32[6,8,512]{2,1,0:T(8,128)S(1)} %gather_fusion.4), channel_id=1, source_target_pairs={{0,1},{1,2},{2,3},{3,4},{4,5},{5,6},{6,7},{7,0},{8,9},{9,10},{10,1... | collective-permute-start | bytes 294920 | tf_op jit(solution)/shard_map/ppermute | solution.py:64
  65.9 7.8 %collective-permute-start.1 = (f32[6,8,512]{2,1,0:T(8,128)S(1)}, f32[6,8,512]{2,1,0:T(8,128)S(1)}, u32[]{:S(2)}, u32[]{:S(2)}) collective-permute-start(f32[6,8,512]{2,1,0:T(8,128)S(1)} %collective-permute-done), channel_id=1, source_target_pairs={{0,7},{1,0},{2,1},{3,2},{4,3},{5,4},{6,5},{7,6},{8,15},{9,8},{10,9... | collective-permute-start | bytes 294920 | tf_op jit(solution)/shard_map/ppermute | solution.py:66
  69.5 7.8 %collective-permute-start.4 = (f32[6,8,512]{2,1,0:T(8,128)S(1)}, f32[6,8,512]{2,1,0:T(8,128)S(1)}, u32[]{:S(2)}, u32[]{:S(2)}) collective-permute-start(f32[6,8,512]{2,1,0:T(8,128)S(1)} %collective-permute-done.3), channel_id=1, source_target_pairs={{0,1},{1,2},{2,3},{3,4},{4,5},{5,6},{6,7},{7,0},{8,9},{9,10},{10,1... | collective-permute-start | bytes 294920 | tf_op jit(solution)/shard_map/ppermute | solution.py:64
  73.7 11.0 %collective-permute-start.2 = (f32[6,8,512]{2,1,0:T(8,128)S(1)}, f32[6,8,512]{2,1,0:T(8,128)S(1)}, u32[]{:S(2)}, u32[]{:S(2)}) collective-permute-start(f32[6,8,512]{2,1,0:T(8,128)S(1)} %collective-permute-done.1), channel_id=1, source_target_pairs={{0,7},{1,0},{2,1},{3,2},{4,3},{5,4},{6,5},{7,6},{8,15},{9,8},{10,9... | collective-permute-start | bytes 294920 | tf_op jit(solution)/shard_map/ppermute | solution.py:66
  77.2 7.5 %collective-permute-start.5 = (f32[6,8,512]{2,1,0:T(8,128)S(1)}, f32[6,8,512]{2,1,0:T(8,128)S(1)}, u32[]{:S(2)}, u32[]{:S(2)}) collective-permute-start(f32[6,8,512]{2,1,0:T(8,128)S(1)} %collective-permute-done.4), channel_id=1, source_target_pairs={{0,1},{1,2},{2,3},{3,4},{4,5},{5,6},{6,7},{7,0},{8,9},{9,10},{10,1... | collective-permute-start | bytes 294920 | tf_op jit(solution)/shard_map/ppermute | solution.py:64
  84.7 7.3 %collective-permute-start.6 = (f32[6,8,512]{2,1,0:T(8,128)S(1)}, f32[6,8,512]{2,1,0:T(8,128)S(1)}, u32[]{:S(2)}, u32[]{:S(2)}) collective-permute-start(f32[6,8,512]{2,1,0:T(8,128)S(1)} %collective-permute-done.5), channel_id=1, source_target_pairs={{0,1},{1,2},{2,3},{3,4},{4,5},{5,6},{6,7},{7,0},{8,9},{9,10},{10,1... | collective-permute-start | bytes 294920 | tf_op jit(solution)/shard_map/ppermute | solution.py:64
  92.1 8.3 %collective-permute-start.13 = (f32[1,3,8,8,512]{4,3,2,1,0:T(8,128)S(1)}, f32[1,3,8,8,512]{4,3,2,1,0:T(8,128)S(1)}, u32[]{:S(2)}, u32[]{:S(2)}) collective-permute-start(f32[1,3,8,8,512]{4,3,2,1,0:T(8,128)S(1)} %get-tuple-element.14), channel_id=1, source_target_pairs={{0,16},{8,56},{16,0},{24,40},{32,48},{40,24},{48,32},{56,8},{64,80... | collective-permute-start | bytes 1179656 | tf_op jit(solution)/shard_map/ppermute | solution.py:49
  93.2 8.2 %collective-permute-start.7 = (f32[1,3,8,8,512]{4,3,2,1,0:T(8,128)S(1)}, f32[1,3,8,8,512]{4,3,2,1,0:T(8,128)S(1)}, u32[]{:S(2)}, u32[]{:S(2)}) collective-permute-start(f32[1,3,8,8,512]{4,3,2,1,0:T(8,128)S(1)} %get-tuple-element.15), channel_id=1, source_target_pairs={{0,64},{8,200},{16,80},{24,216},{32,96},{40,232},{48,112},{56,248}... | collective-permute-start | bytes 1179656 | tf_op jit(solution)/shard_map/ppermute | solution.py:49
  100.5 11.4 %collective-permute-start.14 = (f32[2,3,8,8,512]{4,3,2,1,0:T(8,128)S(1)}, f32[2,3,8,8,512]{4,3,2,1,0:T(8,128)S(1)}, u32[]{:S(2)}, u32[]{:S(2)}) collective-permute-start(f32[2,3,8,8,512]{4,3,2,1,0:T(8,128)S(1)} %pad_maximum_fusion.6), channel_id=1, source_target_pairs={{0,192},{8,72},{16,208},{24,88},{32,224},{40,104},{48,240},{56,120... | collective-permute-start | bytes 2359304 | tf_op jit(solution)/shard_map/ppermute | solution.py:49
  101.6 12.5 %collective-permute-start.8 = (f32[2,3,8,8,512]{4,3,2,1,0:T(8,128)S(1)}, f32[2,3,8,8,512]{4,3,2,1,0:T(8,128)S(1)}, u32[]{:S(2)}, u32[]{:S(2)}) collective-permute-start(f32[2,3,8,8,512]{4,3,2,1,0:T(8,128)S(1)} %pad_maximum_fusion.5), channel_id=1, source_target_pairs={{0,16},{8,56},{16,0},{24,40},{32,48},{40,24},{48,32},{56,8},{64,80... | collective-permute-start | bytes 2359304 | tf_op jit(solution)/shard_map/ppermute | solution.py:49
  112.1 24.3 %collective-permute-start.15 = (f32[4,3,8,8,512]{4,3,2,1,0:T(8,128)S(1)}, f32[4,3,8,8,512]{4,3,2,1,0:T(8,128)S(1)}, u32[]{:S(2)}, u32[]{:S(2)}) collective-permute-start(f32[4,3,8,8,512]{4,3,2,1,0:T(8,128)S(1)} %pad_maximum_fusion.4), channel_id=1, source_target_pairs={{0,48},{8,24},{16,32},{24,8},{32,16},{40,56},{48,0},{56,40},{64,11... | collective-permute-start | bytes 4718600 | tf_op jit(solution)/shard_map/ppermute | solution.py:49
  114.2 24.6 %collective-permute-start.9 = (f32[4,3,8,8,512]{4,3,2,1,0:T(8,128)S(1)}, f32[4,3,8,8,512]{4,3,2,1,0:T(8,128)S(1)}, u32[]{:S(2)}, u32[]{:S(2)}) collective-permute-start(f32[4,3,8,8,512]{4,3,2,1,0:T(8,128)S(1)} %pad_maximum_fusion.3), channel_id=1, source_target_pairs={{0,192},{8,72},{16,208},{24,88},{32,224},{40,104},{48,240},{56,120... | collective-permute-start | bytes 4718600 | tf_op jit(solution)/shard_map/ppermute | solution.py:49
  138.5 49.1 %copy-start.12 = (s32[2]{0:T(128)S(1)}, s32[2]{0:T(128)}, u32[]{:S(2)}) copy-start(s32[2]{0:T(128)} %constant.131.clone) | copy-start | bytes 28
  138.5 49.3 %copy-start.7 = (s32[6,4,4]{0,2,1:T(4,128)S(1)}, s32[6,4,4]{0,2,1:T(4,128)}, u32[]{:S(2)}) copy-start(s32[6,4,4]{0,2,1:T(4,128)} %param.14) | copy-start | bytes 1156
  138.5 49.4 %copy-start.8 = (s32[1,2,16]{2,1,0:T(2,128)S(1)}, s32[1,2,16]{2,1,0:T(2,128)}, u32[]{:S(2)}) copy-start(s32[1,2,16]{2,1,0:T(2,128)} %constant.135) | copy-start | bytes 388
  138.5 49.4 %copy-start.9 = (s32[1,2,16]{2,1,0:T(2,128)S(1)}, s32[1,2,16]{2,1,0:T(2,128)}, u32[]{:S(2)}) copy-start(s32[1,2,16]{2,1,0:T(2,128)} %constant.136) | copy-start | bytes 388
  138.5 49.4 %copy-start.10 = (s32[1,2,16]{2,1,0:T(2,128)S(1)}, s32[1,2,16]{2,1,0:T(2,128)}, u32[]{:S(2)}) copy-start(s32[1,2,16]{2,1,0:T(2,128)} %constant.137) | copy-start | bytes 388
  138.5 49.4 %copy-start.11 = (s32[1,2,16]{2,1,0:T(2,128)S(1)}, s32[1,2,16]{2,1,0:T(2,128)}, u32[]{:S(2)}) copy-start(s32[1,2,16]{2,1,0:T(2,128)} %constant.138) | copy-start | bytes 388
  138.5 40.9 %collective-permute-start.16 = (f32[8,3,8,8,512]{4,3,2,1,0:T(8,128)}, f32[8,3,8,8,512]{4,3,2,1,0:T(8,128)}, u32[]{:S(2)}, u32[]{:S(2)}) collective-permute-start(f32[8,3,8,8,512]{4,3,2,1,0:T(8,128)} %pad_maximum_fusion.1.refs_4_), channel_id=1, source_target_pairs={{0,64},{8,200},{16,80},{24,216},{32,96},{40,232},{48,112},{56,248}... | collective-permute-start | bytes 9437192 | tf_op jit(solution)/shard_map/ppermute | solution.py:52
  139.1 40.3 %collective-permute-start.10 = (f32[8,3,8,8,512]{4,3,2,1,0:T(8,128)S(1)}, f32[8,3,8,8,512]{4,3,2,1,0:T(8,128)}, u32[]{:S(2)}, u32[]{:S(2)}) collective-permute-start(f32[8,3,8,8,512]{4,3,2,1,0:T(8,128)S(1)} %pad_maximum_fusion.refs_0_), channel_id=1, source_target_pairs={{0,48},{8,24},{16,32},{24,8},{32,16},{40,56},{48,0},{56,40},{64,11... | collective-permute-start | bytes 9437192 | tf_op jit(solution)/shard_map/ppermute | solution.py:52
  141.0 49.3 %collective-permute-start.17 = (f32[8,3,8,8,512]{4,3,2,1,0:T(8,128)}, f32[8,3,8,8,512]{4,3,2,1,0:T(8,128)}, u32[]{:S(2)}, u32[]{:S(2)}) collective-permute-start(f32[8,3,8,8,512]{4,3,2,1,0:T(8,128)} %pad_maximum_fusion.1.refs_4_), channel_id=1, source_target_pairs={{0,8},{8,0},{1,9},{9,1},{2,10},{10,2},{3,11},{11,3},{4,12},{12,4},... | collective-permute-start | bytes 9437192 | tf_op jit(solution)/shard_map/ppermute | solution.py:42
  149.1 41.1 %collective-permute-start.11 = (f32[8,3,8,8,512]{4,3,2,1,0:T(8,128)S(1)}, f32[8,3,8,8,512]{4,3,2,1,0:T(8,128)}, u32[]{:S(2)}, u32[]{:S(2)}) collective-permute-start(f32[8,3,8,8,512]{4,3,2,1,0:T(8,128)S(1)} %pad_maximum_fusion.refs_0_), channel_id=1, source_target_pairs={{0,8},{8,0},{1,9},{9,1},{2,10},{10,2},{3,11},{11,3},{4,12},{12,4},... | collective-permute-start | bytes 9437192 | tf_op jit(solution)/shard_map/ppermute | solution.py:42
  179.4 10.9 %collective-permute-start.18 = (f32[8,3,8,8,512]{4,3,2,1,0:T(8,128)}, f32[8,3,8,8,512]{4,3,2,1,0:T(8,128)}, u32[]{:S(2)}, u32[]{:S(2)}) collective-permute-start(f32[8,3,8,8,512]{4,3,2,1,0:T(8,128)} %collective-permute-done.16.refs_5_), channel_id=1, source_target_pairs={{0,8},{8,0},{1,9},{9,1},{2,10},{10,2},{3,11},{11,3},{4,12},{12,4},... | collective-permute-start | bytes 9437192 | tf_op jit(solution)/shard_map/ppermute | solution.py:42
  179.4 13.9 %collective-permute-start.12 = (f32[8,3,8,8,512]{4,3,2,1,0:T(8,128)}, f32[8,3,8,8,512]{4,3,2,1,0:T(8,128)}, u32[]{:S(2)}, u32[]{:S(2)}) collective-permute-start(f32[8,3,8,8,512]{4,3,2,1,0:T(8,128)} %collective-permute-done.10.refs_1_), channel_id=1, source_target_pairs={{0,8},{8,0},{1,9},{9,1},{2,10},{10,2},{3,11},{11,3},{4,12},{12,4},... | collective-permute-start | bytes 9437192 | tf_op jit(solution)/shard_map/ppermute | solution.py:42
  193.3 1.4 copy-start.3
  211.9 5.2 %collective-permute-start.25 = (f32[1,16,1536]{2,1,0:T(8,128)S(1)}, f32[1,16,1536]{2,1,0:T(8,128)S(1)}, u32[]{:S(2)}, u32[]{:S(2)}) collective-permute-start(f32[1,16,1536]{2,1,0:T(8,128)S(1)} %bitcast.70), channel_id=1, source_target_pairs={{0,16},{8,56},{16,0},{24,40},{32,48},{40,24},{48,32},{56,8},{64,80... | collective-permute-start | bytes 294920 | tf_op jit(solution)/shard_map/ppermute | solution.py:49
  212.0 5.2 %collective-permute-start.19 = (f32[1,16,1536]{2,1,0:T(8,128)S(1)}, f32[1,16,1536]{2,1,0:T(8,128)S(1)}, u32[]{:S(2)}, u32[]{:S(2)}) collective-permute-start(f32[1,16,1536]{2,1,0:T(8,128)S(1)} %bitcast.66), channel_id=1, source_target_pairs={{0,64},{8,200},{16,80},{24,216},{32,96},{40,232},{48,112},{56,248}... | collective-permute-start | bytes 294920 | tf_op jit(solution)/shard_map/ppermute | solution.py:49
  217.0 5.0 %collective-permute-start.26 = (f32[2,16,1536]{2,1,0:T(8,128)S(1)}, f32[2,16,1536]{2,1,0:T(8,128)S(1)}, u32[]{:S(2)}, u32[]{:S(2)}) collective-permute-start(f32[2,16,1536]{2,1,0:T(8,128)S(1)} %pad_maximum_fusion.12), channel_id=1, source_target_pairs={{0,192},{8,72},{16,208},{24,88},{32,224},{40,104},{48,240},{56,120... | collective-permute-start | bytes 589832 | tf_op jit(solution)/shard_map/ppermute | solution.py:49
  217.2 6.2 %collective-permute-start.20 = (f32[2,16,1536]{2,1,0:T(8,128)S(1)}, f32[2,16,1536]{2,1,0:T(8,128)S(1)}, u32[]{:S(2)}, u32[]{:S(2)}) collective-permute-start(f32[2,16,1536]{2,1,0:T(8,128)S(1)} %pad_maximum_fusion.11), channel_id=1, source_target_pairs={{0,16},{8,56},{16,0},{24,40},{32,48},{40,24},{48,32},{56,8},{64,80... | collective-permute-start | bytes 589832 | tf_op jit(solution)/shard_map/ppermute | solution.py:49
  222.1 7.0 %collective-permute-start.27 = (f32[4,16,1536]{2,1,0:T(8,128)S(1)}, f32[4,16,1536]{2,1,0:T(8,128)S(1)}, u32[]{:S(2)}, u32[]{:S(2)}) collective-permute-start(f32[4,16,1536]{2,1,0:T(8,128)S(1)} %pad_maximum_fusion.10), channel_id=1, source_target_pairs={{0,48},{8,24},{16,32},{24,8},{32,16},{40,56},{48,0},{56,40},{64,11... | collective-permute-start | bytes 1179656 | tf_op jit(solution)/shard_map/ppermute | solution.py:49
  223.4 7.3 %collective-permute-start.21 = (f32[4,16,1536]{2,1,0:T(8,128)S(1)}, f32[4,16,1536]{2,1,0:T(8,128)S(1)}, u32[]{:S(2)}, u32[]{:S(2)}) collective-permute-start(f32[4,16,1536]{2,1,0:T(8,128)S(1)} %pad_maximum_fusion.9), channel_id=1, source_target_pairs={{0,192},{8,72},{16,208},{24,88},{32,224},{40,104},{48,240},{56,120... | collective-permute-start | bytes 1179656 | tf_op jit(solution)/shard_map/ppermute | solution.py:49
  230.0 12.7 %collective-permute-start.28 = (f32[8,16,1536]{2,1,0:T(8,128)}, f32[8,16,1536]{2,1,0:T(8,128)}, u32[]{:S(2)}, u32[]{:S(2)}) collective-permute-start(f32[8,16,1536]{2,1,0:T(8,128)} %pad_maximum_fusion.8.refs_4_), channel_id=1, source_target_pairs={{0,64},{8,200},{16,80},{24,216},{32,96},{40,232},{48,112},{56,248}... | collective-permute-start | bytes 2359304 | tf_op jit(solution)/shard_map/ppermute | solution.py:52
  231.6 14.7 %collective-permute-start.22 = (f32[8,16,1536]{2,1,0:T(8,128)}, f32[8,16,1536]{2,1,0:T(8,128)}, u32[]{:S(2)}, u32[]{:S(2)}) collective-permute-start(f32[8,16,1536]{2,1,0:T(8,128)} %pad_maximum_fusion.7.refs_0_), channel_id=1, source_target_pairs={{0,48},{8,24},{16,32},{24,8},{32,16},{40,56},{48,0},{56,40},{64,11... | collective-permute-start | bytes 2359304 | tf_op jit(solution)/shard_map/ppermute | solution.py:52
  232.7 18.8 %collective-permute-start.29 = (f32[8,16,1536]{2,1,0:T(8,128)}, f32[8,16,1536]{2,1,0:T(8,128)}, u32[]{:S(2)}, u32[]{:S(2)}) collective-permute-start(f32[8,16,1536]{2,1,0:T(8,128)} %pad_maximum_fusion.8.refs_4_), channel_id=1, source_target_pairs={{0,8},{8,0},{1,9},{9,1},{2,10},{10,2},{3,11},{11,3},{4,12},{12,4},... | collective-permute-start | bytes 2359304 | tf_op jit(solution)/shard_map/ppermute | solution.py:42
  238.9 12.6 %collective-permute-start.23 = (f32[8,16,1536]{2,1,0:T(8,128)}, f32[8,16,1536]{2,1,0:T(8,128)}, u32[]{:S(2)}, u32[]{:S(2)}) collective-permute-start(f32[8,16,1536]{2,1,0:T(8,128)} %pad_maximum_fusion.7.refs_0_), channel_id=1, source_target_pairs={{0,8},{8,0},{1,9},{9,1},{2,10},{10,2},{3,11},{11,3},{4,12},{12,4},... | collective-permute-start | bytes 2359304 | tf_op jit(solution)/shard_map/ppermute | solution.py:42
  242.7 8.8 %collective-permute-start.30 = (f32[8,16,1536]{2,1,0:T(8,128)}, f32[8,16,1536]{2,1,0:T(8,128)}, u32[]{:S(2)}, u32[]{:S(2)}) collective-permute-start(f32[8,16,1536]{2,1,0:T(8,128)} %collective-permute-done.28.refs_5_), channel_id=1, source_target_pairs={{0,8},{8,0},{1,9},{9,1},{2,10},{10,2},{3,11},{11,3},{4,12},{12,4},... | collective-permute-start | bytes 2359304 | tf_op jit(solution)/shard_map/ppermute | solution.py:42
  246.3 5.2 %collective-permute-start.24 = (f32[8,16,1536]{2,1,0:T(8,128)}, f32[8,16,1536]{2,1,0:T(8,128)}, u32[]{:S(2)}, u32[]{:S(2)}) collective-permute-start(f32[8,16,1536]{2,1,0:T(8,128)} %collective-permute-done.22.refs_1_), channel_id=1, source_target_pairs={{0,8},{8,0},{1,9},{9,1},{2,10},{10,2},{3,11},{11,3},{4,12},{12,4},... | collective-permute-start | bytes 2359304 | tf_op jit(solution)/shard_map/ppermute | solution.py:42
  251.5 8.5 %copy-start.2 = (f32[512,1664]{1,0:T(8,128)S(1)}, f32[512,1664]{1,0:T(8,128)}, u32[]{:S(2)}) copy-start(f32[512,1664]{1,0:T(8,128)} %weights.1) | copy-start | bytes 10223620
  256.3 3.7 %copy-start = (bf16[6,512,1536]{2,1,0:T(8,128)(2,1)}, bf16[6,512,1536]{2,1,0:T(8,128)(2,1)S(1)}, u32[]{:S(2)}) copy-start(bf16[6,512,1536]{2,1,0:T(8,128)(2,1)S(1)} %assemble.1.errors) | copy-start | bytes 28311556
  259.9 3.7 %copy-start.1 = (bf16[6,512,1536]{2,1,0:T(8,128)(2,1)S(1)}, bf16[6,512,1536]{2,1,0:T(8,128)(2,1)}, u32[]{:S(2)}) copy-start(bf16[6,512,1536]{2,1,0:T(8,128)(2,1)} %copy-done) | copy-start | bytes 28311556
Sparse Core Ops, SparseCore 0:
  9.1 219.1 all-gather.1

commit v2 on v1

--- a/solution.py
+++ b/solution.py
@@ -19,6 +19,8 @@
 BLOCKS = [(k, m) for k in range(P_SIZE) for m in range(k + 1)]
 SLOTS = 6
 HALF = SLOTS // 2
+EARLY = 4
+ROUND = 4
 MINE = 16
 NARROW = 256
 
@@ -42,17 +44,23 @@
     return lax.ppermute(value, "col_2", [(0, 1), (1, 0)])
 
 
-def spread(streams):
+def after(values, event):
+    return list(lax.optimization_barrier((*values, event))[:-1])
+
+
+def doubled(streams):
     near = [value[None] for value in streams]
     for stage in range(3):
         near = [
             jnp.concatenate([value, lax.ppermute(value, COL, exchange(i, stage))], 0)
             for i, value in enumerate(near)
         ]
+    return near
+
+
+def completed(near):
     far = [lax.ppermute(value, COL, exchange(i, 3)) for i, value in enumerate(near)]
-    return [
-        [near[i], far[i], other_core(near[i]), other_core(far[i])] for i in range(len(streams))
-    ]
+    return [[near[i], far[i], other_core(near[i]), other_core(far[i])] for i in range(len(near))]
 
 
 def all_rows(value):
@@ -122,36 +130,48 @@
     return copies
 
 
-def solve_kernel(source, flags, *refs):
-    parts, (windows, inverse), outs = refs[:8], refs[8:10], refs[10:12]
-    blocks, errors, semaphores = refs[12:]
+def solve_kernel(early, source, flags, *refs):
+    refs = list(refs)
+    parts = [refs.pop(0) for _ in range(8)]
+    windows, inverse = refs.pop(0), refs.pop(0)
+    before = [] if early else [refs.pop(0) for _ in range(3)]
+    outs = [refs.pop(0) for _ in range(3 if early else 2)]
+    blocks, errors, semaphores = refs
 
     def place(stream, number):
-        place_of = source[number]
-        return blocks.at[pl.ds(stream * HALF, HALF), place_of // 8, :, lax.rem(place_of, 8)]
+        there = source[number]
+        depth = pl.ds(stream * ROUND, ROUND)
+        return blocks.at[:, there // 8, depth, lax.rem(there, 8)]
 
     copies = unit_copies(parts, place, semaphores)
     for group in copies:
         for copy in group:
             copy.start()
-    for copy in copies[0]:
-        copy.wait()
-    arrived = 1
+    for k in range(0 if early else EARLY):
+        column = k % 2 * PW
+        high, low = halves(before[k // 2][:, column : column + PW])
+        errors[k, 0] = high
+        errors[k, 1] = low
+    for group in copies:
+        for copy in group:
+            copy.wait()
 
     def block_at(number):
         return halves(blocks[number // 4, lax.rem(number, 4)].reshape(PW, PW))
 
-    for k in range(P_SIZE):
-        base = k * (k + 1) // 2
-        if base + k >= 4 * HALF and arrived == 1:
-            for copy in copies[1]:
-                copy.wait()
-            arrived = 2
-
-        def take(m, acc, base=base):
+    def less(acc, base, first, last):
+        def take(m, acc):
             return acc - product((errors[m, 0], errors[m, 1]), block_at(base + m))
 
-        window = lax.fori_loop(0, k, take, windows[k])
+        return lax.fori_loop(first, last, take, acc)
+
+    skip = 0 if early else 4 * HALF
+    for k in range(EARLY) if early else range(EARLY, P_SIZE):
+        base = k * (k + 1) // 2 - skip
+        if k == EARLY:
+            window = less(before[2][...], base, -base, k)
+        else:
+            window = less(windows[k], base, 0, k)
         block = block_at(base + k)
         done = []
         for a in range(PANEL_TILES):
@@ -163,44 +183,101 @@
             acc = product(halves(acc), halves(inverse[k, a]))
             acc = jnp.where(flags[k, a] != 0, acc, 0.0)
             done.append(halves(acc))
-            column = (k % 3) * PW + a * TILE
-            outs[k // 3][:, column : column + TILE] = acc
+            stream, column = (k // 2, k % 2 * PW) if early else (k - EARLY, 0)
+            outs[stream][:, column + a * TILE : column + (a + 1) * TILE] = acc
         for i in range(2):
             errors[k, i] = jnp.concatenate([d[i] for d in done], 1)
-
-
-def assemble_kernel(source, *refs):
+    if early:
+        base = EARLY * (EARLY + 1) // 2
+        outs[2][...] = less(windows[EARLY], base, 0, 4 * HALF - base)
+
+
+def solve(early, source, flags, parts, windows, inverse, before):
+    smem = pl.BlockSpec(memory_space=pltpu.SMEM)
+    vmem = pl.BlockSpec(memory_space=pltpu.VMEM)
+    widths = (2 * PW, 2 * PW, PW) if early else (PW, PW)
+    return pl.pallas_call(
+        functools.partial(solve_kernel, early),
+        out_shape=[jax.ShapeDtypeStruct((MINE, width), jnp.float32) for width in widths],
+        in_specs=[smem, smem]
+        + [pl.BlockSpec(memory_space=pl.ANY)] * 8
+        + [vmem] * (2 + len(before)),
+        out_specs=[vmem] * len(widths),
+        scratch_shapes=[
+            pltpu.VMEM((HALF, 4, 8, 8, 8, PW), jnp.float32),
+            pltpu.VMEM((P_SIZE, 2, MINE, PW), jnp.bfloat16),
+            pltpu.SemaphoreType.DMA((64,)),
+        ],
+        compiler_params=pltpu.CompilerParams(vmem_limit_bytes=56 << 20),
+        cost_estimate=pl.CostEstimate(
+            flops=6_000_000_000, bytes_accessed=12 << 20, transcendentals=0
+        ),
+        name="solve_early" if early else "solve_late",
+    )(source, flags, *parts[0], *parts[1], windows, inverse, *before)
+
+
+def assemble_kernel(panels, source, *refs):
     parts, (out, errors, semaphores) = refs[:8], refs[8:]
+    n = pl.program_id(0)
 
     def place(stream, number):
         first = pl.multiple_of(source[number] * MINE, MINE)
         return errors.at[stream, pl.ds(first, MINE)]
 
-    copies = unit_copies(parts, place, semaphores)
-    for group in copies:
-        for copy in group:
-            copy.start()
-    for stream, group in enumerate(copies):
-        for copy in group:
-            copy.wait()
-        for k in range(3 * stream, 3 * stream + 3):
-            high, low = halves(errors[stream, :, (k % 3) * PW : (k % 3 + 1) * PW])
-            out[k, :, :PW] = high
-            out[k, :, PW : 2 * PW] = low
-            out[k, :, 2 * PW :] = high
-
-
-def update_kernel(flags, errors, weights, factor, out):
+    @pl.when(n == 0)
+    def _():
+        copies = unit_copies(parts, place, semaphores)
+        for group in copies:
+            for copy in group:
+                copy.start()
+        for group in copies:
+            for copy in group:
+                copy.wait()
+
+    column = pl.multiple_of(lax.rem(n, panels) * PW, PW)
+    high, low = halves(errors[n // panels, :, pl.ds(column, PW)])
+    out[0, :, :PW] = high
+    out[0, :, PW : 2 * PW] = low
+    out[0, :, 2 * PW :] = high
+
+
+def assemble(panels, rows, source, parts):
+    return pl.pallas_call(
+        functools.partial(assemble_kernel, panels),
+        out_shape=jax.ShapeDtypeStruct((2 * panels, rows, 3 * PW), jnp.bfloat16),
+        grid_spec=pltpu.PrefetchScalarGridSpec(
+            num_scalar_prefetch=1,
+            grid=(2 * panels,),
+            in_specs=[pl.BlockSpec(memory_space=pl.ANY)] * 8,
+            out_specs=pl.BlockSpec((1, rows, 3 * PW), lambda i, *_: (i, 0, 0)),
+            scratch_shapes=[
+                pltpu.VMEM((2, rows, panels * PW), jnp.float32),
+                pltpu.SemaphoreType.DMA((64,)),
+            ],
+        ),
+        compiler_params=pltpu.CompilerParams(vmem_limit_bytes=56 << 20),
+        cost_estimate=pl.CostEstimate(
+            flops=20_000_000, bytes_accessed=panels << 22, transcendentals=0
+        ),
+        name=f"assemble_{panels}",
+    )(source, *parts[0], *parts[1])
+
+
+def update_kernel(flags, early, late, weights, factor, out):
     n = pl.program_id(0)
     out[...] = weights[...]
 
-    def take(k, carry):
-        high, low = halves(factor[k])
-        rows = jnp.concatenate([high, high, low], 0)
-        out[...] = out[...] - jnp.dot(errors[k], rows, preferred_element_type=jnp.float32)
-        return carry
-
-    lax.fori_loop(0, P_SIZE, take, 0)
+    def less(first, errors):
+        def take(k, carry):
+            high, low = halves(factor[first + k])
+            rows = jnp.concatenate([high, high, low], 0)
+            out[...] = out[...] - jnp.dot(errors[k], rows, preferred_element_type=jnp.float32)
+            return carry
+
+        lax.fori_loop(0, errors.shape[0], take, 0)
+
+    less(0, early)
+    less(EARLY, late)
     for part in range(NARROW // TILE):
         tile = n * (NARROW // TILE) + part - flags[0]
         inside = jnp.logical_and(tile >= 0, tile < PANEL_TILES)
@@ -242,41 +319,24 @@
     windows = arrived[(owner[:, None] * 4 + jnp.array([2, 3], jnp.int32)).reshape(-1)]
     windows = windows.reshape(P_SIZE, MINE, PW)
     source = sources()
-    spread_parts = spread([picked[:HALF], picked[HALF:]])
-
     own_rows = lax.dynamic_slice(prune_mask, (0, me // 8, 0), (P_SIZE, 1, PANEL_TILES))[:, 0]
-    any_spec = pl.BlockSpec(memory_space=pl.ANY)
-    vmem = pl.BlockSpec(memory_space=pltpu.VMEM)
-    smem = pl.BlockSpec(memory_space=pltpu.SMEM)
-    found = pl.pallas_call(
-        solve_kernel,
-        out_shape=[jax.ShapeDtypeStruct((MINE, 3 * PW), jnp.float32)] * 2,
-        in_specs=[smem, smem] + [any_spec] * 8 + [vmem, vmem],
-        out_specs=[vmem, vmem],
-        scratch_shapes=[
-            pltpu.VMEM((SLOTS, 4, 8, 8, 8, PW), jnp.float32),
-            pltpu.VMEM((P_SIZE, 2, MINE, PW), jnp.bfloat16),
-            pltpu.SemaphoreType.DMA((64,)),
-        ],
-        compiler_params=pltpu.CompilerParams(vmem_limit_bytes=48 << 20),
-        name="solve",
-    )(source, own_rows, *spread_parts[0], *spread_parts[1], windows, diag_inverse)
-
-    spread_errors = spread(found)
+    near = doubled([picked[:HALF, :ROUND], picked[:HALF, ROUND:]])
+    late = after([picked[HALF:, :ROUND], picked[HALF:, ROUND:]], near[0][0, 0, 0, 0, :1])
+    found = solve(True, source, own_rows, completed(near), windows, diag_inverse, [])
+    near = after(doubled(late), found[0][0, :1])
+    spread = completed(doubled(found[:2]))
+    early = assemble(2, rows, source, spread)
+    far = completed(near)
+    event = spread[0][3][0, 0, :1]
+    far = [after(parts[:3], event) + parts[3:] for parts in far]
+    found = solve(False, source, own_rows, far, windows, diag_inverse, found)
+    late = assemble(1, rows, source, completed(doubled(found)))
+
     pruned = jnp.sum(jnp.where(mine[:, None, None], prune_mask, 0), 0).reshape(-1)
     flags = jnp.concatenate([(shift // TILE)[None], pruned]).astype(jnp.int32)
-    split = pl.pallas_call(
-        assemble_kernel,
-        out_shape=jax.ShapeDtypeStruct((P_SIZE, rows, 3 * PW), jnp.bfloat16),
-        in_specs=[smem] + [any_spec] * 8,
-        out_specs=vmem,
-        scratch_shapes=[
-            pltpu.VMEM((2, rows, 3 * PW), jnp.float32),
-            pltpu.SemaphoreType.DMA((64,)),
-        ],
-        compiler_params=pltpu.CompilerParams(vmem_limit_bytes=24 << 20),
-        name="assemble",
-    )(source, *spread_errors[0], *spread_errors[1])
+    whole = lambda value: pl.BlockSpec(
+        value.shape, lambda i, *_: (0, 0, 0), pipeline_mode=pl.Buffered(1)
+    )
     steps = pl.cdiv(width, NARROW)
     column = lambda i, *_: (0, i)
     return pl.pallas_call(
@@ -286,15 +346,16 @@
             num_scalar_prefetch=1,
             grid=(steps,),
             in_specs=[
-                vmem,
+                whole(early),
+                whole(late),
                 pl.BlockSpec((rows, NARROW), column),
                 pl.BlockSpec((P_SIZE, PW, NARROW), lambda i, *_: (0, 0, i)),
             ],
             out_specs=pl.BlockSpec((rows, NARROW), column),
         ),
-        compiler_params=pltpu.CompilerParams(vmem_limit_bytes=40 << 20),
+        compiler_params=pltpu.CompilerParams(vmem_limit_bytes=56 << 20),
         name="update",
-    )(flags, split, weights, gathered)
+    )(flags, early, late, weights, gathered)
 
 
 def solution(mesh):

time: 300 us -> 345 us (1.15); the launches traced: 299 us -> 339 us
  starting transfers between devices: 64.7 us -> 86.9 us
  Pallas kernels: 50.6 us -> 69.5 us
  other arithmetic: 8.75 us -> 20.4 us
  waiting for transfers between devices: 138 us -> 128 us
  local copies, waits for them, and re-layouts: 18 us -> 14.3 us
    ppermute x16 -> x32, starting transfers between devices: 14.1 us -> 32.6 us  [the longest x24 27.7 us: doubled(): lax.ppermute(value, COL, exchange(i, stage))]
    pallas_call x2 -> x4, Pallas kernels: 21.9 us -> 37.9 us  [the longest x2 26.6 us: solve(): pl.pallas_call(functools.partial(solve_kernel, early), out_shape=[jax.Sha...]
    concatenate x12 -> x24, other arithmetic: 4.77 us -> 17.1 us  [doubled(): jnp.concatenate([value, lax.ppermute(value, COL, exchange(i, stage))], 0)]
    ppermute x16 -> x32, waiting for transfers between devices: 84.5 us -> 76.6 us  [the longest x24 67.3 us: doubled(): lax.ppermute(value, COL, exchange(i, stage))]
    unnamed x26 -> x58, local copies, waits for them, and re-layouts: 8.78 us -> 4.89 us
    ppermute x8 -> x16, starting transfers between devices: 29.1 us -> 32.9 us  [other_core(): return lax.ppermute(value, 'col_2', [(0, 1), (1, 0)])]
  transfers between devices with their start and end apart: 33 -> 57, of which waited for: 17 -> 24; matrix products, arithmetic and copies ran while one was open for 6% -> 9% of each run, Pallas kernels for 7% -> 11%
where the time goes in v2:
time: 345 us; the launch traced here: 339 us
  waiting for transfers between devices  128 us (37%)
  starting transfers between devices  86.9 us (25%)
  Pallas kernels  69.5 us (20%)
  other arithmetic  20.4 us (6%)
  between operations  19.9 us (6%)
  local copies, waits for them, and re-layouts  14.3 us (4%)
    ppermute x24, waiting for transfers between devices, doubled(): lax.ppermute(value, COL, exchange(i, stage))  67.3 us
    ppermute x16, starting transfers between devices, other_core(): return lax.ppermute(value, 'col_2', [(0, 1), (1, 0)])  32.9 us
    pallas_call x1, Pallas kernels, shards(): pl.pallas_call(update_kernel, out_shape=jax.ShapeDtypeStruct(weights.shap...  31.5 us
    ppermute x24, starting transfers between devices, doubled(): lax.ppermute(value, COL, exchange(i, stage))  27.7 us
    pallas_call x2, Pallas kernels, solve(): pl.pallas_call(functools.partial(solve_kernel, early), out_shape=[jax.Sha...  26.6 us
    all_to_all x1, waiting for transfers between devices, shards(): lax.all_to_all(jnp.concatenate([eighths, wanted], 1), COL, 0, 0, tiled=True)  26.2 us
    concatenate x24, other arithmetic, doubled(): jnp.concatenate([value, lax.ppermute(value, COL, exchange(i, stage))], 0)  17.1 us
    ppermute x4, waiting for transfers between devices, all_rows(): below.append(lax.ppermute(below[-1], 'row', up))  14.7 us
  transfers between devices with their start and end apart: 57, of which 24 were waited for; matrix products, arithmetic and copies ran while one was open for 9% of the time, Pallas kernels for 11%

profile of v2, /device:TPU:1, one launch (start us, length us, event | category | flops | bytes accessed | tf_op | source)
XLA Modules:
  0.0 339.3 jit_solution(14517152578471058911)
XLA Ops:
  11.6 1.5 dynamic-slice_bitcast_fusion
  13.8 1.7 constant_dynamic-slice_fusion
  15.5 1.5 pad_maximum_fusion
  17.0 8.7 %all-to-all-start = ((f32[32,32,512]{2,1,0:T(8,128)}), f32[32,32,512]{2,1,0:T(8,128)S(1)}, u32[]{:S(2)}, u32[]{:S(2)}) async-start(f32[32,32,512]{2,1,0:T(8,128)} %pad_maximum_fusion), calls=%async_computation | async-start | bytes 4194304 | tf_op jit(solution)/shard_map/all_to_all | solution.py:311
  27.8 26.2 %all-to-all-done = f32[32,32,512]{2,1,0:T(8,128)S(1)} async-done(((f32[32,32,512]{2,1,0:T(8,128)}), f32[32,32,512]{2,1,0:T(8,128)S(1)}, u32[]{:S(2)}, u32[]{:S(2)}) %all-to-all-start) | async-done | bytes 2097184 | tf_op jit(solution)/shard_map/all_to_all | solution.py:311
  54.6 5.7 %collective-permute-start = (f32[6,8,512]{2,1,0:T(8,128)S(1)}, f32[6,8,512]{2,1,0:T(8,128)S(1)}, u32[]{:S(2)}, u32[]{:S(2)}) collective-permute-start(f32[6,8,512]{2,1,0:T(8,128)S(1)} %gather_fusion.4), channel_id=1, source_target_pairs={{0,7},{1,0},{2,1},{3,2},{4,3},{5,4},{6,5},{7,6},{8,15},{9,8},{10,9... | collective-permute-start | bytes 294920 | tf_op jit(solution)/shard_map/ppermute | solution.py:74
  60.3 4.3 %collective-permute-done = f32[6,8,512]{2,1,0:T(8,128)S(1)} collective-permute-done((f32[6,8,512]{2,1,0:T(8,128)S(1)}, f32[6,8,512]{2,1,0:T(8,128)S(1)}, u32[]{:S(2)}, u32[]{:S(2)}) %collective-permute-start) | collective-permute-done | bytes 98336 | tf_op jit(solution)/shard_map/ppermute | solution.py:74
  64.7 3.5 %collective-permute-start.1 = (f32[6,8,512]{2,1,0:T(8,128)S(1)}, f32[6,8,512]{2,1,0:T(8,128)S(1)}, u32[]{:S(2)}, u32[]{:S(2)}) collective-permute-start(f32[6,8,512]{2,1,0:T(8,128)S(1)} %collective-permute-done), channel_id=1, source_target_pairs={{0,7},{1,0},{2,1},{3,2},{4,3},{5,4},{6,5},{7,6},{8,15},{9,8},{10,9... | collective-permute-start | bytes 294920 | tf_op jit(solution)/shard_map/ppermute | solution.py:74
  68.2 4.2 %collective-permute-done.1 = f32[6,8,512]{2,1,0:T(8,128)S(1)} collective-permute-done((f32[6,8,512]{2,1,0:T(8,128)S(1)}, f32[6,8,512]{2,1,0:T(8,128)S(1)}, u32[]{:S(2)}, u32[]{:S(2)}) %collective-permute-start.1) | collective-permute-done | bytes 98336 | tf_op jit(solution)/shard_map/ppermute | solution.py:74
  72.5 3.5 %collective-permute-start.2 = (f32[6,8,512]{2,1,0:T(8,128)S(1)}, f32[6,8,512]{2,1,0:T(8,128)S(1)}, u32[]{:S(2)}, u32[]{:S(2)}) collective-permute-start(f32[6,8,512]{2,1,0:T(8,128)S(1)} %collective-permute-done.1), channel_id=1, source_target_pairs={{0,7},{1,0},{2,1},{3,2},{4,3},{5,4},{6,5},{7,6},{8,15},{9,8},{10,9... | collective-permute-start | bytes 294920 | tf_op jit(solution)/shard_map/ppermute | solution.py:74
  76.0 7.4 %collective-permute-done.5 = f32[6,8,512]{2,1,0:T(8,128)S(1)} collective-permute-done((f32[6,8,512]{2,1,0:T(8,128)S(1)}, f32[6,8,512]{2,1,0:T(8,128)S(1)}, u32[]{:S(2)}, u32[]{:S(2)}) %collective-permute-start.5) | collective-permute-done | bytes 98336 | tf_op jit(solution)/shard_map/ppermute | solution.py:72
  83.5 7.3 %collective-permute-done.6 = f32[6,8,512]{2,1,0:T(8,128)S(1)} collective-permute-done((f32[6,8,512]{2,1,0:T(8,128)S(1)}, f32[6,8,512]{2,1,0:T(8,128)S(1)}, u32[]{:S(2)}, u32[]{:S(2)}) %collective-permute-start.6) | collective-permute-done | bytes 98336 | tf_op jit(solution)/shard_map/ppermute | solution.py:72
  92.3 4.8 %collective-permute-done.13 = f32[1,3,4,8,512]{4,3,2,1,0:T(8,128)S(1)} collective-permute-done((f32[1,3,4,8,512]{4,3,2,1,0:T(8,128)S(1)}, f32[1,3,4,8,512]{4,3,2,1,0:T(8,128)S(1)}, u32[]{:S(2)}, u32[]{:S(2)}) %collective-permute-start.13) | collective-permute-done | bytes 196640 | tf_op jit(solution)/shard_map/ppermute | solution.py:55
  98.1 1.8 collective-permute-start.8
  99.9 4.5 %collective-permute-done.14 = f32[2,3,4,8,512]{4,3,2,1,0:T(8,128)S(1)} collective-permute-done((f32[2,3,4,8,512]{4,3,2,1,0:T(8,128)S(1)}, f32[2,3,4,8,512]{4,3,2,1,0:T(8,128)S(1)}, u32[]{:S(2)}, u32[]{:S(2)}) %collective-permute-start.14) | collective-permute-done | bytes 393248 | tf_op jit(solution)/shard_map/ppermute | solution.py:55
  104.6 1.9 collective-permute-done.8
  108.4 10.5 %collective-permute-done.15 = f32[4,3,4,8,512]{4,3,2,1,0:T(8,128)S(1)} collective-permute-done((f32[4,3,4,8,512]{4,3,2,1,0:T(8,128)S(1)}, f32[4,3,4,8,512]{4,3,2,1,0:T(8,128)S(1)}, u32[]{:S(2)}, u32[]{:S(2)}) %collective-permute-start.15) | collective-permute-done | bytes 786464 | tf_op jit(solution)/shard_map/ppermute | solution.py:55
  118.9 1.4 pad_maximum_fusion.2.refs_4_
  124.0 2.0 collective-permute-start.31
  126.1 6.6 %collective-permute-done.35 = f32[2,3,4,8,512]{4,3,2,1,0:T(8,128)S(1)} collective-permute-done((f32[2,3,4,8,512]{4,3,2,1,0:T(8,128)S(1)}, f32[2,3,4,8,512]{4,3,2,1,0:T(8,128)S(1)}, u32[]{:S(2)}, u32[]{:S(2)}) %collective-permute-start.35) | collective-permute-done | bytes 393248 | tf_op jit(solution)/shard_map/ppermute | solution.py:55
  132.8 2.7 collective-permute-start.36
  135.4 12.5 %collective-permute-start.17 = (f32[8,3,4,8,512]{4,3,2,1,0:T(8,128)}, f32[8,3,4,8,512]{4,3,2,1,0:T(8,128)}, u32[]{:S(2)}, u32[]{:S(2)}) collective-permute-start(f32[8,3,4,8,512]{4,3,2,1,0:T(8,128)} %pad_maximum_fusion.2.refs_4_), channel_id=1, source_target_pairs={{0,8},{8,0},{1,9},{9,1},{2,10},{10,2},{3,11},{11,3},{4,12},{12,4},... | collective-permute-start | bytes 4718600 | tf_op jit(solution)/shard_map/ppermute | solution.py:44
  148.0 2.4 collective-permute-done.31
  150.6 12.3 %collective-permute-done.32 = f32[2,3,4,8,512]{4,3,2,1,0:T(8,128)S(1)} collective-permute-done((f32[2,3,4,8,512]{4,3,2,1,0:T(8,128)S(1)}, f32[2,3,4,8,512]{4,3,2,1,0:T(8,128)S(1)}, u32[]{:S(2)}, u32[]{:S(2)}) %collective-permute-start.32) | collective-permute-done | bytes 393248 | tf_op jit(solution)/shard_map/ppermute | solution.py:55
  167.9 2.6 pad_maximum_fusion.4.refs_4_
  170.5 5.6 %collective-permute-done.33 = f32[4,3,4,8,512]{4,3,2,1,0:T(8,128)} collective-permute-done((f32[4,3,4,8,512]{4,3,2,1,0:T(8,128)}, f32[4,3,4,8,512]{4,3,2,1,0:T(8,128)}, u32[]{:S(2)}, u32[]{:S(2)}) %collective-permute-start.33) | collective-permute-done | bytes 786464 | tf_op jit(solution)/shard_map/ppermute | solution.py:55
  176.2 2.5 pad_maximum_fusion.3.refs_0_
  181.6 14.6 %solve_early.1 = (f32[16,1024]{1,0:T(8,128)}, f32[16,1024]{1,0:T(8,128)}, f32[16,512]{1,0:T(8,128)}) custom-call(s32[64]{0:T(128)} %reshape.308.source, s32[6,4]{1,0:T(8,128)} %copy.41.flags, f32[8,3,4,8,512]{4,3,2,1,0:T(8,128)} %pad_maximum_fusion.1.refs_0_, f32[8,3,4,8,512]{4,3,2,1,0:T(8,128)} %collective-permute-done.10.refs_1_, ...), custom_call_target="tpu_custom_call" | custom-call | flops 6000000000 | bytes 12582912 | tf_op jit(solution)/shard_map/solve_early/pallas_call | solution.py:199
  196.3 2.8 collective-permute-start.19
  199.7 1.6 collective-permute-done.19
  202.2 9.7 %collective-permute-start.20 = (f32[2,16,1024]{2,1,0:T(8,128)S(1)}, f32[2,16,1024]{2,1,0:T(8,128)S(1)}, u32[]{:S(2)}, u32[]{:S(2)}) collective-permute-start(f32[2,16,1024]{2,1,0:T(8,128)S(1)} %pad_maximum_fusion.19), channel_id=1, source_target_pairs={{0,16},{8,56},{16,0},{24,40},{32,48},{40,24},{48,32},{56,8},{64,80... | collective-permute-start | bytes 393224 | tf_op jit(solution)/shard_map/ppermute | solution.py:55
  212.8 3.8 %collective-permute-done.20 = f32[2,16,1024]{2,1,0:T(8,128)S(1)} collective-permute-done((f32[2,16,1024]{2,1,0:T(8,128)S(1)}, f32[2,16,1024]{2,1,0:T(8,128)S(1)}, u32[]{:S(2)}, u32[]{:S(2)}) %collective-permute-start.20) | collective-permute-done | bytes 131104 | tf_op jit(solution)/shard_map/ppermute | solution.py:55
  219.5 3.6 %collective-permute-done.21 = f32[4,16,1024]{2,1,0:T(8,128)S(1)} collective-permute-done((f32[4,16,1024]{2,1,0:T(8,128)S(1)}, f32[4,16,1024]{2,1,0:T(8,128)S(1)}, u32[]{:S(2)}, u32[]{:S(2)}) %collective-permute-start.21) | collective-permute-done | bytes 262176 | tf_op jit(solution)/shard_map/ppermute | solution.py:55
  223.2 5.5 %collective-permute-done.27 = f32[4,16,1024]{2,1,0:T(8,128)S(1)} collective-permute-done((f32[4,16,1024]{2,1,0:T(8,128)S(1)}, f32[4,16,1024]{2,1,0:T(8,128)S(1)}, u32[]{:S(2)}, u32[]{:S(2)}) %collective-permute-start.27) | collective-permute-done | bytes 262176 | tf_op jit(solution)/shard_map/ppermute | solution.py:55
  228.8 8.2 %collective-permute-done.22.refs_1_ = f32[8,16,1024]{2,1,0:T(8,128)S(1)} collective-permute-done((f32[8,16,1024]{2,1,0:T(8,128)S(1)}, f32[8,16,1024]{2,1,0:T(8,128)S(1)}, u32[]{:S(2)}, u32[]{:S(2)}) %collective-permute-start.22) | collective-permute-done | bytes 524320 | tf_op jit(solution)/shard_map/ppermute | solution.py:62
  237.0 2.8 collective-permute-start.24
  239.8 1.5 collective-permute-done.24.refs_3_
  241.3 1.7 collective-permute-start.28
  244.7 12.0 %solve_late.1 = (f32[16,512]{1,0:T(8,128)}, f32[16,512]{1,0:T(8,128)}) custom-call(s32[64]{0:T(128)} %reshape.308.source, s32[6,4]{1,0:T(8,128)} %copy.41.flags, f32[8,3,4,8,512]{4,3,2,1,0:T(8,128)} %pad_maximum_fusion.3.refs_0_, f32[8,3,4,8,512]{4,3,2,1,0:T(8,128)} %collective-permute-done.37.refs_1_, f32[8,3,4,8,512]{4,3,2,1,0:T(8,128)} %copy-done.28, ...), custom_call_target="tpu_custom_call" | custom-call | flops 6000000000 | bytes 12582912 | tf_op jit(solution)/shard_map/solve_late/pallas_call | solution.py:199
  256.7 1.7 collective-permute-start.49
  258.8 2.2 collective-permute-done.49
  265.7 3.1 collective-permute-start.29
  269.8 3.2 collective-permute-start.30
  275.1 4.0 %collective-permute-start.53 = (f32[8,16,512]{2,1,0:T(8,128)S(1)}, f32[8,16,512]{2,1,0:T(8,128)S(1)}, u32[]{:S(2)}, u32[]{:S(2)}) collective-permute-start(f32[8,16,512]{2,1,0:T(8,128)S(1)} %pad_maximum_fusion.18.refs_4_), channel_id=1, source_target_pairs={{0,8},{8,0},{1,9},{9,1},{2,10},{10,2},{3,11},{11,3},{4,12},{12,4},... | collective-permute-start | bytes 786440 | tf_op jit(solution)/shard_map/ppermute | solution.py:44
  280.9 3.9 %collective-permute-start.48 = (f32[8,16,512]{2,1,0:T(8,128)S(1)}, f32[8,16,512]{2,1,0:T(8,128)}, u32[]{:S(2)}, u32[]{:S(2)}) collective-permute-start(f32[8,16,512]{2,1,0:T(8,128)S(1)} %collective-permute-done.46.refs_1_), channel_id=1, source_target_pairs={{0,8},{8,0},{1,9},{9,1},{2,10},{10,2},{3,11},{11,3},{4,12},{12,4},... | collective-permute-start | bytes 786440 | tf_op jit(solution)/shard_map/ppermute | solution.py:44
  288.6 6.7 %assemble_2.1.early = bf16[4,512,1536]{2,1,0:T(8,128)(2,1)} custom-call(s32[64]{0:T(128)} %reshape.308.source, f32[8,16,1024]{2,1,0:T(8,128)} %copy-done.2, f32[8,16,1024]{2,1,0:T(8,128)} %copy-done.11, f32[8,16,1024]{2,1,0:T(8,128)} %copy-done.15, f32[8,16,1024]{2,1,0:T(8,128)} %copy-done.12, f32[8,16,1024]{2,1,0:T(8,128)} %copy-done.3, ...), custom_call_target="tpu_custom_call" | custom-call | flops 20000000 | bytes 8388608 | tf_op jit(solution)/shard_map/assemble_2/pallas_call | solution.py:245
  296.0 4.6 %assemble_1.1.late = bf16[2,512,1536]{2,1,0:T(8,128)(2,1)} custom-call(s32[64]{0:T(128)} %reshape.308.source, f32[8,16,512]{2,1,0:T(8,128)} %copy-done.7, f32[8,16,512]{2,1,0:T(8,128)} %copy-done.18, f32[8,16,512]{2,1,0:T(8,128)} %collective-permute-done.47.refs_2_, f32[8,16,512]{2,1,0:T(8,128)} %collective-permute-done.48.refs_3_, f32[8,16,512]{2,1,0:T(8,128)} %copy-done.6, ...), custom_call_target="tpu_custom_call" | custom-call | flops 20000000 | bytes 4194304 | tf_op jit(solution)/shard_map/assemble_1/pallas_call | solution.py:245
  300.7 31.5 %update.1 = f32[512,1664]{1,0:T(8,128)} custom-call(s32[17]{0:T(128)} %pad_add_fusion.1.flags, bf16[4,512,1536]{2,1,0:T(8,128)(2,1)} %assemble_2.1.early, bf16[2,512,1536]{2,1,0:T(8,128)(2,1)} %assemble_1.1.late, f32[512,1664]{1,0:T(8,128)} %weights.1, f32[6,512,1664]{2,1,0:T(8,128)} %all-gather.2.cloned.1.call-done.factor), custom_call_target="tpu_custom_call" | custom-call | tf_op jit(solution)/shard_map/update/pallas_call | solution.py:342
  (200 shorter events, 41.3 us)
Async XLA Ops:
  6.5 294.2 %all-gather.2.cloned.1.call-start = ((), (), s32[]{:S(2)}) async-start(), calls=%async_computation.1 | async-start | bytes 23003136 | tf_op jit(solution)/shard_map/all_gather | solution.py:302
  17.0 37.1 %all-to-all-start = ((f32[32,32,512]{2,1,0:T(8,128)}), f32[32,32,512]{2,1,0:T(8,128)S(1)}, u32[]{:S(2)}, u32[]{:S(2)}) async-start(f32[32,32,512]{2,1,0:T(8,128)} %pad_maximum_fusion), calls=%async_computation | async-start | bytes 4194304 | tf_op jit(solution)/shard_map/all_to_all | solution.py:311
  54.6 10.1 %collective-permute-start = (f32[6,8,512]{2,1,0:T(8,128)S(1)}, f32[6,8,512]{2,1,0:T(8,128)S(1)}, u32[]{:S(2)}, u32[]{:S(2)}) collective-permute-start(f32[6,8,512]{2,1,0:T(8,128)S(1)} %gather_fusion.4), channel_id=1, source_target_pairs={{0,7},{1,0},{2,1},{3,2},{4,3},{5,4},{6,5},{7,6},{8,15},{9,8},{10,9... | collective-permute-start | bytes 294920 | tf_op jit(solution)/shard_map/ppermute | solution.py:74
  60.2 8.0 %collective-permute-start.3 = (f32[6,8,512]{2,1,0:T(8,128)S(1)}, f32[6,8,512]{2,1,0:T(8,128)S(1)}, u32[]{:S(2)}, u32[]{:S(2)}) collective-permute-start(f32[6,8,512]{2,1,0:T(8,128)S(1)} %gather_fusion.4), channel_id=1, source_target_pairs={{0,1},{1,2},{2,3},{3,4},{4,5},{5,6},{6,7},{7,0},{8,9},{9,10},{10,1... | collective-permute-start | bytes 294920 | tf_op jit(solution)/shard_map/ppermute | solution.py:72
  64.7 7.8 %collective-permute-start.1 = (f32[6,8,512]{2,1,0:T(8,128)S(1)}, f32[6,8,512]{2,1,0:T(8,128)S(1)}, u32[]{:S(2)}, u32[]{:S(2)}) collective-permute-start(f32[6,8,512]{2,1,0:T(8,128)S(1)} %collective-permute-done), channel_id=1, source_target_pairs={{0,7},{1,0},{2,1},{3,2},{4,3},{5,4},{6,5},{7,6},{8,15},{9,8},{10,9... | collective-permute-start | bytes 294920 | tf_op jit(solution)/shard_map/ppermute | solution.py:74
  68.2 7.8 %collective-permute-start.4 = (f32[6,8,512]{2,1,0:T(8,128)S(1)}, f32[6,8,512]{2,1,0:T(8,128)S(1)}, u32[]{:S(2)}, u32[]{:S(2)}) collective-permute-start(f32[6,8,512]{2,1,0:T(8,128)S(1)} %collective-permute-done.3), channel_id=1, source_target_pairs={{0,1},{1,2},{2,3},{3,4},{4,5},{5,6},{6,7},{7,0},{8,9},{9,10},{10,1... | collective-permute-start | bytes 294920 | tf_op jit(solution)/shard_map/ppermute | solution.py:72
  72.5 11.0 %collective-permute-start.2 = (f32[6,8,512]{2,1,0:T(8,128)S(1)}, f32[6,8,512]{2,1,0:T(8,128)S(1)}, u32[]{:S(2)}, u32[]{:S(2)}) collective-permute-start(f32[6,8,512]{2,1,0:T(8,128)S(1)} %collective-permute-done.1), channel_id=1, source_target_pairs={{0,7},{1,0},{2,1},{3,2},{4,3},{5,4},{6,5},{7,6},{8,15},{9,8},{10,9... | collective-permute-start | bytes 294920 | tf_op jit(solution)/shard_map/ppermute | solution.py:74
  76.0 7.5 %collective-permute-start.5 = (f32[6,8,512]{2,1,0:T(8,128)S(1)}, f32[6,8,512]{2,1,0:T(8,128)S(1)}, u32[]{:S(2)}, u32[]{:S(2)}) collective-permute-start(f32[6,8,512]{2,1,0:T(8,128)S(1)} %collective-permute-done.4), channel_id=1, source_target_pairs={{0,1},{1,2},{2,3},{3,4},{4,5},{5,6},{6,7},{7,0},{8,9},{9,10},{10,1... | collective-permute-start | bytes 294920 | tf_op jit(solution)/shard_map/ppermute | solution.py:72
  83.4 7.3 %collective-permute-start.6 = (f32[6,8,512]{2,1,0:T(8,128)S(1)}, f32[6,8,512]{2,1,0:T(8,128)S(1)}, u32[]{:S(2)}, u32[]{:S(2)}) collective-permute-start(f32[6,8,512]{2,1,0:T(8,128)S(1)} %collective-permute-done.5), channel_id=1, source_target_pairs={{0,1},{1,2},{2,3},{3,4},{4,5},{5,6},{6,7},{7,0},{8,9},{9,10},{10,1... | collective-permute-start | bytes 294920 | tf_op jit(solution)/shard_map/ppermute | solution.py:72
  90.9 6.2 %collective-permute-start.13 = (f32[1,3,4,8,512]{4,3,2,1,0:T(8,128)S(1)}, f32[1,3,4,8,512]{4,3,2,1,0:T(8,128)S(1)}, u32[]{:S(2)}, u32[]{:S(2)}) collective-permute-start(f32[1,3,4,8,512]{4,3,2,1,0:T(8,128)S(1)} %get-tuple-element.42), channel_id=1, source_target_pairs={{0,16},{8,56},{16,0},{24,40},{32,48},{40,24},{48,32},{56,8},{64,80... | collective-permute-start | bytes 589832 | tf_op jit(solution)/shard_map/ppermute | solution.py:55
  91.9 6.1 %collective-permute-start.7 = (f32[1,3,4,8,512]{4,3,2,1,0:T(8,128)S(1)}, f32[1,3,4,8,512]{4,3,2,1,0:T(8,128)S(1)}, u32[]{:S(2)}, u32[]{:S(2)}) collective-permute-start(f32[1,3,4,8,512]{4,3,2,1,0:T(8,128)S(1)} %get-tuple-element.43), channel_id=1, source_target_pairs={{0,64},{8,200},{16,80},{24,216},{32,96},{40,232},{48,112},{56,248}... | collective-permute-start | bytes 589832 | tf_op jit(solution)/shard_map/ppermute | solution.py:55
  97.1 7.3 %collective-permute-start.14 = (f32[2,3,4,8,512]{4,3,2,1,0:T(8,128)S(1)}, f32[2,3,4,8,512]{4,3,2,1,0:T(8,128)S(1)}, u32[]{:S(2)}, u32[]{:S(2)}) collective-permute-start(f32[2,3,4,8,512]{4,3,2,1,0:T(8,128)S(1)} %pad_maximum_fusion.12), channel_id=1, source_target_pairs={{0,192},{8,72},{16,208},{24,88},{32,224},{40,104},{48,240},{56,120... | collective-permute-start | bytes 1179656 | tf_op jit(solution)/shard_map/ppermute | solution.py:55
  98.1 8.3 %collective-permute-start.8 = (f32[2,3,4,8,512]{4,3,2,1,0:T(8,128)S(1)}, f32[2,3,4,8,512]{4,3,2,1,0:T(8,128)S(1)}, u32[]{:S(2)}, u32[]{:S(2)}) collective-permute-start(f32[2,3,4,8,512]{4,3,2,1,0:T(8,128)S(1)} %pad_maximum_fusion.11), channel_id=1, source_target_pairs={{0,16},{8,56},{16,0},{24,40},{32,48},{40,24},{48,32},{56,8},{64,80... | collective-permute-start | bytes 1179656 | tf_op jit(solution)/shard_map/ppermute | solution.py:55
  104.5 14.4 %collective-permute-start.15 = (f32[4,3,4,8,512]{4,3,2,1,0:T(8,128)S(1)}, f32[4,3,4,8,512]{4,3,2,1,0:T(8,128)S(1)}, u32[]{:S(2)}, u32[]{:S(2)}) collective-permute-start(f32[4,3,4,8,512]{4,3,2,1,0:T(8,128)S(1)} %pad_maximum_fusion.6), channel_id=1, source_target_pairs={{0,48},{8,24},{16,32},{24,8},{32,16},{40,56},{48,0},{56,40},{64,11... | collective-permute-start | bytes 2359304 | tf_op jit(solution)/shard_map/ppermute | solution.py:55
  106.5 14.6 %collective-permute-start.9 = (f32[4,3,4,8,512]{4,3,2,1,0:T(8,128)S(1)}, f32[4,3,4,8,512]{4,3,2,1,0:T(8,128)S(1)}, u32[]{:S(2)}, u32[]{:S(2)}) collective-permute-start(f32[4,3,4,8,512]{4,3,2,1,0:T(8,128)S(1)} %pad_maximum_fusion.5), channel_id=1, source_target_pairs={{0,192},{8,72},{16,208},{24,88},{32,224},{40,104},{48,240},{56,120... | collective-permute-start | bytes 2359304 | tf_op jit(solution)/shard_map/ppermute | solution.py:55
  107.2 16.0 %collective-permute-start.34 = (f32[1,3,4,8,512]{4,3,2,1,0:T(8,128)S(1)}, f32[1,3,4,8,512]{4,3,2,1,0:T(8,128)S(1)}, u32[]{:S(2)}, u32[]{:S(2)}) collective-permute-start(f32[1,3,4,8,512]{4,3,2,1,0:T(8,128)S(1)} %bitcast.78), channel_id=1, source_target_pairs={{0,16},{8,56},{16,0},{24,40},{32,48},{40,24},{48,32},{56,8},{64,80... | collective-permute-start | bytes 589832 | tf_op jit(solution)/shard_map/ppermute | solution.py:55
  120.3 46.3 %collective-permute-start.16 = (f32[8,3,4,8,512]{4,3,2,1,0:T(8,128)}, f32[8,3,4,8,512]{4,3,2,1,0:T(8,128)}, u32[]{:S(2)}, u32[]{:S(2)}) collective-permute-start(f32[8,3,4,8,512]{4,3,2,1,0:T(8,128)} %pad_maximum_fusion.2.refs_4_), channel_id=1, source_target_pairs={{0,64},{8,200},{16,80},{24,216},{32,96},{40,232},{48,112},{56,248}... | collective-permute-start | bytes 4718600 | tf_op jit(solution)/shard_map/ppermute | solution.py:62
  122.4 44.2 %collective-permute-start.10 = (f32[8,3,4,8,512]{4,3,2,1,0:T(8,128)}, f32[8,3,4,8,512]{4,3,2,1,0:T(8,128)}, u32[]{:S(2)}, u32[]{:S(2)}) collective-permute-start(f32[8,3,4,8,512]{4,3,2,1,0:T(8,128)} %pad_maximum_fusion.1.refs_0_), channel_id=1, source_target_pairs={{0,48},{8,24},{16,32},{24,8},{32,16},{40,56},{48,0},{56,40},{64,11... | collective-permute-start | bytes 4718600 | tf_op jit(solution)/shard_map/ppermute | solution.py:62
  123.2 9.5 %collective-permute-start.35 = (f32[2,3,4,8,512]{4,3,2,1,0:T(8,128)S(1)}, f32[2,3,4,8,512]{4,3,2,1,0:T(8,128)S(1)}, u32[]{:S(2)}, u32[]{:S(2)}) collective-permute-start(f32[2,3,4,8,512]{4,3,2,1,0:T(8,128)S(1)} %pad_maximum_fusion.14), channel_id=1, source_target_pairs={{0,192},{8,72},{16,208},{24,88},{32,224},{40,104},{48,240},{56,120... | collective-permute-start | bytes 1179656 | tf_op jit(solution)/shard_map/ppermute | solution.py:55
  124.0 26.3 %collective-permute-start.31 = (f32[1,3,4,8,512]{4,3,2,1,0:T(8,128)S(1)}, f32[1,3,4,8,512]{4,3,2,1,0:T(8,128)S(1)}, u32[]{:S(2)}, u32[]{:S(2)}) collective-permute-start(f32[1,3,4,8,512]{4,3,2,1,0:T(8,128)S(1)} %bitcast.74), channel_id=1, source_target_pairs={{0,64},{8,200},{16,80},{24,216},{32,96},{40,232},{48,112},{56,248}... | collective-permute-start | bytes 589832 | tf_op jit(solution)/shard_map/ppermute | solution.py:55
  132.8 31.9 %collective-permute-start.36 = (f32[4,3,4,8,512]{4,3,2,1,0:T(8,128)S(1)}, f32[4,3,4,8,512]{4,3,2,1,0:T(8,128)S(1)}, u32[]{:S(2)}, u32[]{:S(2)}) collective-permute-start(f32[4,3,4,8,512]{4,3,2,1,0:T(8,128)S(1)} %pad_maximum_fusion.8), channel_id=1, source_target_pairs={{0,48},{8,24},{16,32},{24,8},{32,16},{40,56},{48,0},{56,40},{64,11... | collective-permute-start | bytes 2359304 | tf_op jit(solution)/shard_map/ppermute | solution.py:55
  135.4 43.3 %collective-permute-start.17 = (f32[8,3,4,8,512]{4,3,2,1,0:T(8,128)}, f32[8,3,4,8,512]{4,3,2,1,0:T(8,128)}, u32[]{:S(2)}, u32[]{:S(2)}) collective-permute-start(f32[8,3,4,8,512]{4,3,2,1,0:T(8,128)} %pad_maximum_fusion.2.refs_4_), channel_id=1, source_target_pairs={{0,8},{8,0},{1,9},{9,1},{2,10},{10,2},{3,11},{11,3},{4,12},{12,4},... | collective-permute-start | bytes 4718600 | tf_op jit(solution)/shard_map/ppermute | solution.py:44
  150.4 12.5 %collective-permute-start.32 = (f32[2,3,4,8,512]{4,3,2,1,0:T(8,128)S(1)}, f32[2,3,4,8,512]{4,3,2,1,0:T(8,128)S(1)}, u32[]{:S(2)}, u32[]{:S(2)}) collective-permute-start(f32[2,3,4,8,512]{4,3,2,1,0:T(8,128)S(1)} %pad_maximum_fusion.13), channel_id=1, source_target_pairs={{0,16},{8,56},{16,0},{24,40},{32,48},{40,24},{48,32},{56,8},{64,80... | collective-permute-start | bytes 1179656 | tf_op jit(solution)/shard_map/ppermute | solution.py:55
  164.7 11.5 %collective-permute-start.33 = (f32[4,3,4,8,512]{4,3,2,1,0:T(8,128)}, f32[4,3,4,8,512]{4,3,2,1,0:T(8,128)}, u32[]{:S(2)}, u32[]{:S(2)}) collective-permute-start(f32[4,3,4,8,512]{4,3,2,1,0:T(8,128)} %pad_maximum_fusion.7), channel_id=1, source_target_pairs={{0,192},{8,72},{16,208},{24,88},{32,224},{40,104},{48,240},{56,120... | collective-permute-start | bytes 2359304 | tf_op jit(solution)/shard_map/ppermute | solution.py:55
  165.6 16.0 %collective-permute-start.11 = (f32[8,3,4,8,512]{4,3,2,1,0:T(8,128)}, f32[8,3,4,8,512]{4,3,2,1,0:T(8,128)}, u32[]{:S(2)}, u32[]{:S(2)}) collective-permute-start(f32[8,3,4,8,512]{4,3,2,1,0:T(8,128)} %pad_maximum_fusion.1.refs_0_), channel_id=1, source_target_pairs={{0,8},{8,0},{1,9},{9,1},{2,10},{10,2},{3,11},{11,3},{4,12},{12,4},... | collective-permute-start | bytes 4718600 | tf_op jit(solution)/shard_map/ppermute | solution.py:44
  166.6 15.0 %collective-permute-start.18 = (f32[8,3,4,8,512]{4,3,2,1,0:T(8,128)}, f32[8,3,4,8,512]{4,3,2,1,0:T(8,128)}, u32[]{:S(2)}, u32[]{:S(2)}) collective-permute-start(f32[8,3,4,8,512]{4,3,2,1,0:T(8,128)} %collective-permute-done.16.refs_5_), channel_id=1, source_target_pairs={{0,8},{8,0},{1,9},{9,1},{2,10},{10,2},{3,11},{11,3},{4,12},{12,4},... | collective-permute-start | bytes 4718600 | tf_op jit(solution)/shard_map/ppermute | solution.py:44
  166.6 15.0 %collective-permute-start.12 = (f32[8,3,4,8,512]{4,3,2,1,0:T(8,128)}, f32[8,3,4,8,512]{4,3,2,1,0:T(8,128)}, u32[]{:S(2)}, u32[]{:S(2)}) collective-permute-start(f32[8,3,4,8,512]{4,3,2,1,0:T(8,128)} %collective-permute-done.10.refs_1_), channel_id=1, source_target_pairs={{0,8},{8,0},{1,9},{9,1},{2,10},{10,2},{3,11},{11,3},{4,12},{12,4},... | collective-permute-start | bytes 4718600 | tf_op jit(solution)/shard_map/ppermute | solution.py:44
  178.6 39.0 %collective-permute-start.40 = (f32[8,3,4,8,512]{4,3,2,1,0:T(8,128)}, f32[8,3,4,8,512]{4,3,2,1,0:T(8,128)}, u32[]{:S(2)}, u32[]{:S(2)}) collective-permute-start(f32[8,3,4,8,512]{4,3,2,1,0:T(8,128)} %pad_maximum_fusion.4.refs_4_), channel_id=1, source_target_pairs={{0,64},{8,200},{16,80},{24,216},{32,96},{40,232},{48,112},{56,248}... | collective-permute-start | bytes 4718600 | tf_op jit(solution)/shard_map/ppermute | solution.py:62
  178.7 39.4 %collective-permute-start.37 = (f32[8,3,4,8,512]{4,3,2,1,0:T(8,128)}, f32[8,3,4,8,512]{4,3,2,1,0:T(8,128)}, u32[]{:S(2)}, u32[]{:S(2)}) collective-permute-start(f32[8,3,4,8,512]{4,3,2,1,0:T(8,128)} %pad_maximum_fusion.3.refs_0_), channel_id=1, source_target_pairs={{0,48},{8,24},{16,32},{24,8},{32,16},{40,56},{48,0},{56,40},{64,11... | collective-permute-start | bytes 4718600 | tf_op jit(solution)/shard_map/ppermute | solution.py:62
  199.0 12.8 %collective-permute-start.25 = (f32[1,16,1024]{2,1,0:T(8,128)}, f32[1,16,1024]{2,1,0:T(8,128)S(1)}, u32[]{:S(2)}, u32[]{:S(2)}) collective-permute-start(f32[1,16,1024]{2,1,0:T(8,128)} %bitcast.88), channel_id=1, source_target_pairs={{0,16},{8,56},{16,0},{24,40},{32,48},{40,24},{48,32},{56,8},{64,80... | collective-permute-start | bytes 196616 | tf_op jit(solution)/shard_map/ppermute | solution.py:55
  202.2 14.4 %collective-permute-start.20 = (f32[2,16,1024]{2,1,0:T(8,128)S(1)}, f32[2,16,1024]{2,1,0:T(8,128)S(1)}, u32[]{:S(2)}, u32[]{:S(2)}) collective-permute-start(f32[2,16,1024]{2,1,0:T(8,128)S(1)} %pad_maximum_fusion.19), channel_id=1, source_target_pairs={{0,16},{8,56},{16,0},{24,40},{32,48},{40,24},{48,32},{56,8},{64,80... | collective-permute-start | bytes 393224 | tf_op jit(solution)/shard_map/ppermute | solution.py:55
  217.4 5.7 %collective-permute-start.21 = (f32[4,16,1024]{2,1,0:T(8,128)S(1)}, f32[4,16,1024]{2,1,0:T(8,128)S(1)}, u32[]{:S(2)}, u32[]{:S(2)}) collective-permute-start(f32[4,16,1024]{2,1,0:T(8,128)S(1)} %pad_maximum_fusion.15), channel_id=1, source_target_pairs={{0,192},{8,72},{16,208},{24,88},{32,224},{40,104},{48,240},{56,120... | collective-permute-start | bytes 786440 | tf_op jit(solution)/shard_map/ppermute | solution.py:55
  217.5 25.5 %collective-permute-start.41 = (f32[8,3,4,8,512]{4,3,2,1,0:T(8,128)}, f32[8,3,4,8,512]{4,3,2,1,0:T(8,128)S(1)}, u32[]{:S(2)}, u32[]{:S(2)}) collective-permute-start(f32[8,3,4,8,512]{4,3,2,1,0:T(8,128)} %pad_maximum_fusion.4.refs_4_), channel_id=1, source_target_pairs={{0,8},{8,0},{1,9},{9,1},{2,10},{10,2},{3,11},{11,3},{4,12},{12,4},... | collective-permute-start | bytes 4718600 | tf_op jit(solution)/shard_map/ppermute | solution.py:44
  217.6 25.4 %collective-permute-start.38 = (f32[8,3,4,8,512]{4,3,2,1,0:T(8,128)}, f32[8,3,4,8,512]{4,3,2,1,0:T(8,128)S(1)}, u32[]{:S(2)}, u32[]{:S(2)}) collective-permute-start(f32[8,3,4,8,512]{4,3,2,1,0:T(8,128)} %pad_maximum_fusion.3.refs_0_), channel_id=1, source_target_pairs={{0,8},{8,0},{1,9},{9,1},{2,10},{10,2},{3,11},{11,3},{4,12},{12,4},... | collective-permute-start | bytes 4718600 | tf_op jit(solution)/shard_map/ppermute | solution.py:44
  218.1 24.9 %collective-permute-start.39 = (f32[8,3,4,8,512]{4,3,2,1,0:T(8,128)}, f32[8,3,4,8,512]{4,3,2,1,0:T(8,128)}, u32[]{:S(2)}, u32[]{:S(2)}) collective-permute-start(f32[8,3,4,8,512]{4,3,2,1,0:T(8,128)} %collective-permute-done.37.refs_1_), channel_id=1, source_target_pairs={{0,8},{8,0},{1,9},{9,1},{2,10},{10,2},{3,11},{11,3},{4,12},{12,4},... | collective-permute-start | bytes 4718600 | tf_op jit(solution)/shard_map/ppermute | solution.py:44
  218.2 24.8 %collective-permute-start.42 = (f32[8,3,4,8,512]{4,3,2,1,0:T(8,128)}, f32[8,3,4,8,512]{4,3,2,1,0:T(8,128)}, u32[]{:S(2)}, u32[]{:S(2)}) collective-permute-start(f32[8,3,4,8,512]{4,3,2,1,0:T(8,128)} %collective-permute-done.40.refs_5_), channel_id=1, source_target_pairs={{0,8},{8,0},{1,9},{9,1},{2,10},{10,2},{3,11},{11,3},{4,12},{12,4},... | collective-permute-start | bytes 4718600 | tf_op jit(solution)/shard_map/ppermute | solution.py:44
  228.7 8.3 %collective-permute-start.22 = (f32[8,16,1024]{2,1,0:T(8,128)S(1)}, f32[8,16,1024]{2,1,0:T(8,128)S(1)}, u32[]{:S(2)}, u32[]{:S(2)}) collective-permute-start(f32[8,16,1024]{2,1,0:T(8,128)S(1)} %pad_maximum_fusion.9.refs_0_), channel_id=1, source_target_pairs={{0,48},{8,24},{16,32},{24,8},{32,16},{40,56},{48,0},{56,40},{64,11... | collective-permute-start | bytes 1572872 | tf_op jit(solution)/shard_map/ppermute | solution.py:62
  241.3 28.5 %collective-permute-start.28 = (f32[8,16,1024]{2,1,0:T(8,128)S(1)}, f32[8,16,1024]{2,1,0:T(8,128)S(1)}, u32[]{:S(2)}, u32[]{:S(2)}) collective-permute-start(f32[8,16,1024]{2,1,0:T(8,128)S(1)} %pad_maximum_fusion.10.refs_4_), channel_id=1, source_target_pairs={{0,64},{8,200},{16,80},{24,216},{32,96},{40,232},{48,112},{56,248}... | collective-permute-start | bytes 1572872 | tf_op jit(solution)/shard_map/ppermute | solution.py:62
  265.6 7.3 %collective-permute-start.51 = (f32[4,16,512]{2,1,0:T(8,128)S(1)}, f32[4,16,512]{2,1,0:T(8,128)S(1)}, u32[]{:S(2)}, u32[]{:S(2)}) collective-permute-start(f32[4,16,512]{2,1,0:T(8,128)S(1)} %pad_maximum_fusion.22), channel_id=1, source_target_pairs={{0,48},{8,24},{16,32},{24,8},{32,16},{40,56},{48,0},{56,40},{64,11... | collective-permute-start | bytes 393224 | tf_op jit(solution)/shard_map/ppermute | solution.py:55
  265.7 9.4 %collective-permute-start.29 = (f32[8,16,1024]{2,1,0:T(8,128)S(1)}, f32[8,16,1024]{2,1,0:T(8,128)S(1)}, u32[]{:S(2)}, u32[]{:S(2)}) collective-permute-start(f32[8,16,1024]{2,1,0:T(8,128)S(1)} %pad_maximum_fusion.10.refs_4_), channel_id=1, source_target_pairs={{0,8},{8,0},{1,9},{9,1},{2,10},{10,2},{3,11},{11,3},{4,12},{12,4},... | collective-permute-start | bytes 1572872 | tf_op jit(solution)/shard_map/ppermute | solution.py:44
  268.8 10.4 %collective-permute-start.23 = (f32[8,16,1024]{2,1,0:T(8,128)S(1)}, f32[8,16,1024]{2,1,0:T(8,128)S(1)}, u32[]{:S(2)}, u32[]{:S(2)}) collective-permute-start(f32[8,16,1024]{2,1,0:T(8,128)S(1)} %pad_maximum_fusion.9.refs_0_), channel_id=1, source_target_pairs={{0,8},{8,0},{1,9},{9,1},{2,10},{10,2},{3,11},{11,3},{4,12},{12,4},... | collective-permute-start | bytes 1572872 | tf_op jit(solution)/shard_map/ppermute | solution.py:44
  269.8 18.0 %collective-permute-start.30 = (f32[8,16,1024]{2,1,0:T(8,128)S(1)}, f32[8,16,1024]{2,1,0:T(8,128)S(1)}, u32[]{:S(2)}, u32[]{:S(2)}) collective-permute-start(f32[8,16,1024]{2,1,0:T(8,128)S(1)} %collective-permute-done.28.refs_5_), channel_id=1, source_target_pairs={{0,8},{8,0},{1,9},{9,1},{2,10},{10,2},{3,11},{11,3},{4,12},{12,4},... | collective-permute-start | bytes 1572872 | tf_op jit(solution)/shard_map/ppermute | solution.py:44
  273.7 6.5 %collective-permute-start.52 = (f32[8,16,512]{2,1,0:T(8,128)S(1)}, f32[8,16,512]{2,1,0:T(8,128)S(1)}, u32[]{:S(2)}, u32[]{:S(2)}) collective-permute-start(f32[8,16,512]{2,1,0:T(8,128)S(1)} %pad_maximum_fusion.18.refs_4_), channel_id=1, source_target_pairs={{0,64},{8,200},{16,80},{24,216},{32,96},{40,232},{48,112},{56,248}... | collective-permute-start | bytes 786440 | tf_op jit(solution)/shard_map/ppermute | solution.py:62
  275.0 5.9 %collective-permute-start.46 = (f32[8,16,512]{2,1,0:T(8,128)S(1)}, f32[8,16,512]{2,1,0:T(8,128)S(1)}, u32[]{:S(2)}, u32[]{:S(2)}) collective-permute-start(f32[8,16,512]{2,1,0:T(8,128)S(1)} %pad_maximum_fusion.17.refs_0_), channel_id=1, source_target_pairs={{0,48},{8,24},{16,32},{24,8},{32,16},{40,56},{48,0},{56,40},{64,11... | collective-permute-start | bytes 786440 | tf_op jit(solution)/shard_map/ppermute | solution.py:62
  275.1 20.2 %collective-permute-start.53 = (f32[8,16,512]{2,1,0:T(8,128)S(1)}, f32[8,16,512]{2,1,0:T(8,128)S(1)}, u32[]{:S(2)}, u32[]{:S(2)}) collective-permute-start(f32[8,16,512]{2,1,0:T(8,128)S(1)} %pad_maximum_fusion.18.refs_4_), channel_id=1, source_target_pairs={{0,8},{8,0},{1,9},{9,1},{2,10},{10,2},{3,11},{11,3},{4,12},{12,4},... | collective-permute-start | bytes 786440 | tf_op jit(solution)/shard_map/ppermute | solution.py:44
  279.1 16.2 %collective-permute-start.47 = (f32[8,16,512]{2,1,0:T(8,128)S(1)}, f32[8,16,512]{2,1,0:T(8,128)}, u32[]{:S(2)}, u32[]{:S(2)}) collective-permute-start(f32[8,16,512]{2,1,0:T(8,128)S(1)} %pad_maximum_fusion.17.refs_0_), channel_id=1, source_target_pairs={{0,8},{8,0},{1,9},{9,1},{2,10},{10,2},{3,11},{11,3},{4,12},{12,4},... | collective-permute-start | bytes 786440 | tf_op jit(solution)/shard_map/ppermute | solution.py:44
  280.3 15.1 %collective-permute-start.54 = (f32[8,16,512]{2,1,0:T(8,128)S(1)}, f32[8,16,512]{2,1,0:T(8,128)}, u32[]{:S(2)}, u32[]{:S(2)}) collective-permute-start(f32[8,16,512]{2,1,0:T(8,128)S(1)} %collective-permute-done.52.refs_5_), channel_id=1, source_target_pairs={{0,8},{8,0},{1,9},{9,1},{2,10},{10,2},{3,11},{11,3},{4,12},{12,4},... | collective-permute-start | bytes 786440 | tf_op jit(solution)/shard_map/ppermute | solution.py:44
  280.9 14.5 %collective-permute-start.48 = (f32[8,16,512]{2,1,0:T(8,128)S(1)}, f32[8,16,512]{2,1,0:T(8,128)}, u32[]{:S(2)}, u32[]{:S(2)}) collective-permute-start(f32[8,16,512]{2,1,0:T(8,128)S(1)} %collective-permute-done.46.refs_1_), channel_id=1, source_target_pairs={{0,8},{8,0},{1,9},{9,1},{2,10},{10,2},{3,11},{11,3},{4,12},{12,4},... | collective-permute-start | bytes 786440 | tf_op jit(solution)/shard_map/ppermute | solution.py:44
  (38 other events, 460.2 us)
Sparse Core Ops, SparseCore 0:
  9.1 219.1 all-gather.1

commit v3 on v1

--- a/solution.py
+++ b/solution.py
@@ -17,8 +17,7 @@
 COL = ("col_0", "col_1", "col_2")
 HOPS = ((0, 1), (1, 1), (0, 3), (1, 3))
 BLOCKS = [(k, m) for k in range(P_SIZE) for m in range(k + 1)]
-SLOTS = 6
-HALF = SLOTS // 2
+EARLY = 10
 MINE = 16
 NARROW = 256
 
@@ -43,16 +42,16 @@
 
 
 def spread(streams):
-    near = [value[None] for value in streams]
-    for stage in range(3):
-        near = [
-            jnp.concatenate([value, lax.ppermute(value, COL, exchange(i, stage))], 0)
-            for i, value in enumerate(near)
-        ]
-    far = [lax.ppermute(value, COL, exchange(i, 3)) for i, value in enumerate(near)]
-    return [
-        [near[i], far[i], other_core(near[i]), other_core(far[i])] for i in range(len(streams))
-    ]
+    every = []
+    for i, value in enumerate(streams):
+        value = value[None]
+        for stage in range(2):
+            value = jnp.concatenate([value, lax.ppermute(value, COL, exchange(i, stage))], 0)
+        every.append([value])
+    for stage in (2, 3):
+        for i, parts in enumerate(every):
+            parts += [lax.ppermute(part, COL, exchange(i, stage)) for part in parts]
+    return [parts + [other_core(part) for part in parts] for parts in every]
 
 
 def all_rows(value):
@@ -108,12 +107,12 @@
     copies = []
     for stream in range(2):
         group = []
-        for part in range(4):
-            for unit in range(8):
-                number = (stream * 2 + part // 2) * 16 + part % 2 * 8 + unit
+        for part in range(8):
+            for unit in range(4):
+                number = stream * 32 + part * 4 + unit
                 group.append(
                     pltpu.make_async_copy(
-                        refs[stream * 4 + part].at[unit],
+                        refs[stream * 8 + part].at[unit],
                         place(stream, number),
                         semaphores.at[number],
                     )
@@ -123,12 +122,14 @@
 
 
 def solve_kernel(source, flags, *refs):
-    parts, (windows, inverse), outs = refs[:8], refs[8:10], refs[10:12]
-    blocks, errors, semaphores = refs[12:]
+    parts, (windows, inverse), outs = refs[:16], refs[16:18], refs[18:20]
+    blocks, errors, semaphores = refs[20:]
 
     def place(stream, number):
-        place_of = source[number]
-        return blocks.at[pl.ds(stream * HALF, HALF), place_of // 8, :, lax.rem(place_of, 8)]
+        there = source[number]
+        first, count = (0, EARLY) if stream == 0 else (EARLY, len(BLOCKS) - EARLY)
+        column = pl.multiple_of(there // 8 * TILE, TILE)
+        return blocks.at[pl.ds(first, count), :, lax.rem(there, 8), :, pl.ds(column, TILE)]
 
     copies = unit_copies(parts, place, semaphores)
     for group in copies:
@@ -136,17 +137,15 @@
             copy.start()
     for copy in copies[0]:
         copy.wait()
-    arrived = 1
 
     def block_at(number):
-        return halves(blocks[number // 4, lax.rem(number, 4)].reshape(PW, PW))
+        return halves(blocks[number].reshape(PW, PW))
 
     for k in range(P_SIZE):
         base = k * (k + 1) // 2
-        if base + k >= 4 * HALF and arrived == 1:
+        if base == EARLY:
             for copy in copies[1]:
                 copy.wait()
-            arrived = 2
 
         def take(m, acc, base=base):
             return acc - product((errors[m, 0], errors[m, 1]), block_at(base + m))
@@ -169,35 +168,40 @@
             errors[k, i] = jnp.concatenate([d[i] for d in done], 1)
 
 
-def assemble_kernel(source, *refs):
-    parts, (out, errors, semaphores) = refs[:8], refs[8:]
+def update_kernel(source, flags, *refs):
+    parts, (weights, factor, out), (errors, split, semaphores) = refs[:16], refs[16:19], refs[19:]
+    n = pl.program_id(0)
 
     def place(stream, number):
         first = pl.multiple_of(source[number] * MINE, MINE)
         return errors.at[stream, pl.ds(first, MINE)]
 
-    copies = unit_copies(parts, place, semaphores)
-    for group in copies:
-        for copy in group:
-            copy.start()
-    for stream, group in enumerate(copies):
-        for copy in group:
-            copy.wait()
-        for k in range(3 * stream, 3 * stream + 3):
-            high, low = halves(errors[stream, :, (k % 3) * PW : (k % 3 + 1) * PW])
-            out[k, :, :PW] = high
-            out[k, :, PW : 2 * PW] = low
-            out[k, :, 2 * PW :] = high
-
-
-def update_kernel(flags, errors, weights, factor, out):
-    n = pl.program_id(0)
+    @pl.when(n == 0)
+    def _():
+        copies = unit_copies(parts, place, semaphores)
+        for group in copies:
+            for copy in group:
+                copy.start()
+        for group in copies:
+            for copy in group:
+                copy.wait()
+
+        def divide(k, carry):
+            column = pl.multiple_of(lax.rem(k, 3) * PW, PW)
+            high, low = halves(errors[k // 3, :, pl.ds(column, PW)])
+            split[k, :, :PW] = high
+            split[k, :, PW : 2 * PW] = low
+            split[k, :, 2 * PW :] = high
+            return carry
+
+        lax.fori_loop(0, P_SIZE, divide, 0)
+
     out[...] = weights[...]
 
     def take(k, carry):
         high, low = halves(factor[k])
         rows = jnp.concatenate([high, high, low], 0)
-        out[...] = out[...] - jnp.dot(errors[k], rows, preferred_element_type=jnp.float32)
+        out[...] = out[...] - jnp.dot(split[k], rows, preferred_element_type=jnp.float32)
         return carry
 
     lax.fori_loop(0, P_SIZE, take, 0)
@@ -225,24 +229,23 @@
     gathered = lax.all_gather(factor, "row", axis=1, tiled=True)
 
     window = lax.dynamic_slice(factor, (0, 0, shift), (P_SIZE, slab, PW))
-    window = window.reshape(P_SIZE, 8, 8, PW)
-    turn = lax.rem(panel * (panel + 1) // 2, 4)
-    order = lax.rem(jnp.arange(4, dtype=jnp.int32) + 4 - turn, 4)
-    order = jnp.minimum(order[:, None] + jnp.array([0, 4], jnp.int32), P_SIZE - 1)
-    eighths = jnp.swapaxes(window[order], 1, 2).reshape(N_COL, 16, PW)
-    wanted = lax.dynamic_slice(weights, (0, shift), (rows, PW)).reshape(N_COL, MINE, PW)
-    arrived = lax.all_to_all(
-        jnp.concatenate([eighths, wanted], 1), COL, 0, 0, tiled=True
-    ).reshape(4 * N_COL, 8, PW)
-
-    numbers = jnp.minimum(4 * jnp.arange(SLOTS, dtype=jnp.int32) + me // 8, len(BLOCKS) - 1)
-    panels = jnp.array([k for k, _ in BLOCKS], jnp.int32)[numbers]
-    parts = jnp.array([m // 4 for _, m in BLOCKS], jnp.int32)[numbers]
-    picked = all_rows(arrived[owner[panels] * 4 + parts])
-    windows = arrived[(owner[:, None] * 4 + jnp.array([2, 3], jnp.int32)).reshape(-1)]
+    pieces = window.reshape(P_SIZE, 8, 8, 4, TILE).transpose(3, 1, 0, 2, 4)
+    pieces = pieces.reshape(N_COL, P_SIZE, 8, TILE)
+    wanted = lax.dynamic_slice(weights, (0, shift), (rows, PW))
+    wanted = wanted.reshape(N_COL, 2, 8, 4, TILE).transpose(0, 1, 3, 2, 4)
+    wanted = wanted.reshape(N_COL, 8, 8, TILE)
+    arrived = lax.all_to_all(jnp.concatenate([pieces, wanted], 1), COL, 0, 0, tiled=True)
+
+    each = arrived.shape[1]
+    arrived = arrived.reshape(N_COL * each, 8, TILE)
+    panels = np.array([k for k, _ in BLOCKS])
+    rows_of = jnp.array([m for _, m in BLOCKS], jnp.int32)
+    picked = all_rows(arrived[owner[panels] * each + rows_of])
+    windows = arrived[(owner[:, None] * each + jnp.arange(P_SIZE, each)).reshape(-1)]
+    windows = windows.reshape(P_SIZE, 2, 4, 8, TILE).transpose(0, 1, 3, 2, 4)
     windows = windows.reshape(P_SIZE, MINE, PW)
     source = sources()
-    spread_parts = spread([picked[:HALF], picked[HALF:]])
+    spread_parts = spread([picked[:EARLY], picked[EARLY:]])
 
     own_rows = lax.dynamic_slice(prune_mask, (0, me // 8, 0), (P_SIZE, 1, PANEL_TILES))[:, 0]
     any_spec = pl.BlockSpec(memory_space=pl.ANY)
@@ -251,50 +254,43 @@
     found = pl.pallas_call(
         solve_kernel,
         out_shape=[jax.ShapeDtypeStruct((MINE, 3 * PW), jnp.float32)] * 2,
-        in_specs=[smem, smem] + [any_spec] * 8 + [vmem, vmem],
+        in_specs=[smem, smem] + [any_spec] * 16 + [vmem, vmem],
         out_specs=[vmem, vmem],
         scratch_shapes=[
-            pltpu.VMEM((SLOTS, 4, 8, 8, 8, PW), jnp.float32),
+            pltpu.VMEM((len(BLOCKS), 8, 8, 8, PW), jnp.float32),
             pltpu.VMEM((P_SIZE, 2, MINE, PW), jnp.bfloat16),
             pltpu.SemaphoreType.DMA((64,)),
         ],
-        compiler_params=pltpu.CompilerParams(vmem_limit_bytes=48 << 20),
+        compiler_params=pltpu.CompilerParams(vmem_limit_bytes=58 << 20),
         name="solve",
     )(source, own_rows, *spread_parts[0], *spread_parts[1], windows, diag_inverse)
 
     spread_errors = spread(found)
     pruned = jnp.sum(jnp.where(mine[:, None, None], prune_mask, 0), 0).reshape(-1)
     flags = jnp.concatenate([(shift // TILE)[None], pruned]).astype(jnp.int32)
-    split = pl.pallas_call(
-        assemble_kernel,
-        out_shape=jax.ShapeDtypeStruct((P_SIZE, rows, 3 * PW), jnp.bfloat16),
-        in_specs=[smem] + [any_spec] * 8,
-        out_specs=vmem,
-        scratch_shapes=[
-            pltpu.VMEM((2, rows, 3 * PW), jnp.float32),
-            pltpu.SemaphoreType.DMA((64,)),
-        ],
-        compiler_params=pltpu.CompilerParams(vmem_limit_bytes=24 << 20),
-        name="assemble",
-    )(source, *spread_errors[0], *spread_errors[1])
     steps = pl.cdiv(width, NARROW)
     column = lambda i, *_: (0, i)
     return pl.pallas_call(
         update_kernel,
         out_shape=jax.ShapeDtypeStruct(weights.shape, jnp.float32),
         grid_spec=pltpu.PrefetchScalarGridSpec(
-            num_scalar_prefetch=1,
+            num_scalar_prefetch=2,
             grid=(steps,),
-            in_specs=[
-                vmem,
+            in_specs=[any_spec] * 16
+            + [
                 pl.BlockSpec((rows, NARROW), column),
                 pl.BlockSpec((P_SIZE, PW, NARROW), lambda i, *_: (0, 0, i)),
             ],
             out_specs=pl.BlockSpec((rows, NARROW), column),
+            scratch_shapes=[
+                pltpu.VMEM((2, rows, 3 * PW), jnp.float32),
+                pltpu.VMEM((P_SIZE, rows, 3 * PW), jnp.bfloat16),
+                pltpu.SemaphoreType.DMA((64,)),
+            ],
         ),
-        compiler_params=pltpu.CompilerParams(vmem_limit_bytes=40 << 20),
+        compiler_params=pltpu.CompilerParams(vmem_limit_bytes=58 << 20),
         name="update",
-    )(flags, split, weights, gathered)
+    )(source, flags, *spread_errors[0], *spread_errors[1], weights, gathered)
 
 
 def solution(mesh):

time: 300 us -> 270 us (0.900)
  waiting for transfers between devices: 138 us -> 100 us
  starting transfers between devices: 64.7 us -> 81.6 us
  local copies, waits for them, and re-layouts: 18 us -> 11.9 us
    ppermute x12 -> x8, waiting for transfers between devices: 50.6 us -> 22.4 us  [spread(): lax.ppermute(value, COL, exchange(i, stage))]
    ppermute x8 -> x16, starting transfers between devices: 29.1 us -> 41.5 us  [other_core(): return lax.ppermute(value, 'col_2', [(0, 1), (1, 0)])]
    ppermute x4 -> x12, starting transfers between devices: 3.81 us -> 13.1 us  [spread(): parts += [lax.ppermute(part, COL, exchange(i, stage)) for part in parts]]
    unnamed x26 -> x52, local copies, waits for them, and re-layouts: 8.78 us -> 2.94 us
    pallas_call x1, Pallas kernels: 28.7 us -> 33.5 us  [shards(): pl.pallas_call(update_kernel, out_shape=jax.ShapeDtypeStruct(weights.shap...]
    pallas_call x1 -> x0, Pallas kernels: 4.76 us -> none  [shards(): pl.pallas_call(assemble_kernel, out_shape=jax.ShapeDtypeStruct((P_SIZE, r...]
    ppermute x12 -> x8, starting transfers between devices: 10.3 us -> 5.58 us  [spread(): lax.ppermute(value, COL, exchange(i, stage))]
    ppermute x4 -> x12, waiting for transfers between devices: 34 us -> 29.6 us  [spread(): parts += [lax.ppermute(part, COL, exchange(i, stage)) for part in parts]]
  transfers between devices with their start and end apart: 33 -> 45, of which waited for: 17 -> 17; matrix products, arithmetic and copies ran while one was open for 6% -> 6% of each run, Pallas kernels for 7% -> 7%
where the time goes in v3:
time: 270 us; the launch traced here: 269 us
  waiting for transfers between devices  100 us (37%)
  starting transfers between devices  81.6 us (30%)
  Pallas kernels  52 us (19%)
  between operations  17.5 us (6%)
  local copies, waits for them, and re-layouts  11.9 us (4%)
  other arithmetic  5.98 us (2%)
    ppermute x16, starting transfers between devices, other_core(): return lax.ppermute(value, 'col_2', [(0, 1), (1, 0)])  41.5 us
    pallas_call x1, Pallas kernels, shards(): pl.pallas_call(update_kernel, out_shape=jax.ShapeDtypeStruct(weights.shap...  33.5 us
    ppermute x12, waiting for transfers between devices, spread(): parts += [lax.ppermute(part, COL, exchange(i, stage)) for part in parts]  29.6 us
    all_to_all x1, waiting for transfers between devices, shards(): lax.all_to_all(jnp.concatenate([pieces, wanted], 1), COL, 0, 0, tiled=True)  24.7 us
    ppermute x8, waiting for transfers between devices, spread(): lax.ppermute(value, COL, exchange(i, stage))  22.4 us
    pallas_call x1, Pallas kernels, shards(): pl.pallas_call(solve_kernel, out_shape=[jax.ShapeDtypeStruct((MINE, 3 * P...  18.5 us
    ppermute x4, waiting for transfers between devices, all_rows(): below.append(lax.ppermute(below[-1], 'row', up))  13.8 us
    ppermute x12, starting transfers between devices, spread(): parts += [lax.ppermute(part, COL, exchange(i, stage)) for part in parts]  13.1 us
  transfers between devices with their start and end apart: 45, of which 17 were waited for; matrix products, arithmetic and copies ran while one was open for 6% of the time, Pallas kernels for 7%

profile of v3, /device:TPU:1, one launch (start us, length us, event | category | flops | bytes accessed | tf_op | source)
XLA Modules:
  0.0 269.4 jit_solution(941884274995864930)
XLA Ops:
  6.5 0.7 all-gather.2.cloned.1.call-update
  9.7 1.5 dynamic-slice_bitcast_fusion
  11.2 1.7 constant_dynamic-slice_fusion
  12.9 1.4 pad_maximum_fusion
  14.2 8.7 %all-to-all-start = ((f32[32,14,8,128]{3,2,1,0:T(8,128)}), f32[32,14,8,128]{3,2,1,0:T(8,128)S(1)}, u32[]{:S(2)}, u32[]{:S(2)}) async-start(f32[32,14,8,128]{3,2,1,0:T(8,128)} %pad_maximum_fusion), calls=%async_computation | async-start | bytes 3670016 | tf_op jit(solution)/shard_map/all_to_all | solution.py:237
  23.8 24.7 %all-to-all-done = f32[32,14,8,128]{3,2,1,0:T(8,128)S(1)} async-done(((f32[32,14,8,128]{3,2,1,0:T(8,128)}), f32[32,14,8,128]{3,2,1,0:T(8,128)S(1)}, u32[]{:S(2)}, u32[]{:S(2)}) %all-to-all-start) | async-done | bytes 1835040 | tf_op jit(solution)/shard_map/all_to_all | solution.py:237
  49.1 5.7 %collective-permute-start = (f32[21,8,128]{2,1,0:T(8,128)S(1)}, f32[21,8,128]{2,1,0:T(8,128)S(1)}, u32[]{:S(2)}, u32[]{:S(2)}) collective-permute-start(f32[21,8,128]{2,1,0:T(8,128)S(1)} %gather_fusion.1), channel_id=1, source_target_pairs={{0,7},{1,0},{2,1},{3,2},{4,3},{5,4},{6,5},{7,6},{8,15},{9,8},{10,9... | collective-permute-start | bytes 258056 | tf_op jit(solution)/shard_map/ppermute | solution.py:65
  54.8 3.9 %collective-permute-done = f32[21,8,128]{2,1,0:T(8,128)S(1)} collective-permute-done((f32[21,8,128]{2,1,0:T(8,128)S(1)}, f32[21,8,128]{2,1,0:T(8,128)S(1)}, u32[]{:S(2)}, u32[]{:S(2)}) %collective-permute-start) | collective-permute-done | bytes 86048 | tf_op jit(solution)/shard_map/ppermute | solution.py:65
  58.7 3.5 %collective-permute-start.1 = (f32[21,8,128]{2,1,0:T(8,128)S(1)}, f32[21,8,128]{2,1,0:T(8,128)S(1)}, u32[]{:S(2)}, u32[]{:S(2)}) collective-permute-start(f32[21,8,128]{2,1,0:T(8,128)S(1)} %collective-permute-done), channel_id=1, source_target_pairs={{0,7},{1,0},{2,1},{3,2},{4,3},{5,4},{6,5},{7,6},{8,15},{9,8},{10,9... | collective-permute-start | bytes 258056 | tf_op jit(solution)/shard_map/ppermute | solution.py:65
  62.2 3.7 %collective-permute-done.1 = f32[21,8,128]{2,1,0:T(8,128)S(1)} collective-permute-done((f32[21,8,128]{2,1,0:T(8,128)S(1)}, f32[21,8,128]{2,1,0:T(8,128)S(1)}, u32[]{:S(2)}, u32[]{:S(2)}) %collective-permute-start.1) | collective-permute-done | bytes 86048 | tf_op jit(solution)/shard_map/ppermute | solution.py:65
  65.9 3.5 %collective-permute-start.2 = (f32[21,8,128]{2,1,0:T(8,128)S(1)}, f32[21,8,128]{2,1,0:T(8,128)S(1)}, u32[]{:S(2)}, u32[]{:S(2)}) collective-permute-start(f32[21,8,128]{2,1,0:T(8,128)S(1)} %collective-permute-done.1), channel_id=1, source_target_pairs={{0,7},{1,0},{2,1},{3,2},{4,3},{5,4},{6,5},{7,6},{8,15},{9,8},{10,9... | collective-permute-start | bytes 258056 | tf_op jit(solution)/shard_map/ppermute | solution.py:65
  69.5 7.0 %collective-permute-done.5 = f32[21,8,128]{2,1,0:T(8,128)S(1)} collective-permute-done((f32[21,8,128]{2,1,0:T(8,128)S(1)}, f32[21,8,128]{2,1,0:T(8,128)S(1)}, u32[]{:S(2)}, u32[]{:S(2)}) %collective-permute-start.5) | collective-permute-done | bytes 86048 | tf_op jit(solution)/shard_map/ppermute | solution.py:63
  76.5 6.9 %collective-permute-done.6 = f32[21,8,128]{2,1,0:T(8,128)S(1)} collective-permute-done((f32[21,8,128]{2,1,0:T(8,128)S(1)}, f32[21,8,128]{2,1,0:T(8,128)S(1)}, u32[]{:S(2)}, u32[]{:S(2)}) %collective-permute-start.6) | collective-permute-done | bytes 86048 | tf_op jit(solution)/shard_map/ppermute | solution.py:63
  83.5 1.1 collective-permute-start.16
  85.2 6.2 %collective-permute-done.16 = f32[1,11,8,8,128]{4,3,2,1,0:T(8,128)S(1)} collective-permute-done((f32[1,11,8,8,128]{4,3,2,1,0:T(8,128)S(1)}, f32[1,11,8,8,128]{4,3,2,1,0:T(8,128)S(1)}, u32[]{:S(2)}, u32[]{:S(2)}) %collective-permute-start.16) | collective-permute-done | bytes 360480 | tf_op jit(solution)/shard_map/ppermute | solution.py:49
  92.3 1.8 collective-permute-start.8
  94.0 8.1 %collective-permute-done.17 = f32[2,11,8,8,128]{4,3,2,1,0:T(8,128)S(1)} collective-permute-done((f32[2,11,8,8,128]{4,3,2,1,0:T(8,128)S(1)}, f32[2,11,8,8,128]{4,3,2,1,0:T(8,128)S(1)}, u32[]{:S(2)}, u32[]{:S(2)}) %collective-permute-start.17) | collective-permute-done | bytes 720928 | tf_op jit(solution)/shard_map/ppermute | solution.py:49
  102.3 1.5 collective-permute-start.18
  104.4 7.7 %collective-permute-start.12 = (f32[4,10,8,8,128]{4,3,2,1,0:T(8,128)S(1)}, f32[4,10,8,8,128]{4,3,2,1,0:T(8,128)S(1)}, u32[]{:S(2)}, u32[]{:S(2)}) collective-permute-start(f32[4,10,8,8,128]{4,3,2,1,0:T(8,128)S(1)} %pad_maximum_fusion.2.refs_0_), channel_id=1, source_target_pairs={{0,8},{8,0},{1,9},{9,1},{2,10},{10,2},{3,11},{11,3},{4,12},{12,4},... | collective-permute-start | bytes 3932168 | tf_op jit(solution)/shard_map/ppermute | solution.py:41
  112.2 2.8 %collective-permute-start.19 = (f32[4,11,8,8,128]{4,3,2,1,0:T(8,128)S(1)}, f32[4,11,8,8,128]{4,3,2,1,0:T(8,128)}, u32[]{:S(2)}, u32[]{:S(2)}) collective-permute-start(f32[4,11,8,8,128]{4,3,2,1,0:T(8,128)S(1)} %pad_maximum_fusion.1.refs_8_), channel_id=1, source_target_pairs={{0,64},{8,200},{16,80},{24,216},{32,96},{40,232},{48,112},{56,248}... | collective-permute-start | bytes 4325384 | tf_op jit(solution)/shard_map/ppermute | solution.py:53
  114.9 11.1 %collective-permute-done.9.refs_1_ = f32[4,10,8,8,128]{4,3,2,1,0:T(8,128)S(1)} collective-permute-done((f32[4,10,8,8,128]{4,3,2,1,0:T(8,128)S(1)}, f32[4,10,8,8,128]{4,3,2,1,0:T(8,128)S(1)}, u32[]{:S(2)}, u32[]{:S(2)}) %collective-permute-start.9) | collective-permute-done | bytes 1310752 | tf_op jit(solution)/shard_map/ppermute | solution.py:53
  126.0 18.8 %collective-permute-start.21 = (f32[4,11,8,8,128]{4,3,2,1,0:T(8,128)S(1)}, f32[4,11,8,8,128]{4,3,2,1,0:T(8,128)S(1)}, u32[]{:S(2)}, u32[]{:S(2)}) collective-permute-start(f32[4,11,8,8,128]{4,3,2,1,0:T(8,128)S(1)} %pad_maximum_fusion.1.refs_8_), channel_id=1, source_target_pairs={{0,8},{8,0},{1,9},{9,1},{2,10},{10,2},{3,11},{11,3},{4,12},{12,4},... | collective-permute-start | bytes 4325384 | tf_op jit(solution)/shard_map/ppermute | solution.py:41
  144.8 2.1 collective-permute-start.11
  147.7 1.1 copy-done.5
  149.2 15.4 %collective-permute-done.20.refs_11_ = f32[4,11,8,8,128]{4,3,2,1,0:T(8,128)} collective-permute-done((f32[4,11,8,8,128]{4,3,2,1,0:T(8,128)}, f32[4,11,8,8,128]{4,3,2,1,0:T(8,128)}, u32[]{:S(2)}, u32[]{:S(2)}) %collective-permute-start.20) | collective-permute-done | bytes 1441824 | tf_op jit(solution)/shard_map/ppermute | solution.py:53
  165.0 1.1 copy-done.8
  167.7 2.8 %gather_fusion.2 = f32[48,8,128]{2,1,0:T(8,128)} fusion(f32[448,8,128]{2,1,0:T(8,128)} %bitcast.64, s32[1024]{0:T(1024)S(1)} %pad_clamp_fusion), kind=kCustom, calls=%fused_computation.2 | custom fusion | bytes 393408 | tf_op jit(solution)/shard_map/gather | solution.py:244
  170.5 1.3 collective-permute-done.15.refs_7_
  171.8 18.5 %solve.1 = (f32[16,1536]{1,0:T(8,128)}, f32[16,1536]{1,0:T(8,128)}) custom-call(s32[64]{0:T(128)} %reshape.190.source, s32[6,4]{1,0:T(8,128)} %copy.38.flags, f32[4,10,8,8,128]{4,3,2,1,0:T(8,128)} %copy-done.1, f32[4,10,8,8,128]{4,3,2,1,0:T(8,128)} %copy-done.6, f32[4,10,8,8,128]{4,3,2,1,0:T(8,128)} %collective-permute-done.10.refs_2_, ...), custom_call_target="tpu_custom_call" | custom-call | tf_op jit(solution)/shard_map/solve/pallas_call | solution.py:254
  190.6 5.2 %collective-permute-done.34 = f32[1,16,1536]{2,1,0:T(8,128)S(1)} collective-permute-done((f32[1,16,1536]{2,1,0:T(8,128)}, f32[1,16,1536]{2,1,0:T(8,128)S(1)}, u32[]{:S(2)}, u32[]{:S(2)}) %collective-permute-start.34) | collective-permute-done | bytes 98336 | tf_op jit(solution)/shard_map/ppermute | solution.py:49
  195.7 0.9 pad_maximum_fusion.8
  196.8 0.9 pad_maximum_fusion.7
  197.7 1.7 collective-permute-start.26
  199.4 2.2 collective-permute-done.35
  201.6 0.9 pad_maximum_fusion.6.refs_8_
  202.6 0.9 collective-permute-start.36
  203.5 1.5 collective-permute-start.39
  205.1 1.7 collective-permute-start.27
  206.8 1.7 collective-permute-start.28
  208.6 1.1 collective-permute-done.36.refs_9_
  209.7 3.9 %collective-permute-start.30 = (f32[4,16,1536]{2,1,0:T(8,128)S(1)}, f32[4,16,1536]{2,1,0:T(8,128)S(1)}, u32[]{:S(2)}, u32[]{:S(2)}) collective-permute-start(f32[4,16,1536]{2,1,0:T(8,128)S(1)} %pad_maximum_fusion.5.refs_0_), channel_id=1, source_target_pairs={{0,8},{8,0},{1,9},{9,1},{2,10},{10,2},{3,11},{11,3},{4,12},{12,4},... | collective-permute-start | bytes 1179656 | tf_op jit(solution)/shard_map/ppermute | solution.py:41
  213.8 3.2 %collective-permute-start.40 = (f32[4,16,1536]{2,1,0:T(8,128)S(1)}, f32[4,16,1536]{2,1,0:T(8,128)S(1)}, u32[]{:S(2)}, u32[]{:S(2)}) collective-permute-start(f32[4,16,1536]{2,1,0:T(8,128)S(1)} %collective-permute-done.36.refs_9_), channel_id=1, source_target_pairs={{0,8},{8,0},{1,9},{9,1},{2,10},{10,2},{3,11},{11,3},{4,12},{12,4},... | collective-permute-start | bytes 1179656 | tf_op jit(solution)/shard_map/ppermute | solution.py:41
  217.0 1.7 collective-permute-start.29
  218.7 1.3 collective-permute-start.31
  220.2 1.8 collective-permute-done.38.refs_11_
  222.0 2.7 collective-permute-start.32
  225.4 0.8 collective-permute-start.33
  229.0 33.5 %update.1 = f32[512,1664]{1,0:T(8,128)} custom-call(s32[64]{0:T(128)} %reshape.190.source, s32[17]{0:T(128)} %pad_add_fusion.1.flags, f32[4,16,1536]{2,1,0:T(8,128)} %copy-done.4, f32[4,16,1536]{2,1,0:T(8,128)} %copy-done.12, f32[4,16,1536]{2,1,0:T(8,128)} %copy-done.13, f32[4,16,1536]{2,1,0:T(8,128)} %collective-permute-done.29.refs_3_, ...), custom_call_target="tpu_custom_call" | custom-call | tf_op jit(solution)/shard_map/update/pallas_call | solution.py:273
  (142 shorter events, 9.9 us)
Async XLA Ops:
  6.5 222.3 %all-gather.2.cloned.1.call-start = ((), (), s32[]{:S(2)}) async-start(), calls=%async_computation.1 | async-start | bytes 23003136 | tf_op jit(solution)/shard_map/all_gather | solution.py:229
  14.2 34.2 %all-to-all-start = ((f32[32,14,8,128]{3,2,1,0:T(8,128)}), f32[32,14,8,128]{3,2,1,0:T(8,128)S(1)}, u32[]{:S(2)}, u32[]{:S(2)}) async-start(f32[32,14,8,128]{3,2,1,0:T(8,128)} %pad_maximum_fusion), calls=%async_computation | async-start | bytes 3670016 | tf_op jit(solution)/shard_map/all_to_all | solution.py:237
  49.1 9.6 %collective-permute-start = (f32[21,8,128]{2,1,0:T(8,128)S(1)}, f32[21,8,128]{2,1,0:T(8,128)S(1)}, u32[]{:S(2)}, u32[]{:S(2)}) collective-permute-start(f32[21,8,128]{2,1,0:T(8,128)S(1)} %gather_fusion.1), channel_id=1, source_target_pairs={{0,7},{1,0},{2,1},{3,2},{4,3},{5,4},{6,5},{7,6},{8,15},{9,8},{10,9... | collective-permute-start | bytes 258056 | tf_op jit(solution)/shard_map/ppermute | solution.py:65
  54.7 7.5 %collective-permute-start.3 = (f32[21,8,128]{2,1,0:T(8,128)S(1)}, f32[21,8,128]{2,1,0:T(8,128)S(1)}, u32[]{:S(2)}, u32[]{:S(2)}) collective-permute-start(f32[21,8,128]{2,1,0:T(8,128)S(1)} %gather_fusion.1), channel_id=1, source_target_pairs={{0,1},{1,2},{2,3},{3,4},{4,5},{5,6},{6,7},{7,0},{8,9},{9,10},{10,1... | collective-permute-start | bytes 258056 | tf_op jit(solution)/shard_map/ppermute | solution.py:63
  58.7 7.3 %collective-permute-start.1 = (f32[21,8,128]{2,1,0:T(8,128)S(1)}, f32[21,8,128]{2,1,0:T(8,128)S(1)}, u32[]{:S(2)}, u32[]{:S(2)}) collective-permute-start(f32[21,8,128]{2,1,0:T(8,128)S(1)} %collective-permute-done), channel_id=1, source_target_pairs={{0,7},{1,0},{2,1},{3,2},{4,3},{5,4},{6,5},{7,6},{8,15},{9,8},{10,9... | collective-permute-start | bytes 258056 | tf_op jit(solution)/shard_map/ppermute | solution.py:65
  62.2 7.3 %collective-permute-start.4 = (f32[21,8,128]{2,1,0:T(8,128)S(1)}, f32[21,8,128]{2,1,0:T(8,128)S(1)}, u32[]{:S(2)}, u32[]{:S(2)}) collective-permute-start(f32[21,8,128]{2,1,0:T(8,128)S(1)} %collective-permute-done.3), channel_id=1, source_target_pairs={{0,1},{1,2},{2,3},{3,4},{4,5},{5,6},{6,7},{7,0},{8,9},{9,10},{10,1... | collective-permute-start | bytes 258056 | tf_op jit(solution)/shard_map/ppermute | solution.py:63
  65.9 10.5 %collective-permute-start.2 = (f32[21,8,128]{2,1,0:T(8,128)S(1)}, f32[21,8,128]{2,1,0:T(8,128)S(1)}, u32[]{:S(2)}, u32[]{:S(2)}) collective-permute-start(f32[21,8,128]{2,1,0:T(8,128)S(1)} %collective-permute-done.1), channel_id=1, source_target_pairs={{0,7},{1,0},{2,1},{3,2},{4,3},{5,4},{6,5},{7,6},{8,15},{9,8},{10,9... | collective-permute-start | bytes 258056 | tf_op jit(solution)/shard_map/ppermute | solution.py:65
  69.5 7.0 %collective-permute-start.5 = (f32[21,8,128]{2,1,0:T(8,128)S(1)}, f32[21,8,128]{2,1,0:T(8,128)S(1)}, u32[]{:S(2)}, u32[]{:S(2)}) collective-permute-start(f32[21,8,128]{2,1,0:T(8,128)S(1)} %collective-permute-done.4), channel_id=1, source_target_pairs={{0,1},{1,2},{2,3},{3,4},{4,5},{5,6},{6,7},{7,0},{8,9},{9,10},{10,1... | collective-permute-start | bytes 258056 | tf_op jit(solution)/shard_map/ppermute | solution.py:63
  76.4 6.9 %collective-permute-start.6 = (f32[21,8,128]{2,1,0:T(8,128)S(1)}, f32[21,8,128]{2,1,0:T(8,128)S(1)}, u32[]{:S(2)}, u32[]{:S(2)}) collective-permute-start(f32[21,8,128]{2,1,0:T(8,128)S(1)} %collective-permute-done.5), channel_id=1, source_target_pairs={{0,1},{1,2},{2,3},{3,4},{4,5},{5,6},{6,7},{7,0},{8,9},{9,10},{10,1... | collective-permute-start | bytes 258056 | tf_op jit(solution)/shard_map/ppermute | solution.py:63
  83.5 8.0 %collective-permute-start.16 = (f32[1,11,8,8,128]{4,3,2,1,0:T(8,128)S(1)}, f32[1,11,8,8,128]{4,3,2,1,0:T(8,128)S(1)}, u32[]{:S(2)}, u32[]{:S(2)}) collective-permute-start(f32[1,11,8,8,128]{4,3,2,1,0:T(8,128)S(1)} %slice_bitcast_fusion), channel_id=1, source_target_pairs={{0,16},{8,56},{16,0},{24,40},{32,48},{40,24},{48,32},{56,8},{64,80... | collective-permute-start | bytes 1081352 | tf_op jit(solution)/shard_map/ppermute | solution.py:49
  84.6 7.6 %collective-permute-start.7 = (f32[1,10,8,8,128]{4,3,2,1,0:T(8,128)S(1)}, f32[1,10,8,8,128]{4,3,2,1,0:T(8,128)S(1)}, u32[]{:S(2)}, u32[]{:S(2)}) collective-permute-start(f32[1,10,8,8,128]{4,3,2,1,0:T(8,128)S(1)} %slice_bitcast_fusion.1), channel_id=1, source_target_pairs={{0,64},{8,200},{16,80},{24,216},{32,96},{40,232},{48,112},{56,248}... | collective-permute-start | bytes 983048 | tf_op jit(solution)/shard_map/ppermute | solution.py:49
  91.5 10.6 %collective-permute-start.17 = (f32[2,11,8,8,128]{4,3,2,1,0:T(8,128)S(1)}, f32[2,11,8,8,128]{4,3,2,1,0:T(8,128)S(1)}, u32[]{:S(2)}, u32[]{:S(2)}) collective-permute-start(f32[2,11,8,8,128]{4,3,2,1,0:T(8,128)S(1)} %pad_maximum_fusion.3), channel_id=1, source_target_pairs={{0,192},{8,72},{16,208},{24,88},{32,224},{40,104},{48,240},{56,120... | collective-permute-start | bytes 2162696 | tf_op jit(solution)/shard_map/ppermute | solution.py:49
  92.3 11.5 %collective-permute-start.8 = (f32[2,10,8,8,128]{4,3,2,1,0:T(8,128)S(1)}, f32[2,10,8,8,128]{4,3,2,1,0:T(8,128)S(1)}, u32[]{:S(2)}, u32[]{:S(2)}) collective-permute-start(f32[2,10,8,8,128]{4,3,2,1,0:T(8,128)S(1)} %pad_maximum_fusion.4), channel_id=1, source_target_pairs={{0,16},{8,56},{16,0},{24,40},{32,48},{40,24},{48,32},{56,8},{64,80... | collective-permute-start | bytes 1966088 | tf_op jit(solution)/shard_map/ppermute | solution.py:49
  102.2 68.3 %copy-start = (f32[4,11,8,8,128]{4,3,2,1,0:T(8,128)}, f32[4,11,8,8,128]{4,3,2,1,0:T(8,128)S(1)}, u32[]{:S(2)}) copy-start(f32[4,11,8,8,128]{4,3,2,1,0:T(8,128)S(1)} %pad_maximum_fusion.1.refs_8_) | copy-start | bytes 4325380
  102.2 64.7 %copy-start.19 = (s32[1,2,16]{2,1,0:T(2,128)S(1)}, s32[1,2,16]{2,1,0:T(2,128)}, u32[]{:S(2)}) copy-start(s32[1,2,16]{2,1,0:T(2,128)} %constant.111) | copy-start | bytes 388
  102.3 42.5 %collective-permute-start.18 = (f32[4,11,8,8,128]{4,3,2,1,0:T(8,128)S(1)}, f32[4,11,8,8,128]{4,3,2,1,0:T(8,128)}, u32[]{:S(2)}, u32[]{:S(2)}) collective-permute-start(f32[4,11,8,8,128]{4,3,2,1,0:T(8,128)S(1)} %pad_maximum_fusion.1.refs_8_), channel_id=1, source_target_pairs={{0,48},{8,24},{16,32},{24,8},{32,16},{40,56},{48,0},{56,40},{64,11... | collective-permute-start | bytes 4325384 | tf_op jit(solution)/shard_map/ppermute | solution.py:53
  103.9 67.9 %copy-start.1 = (f32[4,10,8,8,128]{4,3,2,1,0:T(8,128)}, f32[4,10,8,8,128]{4,3,2,1,0:T(8,128)S(1)}, u32[]{:S(2)}) copy-start(f32[4,10,8,8,128]{4,3,2,1,0:T(8,128)S(1)} %pad_maximum_fusion.2.refs_0_) | copy-start | bytes 3932164
  103.9 22.1 %collective-permute-start.9 = (f32[4,10,8,8,128]{4,3,2,1,0:T(8,128)S(1)}, f32[4,10,8,8,128]{4,3,2,1,0:T(8,128)S(1)}, u32[]{:S(2)}, u32[]{:S(2)}) collective-permute-start(f32[4,10,8,8,128]{4,3,2,1,0:T(8,128)S(1)} %pad_maximum_fusion.2.refs_0_), channel_id=1, source_target_pairs={{0,192},{8,72},{16,208},{24,88},{32,224},{40,104},{48,240},{56,120... | collective-permute-start | bytes 3932168 | tf_op jit(solution)/shard_map/ppermute | solution.py:53
  104.4 40.4 %collective-permute-start.10 = (f32[4,10,8,8,128]{4,3,2,1,0:T(8,128)S(1)}, f32[4,10,8,8,128]{4,3,2,1,0:T(8,128)}, u32[]{:S(2)}, u32[]{:S(2)}) collective-permute-start(f32[4,10,8,8,128]{4,3,2,1,0:T(8,128)S(1)} %pad_maximum_fusion.2.refs_0_), channel_id=1, source_target_pairs={{0,48},{8,24},{16,32},{24,8},{32,16},{40,56},{48,0},{56,40},{64,11... | collective-permute-start | bytes 3932168 | tf_op jit(solution)/shard_map/ppermute | solution.py:53
  104.4 42.5 %collective-permute-start.12 = (f32[4,10,8,8,128]{4,3,2,1,0:T(8,128)S(1)}, f32[4,10,8,8,128]{4,3,2,1,0:T(8,128)S(1)}, u32[]{:S(2)}, u32[]{:S(2)}) collective-permute-start(f32[4,10,8,8,128]{4,3,2,1,0:T(8,128)S(1)} %pad_maximum_fusion.2.refs_0_), channel_id=1, source_target_pairs={{0,8},{8,0},{1,9},{9,1},{2,10},{10,2},{3,11},{11,3},{4,12},{12,4},... | collective-permute-start | bytes 3932168 | tf_op jit(solution)/shard_map/ppermute | solution.py:41
  112.2 34.8 %collective-permute-start.19 = (f32[4,11,8,8,128]{4,3,2,1,0:T(8,128)S(1)}, f32[4,11,8,8,128]{4,3,2,1,0:T(8,128)}, u32[]{:S(2)}, u32[]{:S(2)}) collective-permute-start(f32[4,11,8,8,128]{4,3,2,1,0:T(8,128)S(1)} %pad_maximum_fusion.1.refs_8_), channel_id=1, source_target_pairs={{0,64},{8,200},{16,80},{24,216},{32,96},{40,232},{48,112},{56,248}... | collective-permute-start | bytes 4325384 | tf_op jit(solution)/shard_map/ppermute | solution.py:53
  126.0 21.6 %collective-permute-start.21 = (f32[4,11,8,8,128]{4,3,2,1,0:T(8,128)S(1)}, f32[4,11,8,8,128]{4,3,2,1,0:T(8,128)S(1)}, u32[]{:S(2)}, u32[]{:S(2)}) collective-permute-start(f32[4,11,8,8,128]{4,3,2,1,0:T(8,128)S(1)} %pad_maximum_fusion.1.refs_8_), channel_id=1, source_target_pairs={{0,8},{8,0},{1,9},{9,1},{2,10},{10,2},{3,11},{11,3},{4,12},{12,4},... | collective-permute-start | bytes 4325384 | tf_op jit(solution)/shard_map/ppermute | solution.py:41
  144.8 19.7 %collective-permute-start.20 = (f32[4,11,8,8,128]{4,3,2,1,0:T(8,128)}, f32[4,11,8,8,128]{4,3,2,1,0:T(8,128)}, u32[]{:S(2)}, u32[]{:S(2)}) collective-permute-start(f32[4,11,8,8,128]{4,3,2,1,0:T(8,128)} %collective-permute-done.18.refs_9_), channel_id=1, source_target_pairs={{0,64},{8,200},{16,80},{24,216},{32,96},{40,232},{48,112},{56,248}... | collective-permute-start | bytes 4325384 | tf_op jit(solution)/shard_map/ppermute | solution.py:53
  144.8 19.7 %collective-permute-start.11 = (f32[4,10,8,8,128]{4,3,2,1,0:T(8,128)S(1)}, f32[4,10,8,8,128]{4,3,2,1,0:T(8,128)}, u32[]{:S(2)}, u32[]{:S(2)}) collective-permute-start(f32[4,10,8,8,128]{4,3,2,1,0:T(8,128)S(1)} %collective-permute-done.9.refs_1_), channel_id=1, source_target_pairs={{0,48},{8,24},{16,32},{24,8},{32,16},{40,56},{48,0},{56,40},{64,11... | collective-permute-start | bytes 3932168 | tf_op jit(solution)/shard_map/ppermute | solution.py:53
  147.0 18.1 %collective-permute-start.13 = (f32[4,10,8,8,128]{4,3,2,1,0:T(8,128)S(1)}, f32[4,10,8,8,128]{4,3,2,1,0:T(8,128)S(1)}, u32[]{:S(2)}, u32[]{:S(2)}) collective-permute-start(f32[4,10,8,8,128]{4,3,2,1,0:T(8,128)S(1)} %collective-permute-done.9.refs_1_), channel_id=1, source_target_pairs={{0,8},{8,0},{1,9},{9,1},{2,10},{10,2},{3,11},{11,3},{4,12},{12,4},... | collective-permute-start | bytes 3932168 | tf_op jit(solution)/shard_map/ppermute | solution.py:41
  147.0 23.5 %collective-permute-start.22 = (f32[4,11,8,8,128]{4,3,2,1,0:T(8,128)}, f32[4,11,8,8,128]{4,3,2,1,0:T(8,128)}, u32[]{:S(2)}, u32[]{:S(2)}) collective-permute-start(f32[4,11,8,8,128]{4,3,2,1,0:T(8,128)} %collective-permute-done.18.refs_9_), channel_id=1, source_target_pairs={{0,8},{8,0},{1,9},{9,1},{2,10},{10,2},{3,11},{11,3},{4,12},{12,4},... | collective-permute-start | bytes 4325384 | tf_op jit(solution)/shard_map/ppermute | solution.py:41
  148.8 21.7 %collective-permute-start.23 = (f32[4,11,8,8,128]{4,3,2,1,0:T(8,128)}, f32[4,11,8,8,128]{4,3,2,1,0:T(8,128)}, u32[]{:S(2)}, u32[]{:S(2)}) collective-permute-start(f32[4,11,8,8,128]{4,3,2,1,0:T(8,128)} %collective-permute-done.19.refs_10_), channel_id=1, source_target_pairs={{0,8},{8,0},{1,9},{9,1},{2,10},{10,2},{3,11},{11,3},{4,12},{12,4},... | collective-permute-start | bytes 4325384 | tf_op jit(solution)/shard_map/ppermute | solution.py:41
  164.5 7.3 %collective-permute-start.24 = (f32[4,11,8,8,128]{4,3,2,1,0:T(8,128)}, f32[4,11,8,8,128]{4,3,2,1,0:T(8,128)}, u32[]{:S(2)}, u32[]{:S(2)}) collective-permute-start(f32[4,11,8,8,128]{4,3,2,1,0:T(8,128)} %collective-permute-done.20.refs_11_), channel_id=1, source_target_pairs={{0,8},{8,0},{1,9},{9,1},{2,10},{10,2},{3,11},{11,3},{4,12},{12,4},... | collective-permute-start | bytes 4325384 | tf_op jit(solution)/shard_map/ppermute | solution.py:41
  164.5 6.0 %collective-permute-start.14 = (f32[4,10,8,8,128]{4,3,2,1,0:T(8,128)}, f32[4,10,8,8,128]{4,3,2,1,0:T(8,128)}, u32[]{:S(2)}, u32[]{:S(2)}) collective-permute-start(f32[4,10,8,8,128]{4,3,2,1,0:T(8,128)} %collective-permute-done.10.refs_2_), channel_id=1, source_target_pairs={{0,8},{8,0},{1,9},{9,1},{2,10},{10,2},{3,11},{11,3},{4,12},{12,4},... | collective-permute-start | bytes 3932168 | tf_op jit(solution)/shard_map/ppermute | solution.py:41
  166.1 5.7 %collective-permute-start.15 = (f32[4,10,8,8,128]{4,3,2,1,0:T(8,128)}, f32[4,10,8,8,128]{4,3,2,1,0:T(8,128)}, u32[]{:S(2)}, u32[]{:S(2)}) collective-permute-start(f32[4,10,8,8,128]{4,3,2,1,0:T(8,128)} %collective-permute-done.11.refs_3_), channel_id=1, source_target_pairs={{0,8},{8,0},{1,9},{9,1},{2,10},{10,2},{3,11},{11,3},{4,12},{12,4},... | collective-permute-start | bytes 3932168 | tf_op jit(solution)/shard_map/ppermute | solution.py:41
  190.3 5.4 %collective-permute-start.34 = (f32[1,16,1536]{2,1,0:T(8,128)}, f32[1,16,1536]{2,1,0:T(8,128)S(1)}, u32[]{:S(2)}, u32[]{:S(2)}) collective-permute-start(f32[1,16,1536]{2,1,0:T(8,128)} %bitcast.69), channel_id=1, source_target_pairs={{0,16},{8,56},{16,0},{24,40},{32,48},{40,24},{48,32},{56,8},{64,80... | collective-permute-start | bytes 294920 | tf_op jit(solution)/shard_map/ppermute | solution.py:49
  190.4 6.3 %collective-permute-start.25 = (f32[1,16,1536]{2,1,0:T(8,128)}, f32[1,16,1536]{2,1,0:T(8,128)S(1)}, u32[]{:S(2)}, u32[]{:S(2)}) collective-permute-start(f32[1,16,1536]{2,1,0:T(8,128)} %bitcast.66), channel_id=1, source_target_pairs={{0,64},{8,200},{16,80},{24,216},{32,96},{40,232},{48,112},{56,248}... | collective-permute-start | bytes 294920 | tf_op jit(solution)/shard_map/ppermute | solution.py:49
  196.6 5.0 %collective-permute-start.35 = (f32[2,16,1536]{2,1,0:T(8,128)S(1)}, f32[2,16,1536]{2,1,0:T(8,128)S(1)}, u32[]{:S(2)}, u32[]{:S(2)}) collective-permute-start(f32[2,16,1536]{2,1,0:T(8,128)S(1)} %pad_maximum_fusion.8), channel_id=1, source_target_pairs={{0,192},{8,72},{16,208},{24,88},{32,224},{40,104},{48,240},{56,120... | collective-permute-start | bytes 589832 | tf_op jit(solution)/shard_map/ppermute | solution.py:49
  197.7 7.4 %collective-permute-start.26 = (f32[2,16,1536]{2,1,0:T(8,128)S(1)}, f32[2,16,1536]{2,1,0:T(8,128)S(1)}, u32[]{:S(2)}, u32[]{:S(2)}) collective-permute-start(f32[2,16,1536]{2,1,0:T(8,128)S(1)} %pad_maximum_fusion.7), channel_id=1, source_target_pairs={{0,16},{8,56},{16,0},{24,40},{32,48},{40,24},{48,32},{56,8},{64,80... | collective-permute-start | bytes 589832 | tf_op jit(solution)/shard_map/ppermute | solution.py:49
  202.6 7.1 %collective-permute-start.36 = (f32[4,16,1536]{2,1,0:T(8,128)S(1)}, f32[4,16,1536]{2,1,0:T(8,128)S(1)}, u32[]{:S(2)}, u32[]{:S(2)}) collective-permute-start(f32[4,16,1536]{2,1,0:T(8,128)S(1)} %pad_maximum_fusion.6.refs_8_), channel_id=1, source_target_pairs={{0,48},{8,24},{16,32},{24,8},{32,16},{40,56},{48,0},{56,40},{64,11... | collective-permute-start | bytes 1179656 | tf_op jit(solution)/shard_map/ppermute | solution.py:53
  203.5 10.3 %collective-permute-start.37 = (f32[4,16,1536]{2,1,0:T(8,128)S(1)}, f32[4,16,1536]{2,1,0:T(8,128)S(1)}, u32[]{:S(2)}, u32[]{:S(2)}) collective-permute-start(f32[4,16,1536]{2,1,0:T(8,128)S(1)} %pad_maximum_fusion.6.refs_8_), channel_id=1, source_target_pairs={{0,64},{8,200},{16,80},{24,216},{32,96},{40,232},{48,112},{56,248}... | collective-permute-start | bytes 1179656 | tf_op jit(solution)/shard_map/ppermute | solution.py:53
  203.5 10.2 %collective-permute-start.39 = (f32[4,16,1536]{2,1,0:T(8,128)S(1)}, f32[4,16,1536]{2,1,0:T(8,128)S(1)}, u32[]{:S(2)}, u32[]{:S(2)}) collective-permute-start(f32[4,16,1536]{2,1,0:T(8,128)S(1)} %pad_maximum_fusion.6.refs_8_), channel_id=1, source_target_pairs={{0,8},{8,0},{1,9},{9,1},{2,10},{10,2},{3,11},{11,3},{4,12},{12,4},... | collective-permute-start | bytes 1179656 | tf_op jit(solution)/shard_map/ppermute | solution.py:41
  205.1 11.9 %collective-permute-start.27 = (f32[4,16,1536]{2,1,0:T(8,128)S(1)}, f32[4,16,1536]{2,1,0:T(8,128)S(1)}, u32[]{:S(2)}, u32[]{:S(2)}) collective-permute-start(f32[4,16,1536]{2,1,0:T(8,128)S(1)} %pad_maximum_fusion.5.refs_0_), channel_id=1, source_target_pairs={{0,192},{8,72},{16,208},{24,88},{32,224},{40,104},{48,240},{56,120... | collective-permute-start | bytes 1179656 | tf_op jit(solution)/shard_map/ppermute | solution.py:53
  206.8 11.9 %collective-permute-start.28 = (f32[4,16,1536]{2,1,0:T(8,128)S(1)}, f32[4,16,1536]{2,1,0:T(8,128)S(1)}, u32[]{:S(2)}, u32[]{:S(2)}) collective-permute-start(f32[4,16,1536]{2,1,0:T(8,128)S(1)} %pad_maximum_fusion.5.refs_0_), channel_id=1, source_target_pairs={{0,48},{8,24},{16,32},{24,8},{32,16},{40,56},{48,0},{56,40},{64,11... | collective-permute-start | bytes 1179656 | tf_op jit(solution)/shard_map/ppermute | solution.py:53
  209.7 10.3 %collective-permute-start.30 = (f32[4,16,1536]{2,1,0:T(8,128)S(1)}, f32[4,16,1536]{2,1,0:T(8,128)S(1)}, u32[]{:S(2)}, u32[]{:S(2)}) collective-permute-start(f32[4,16,1536]{2,1,0:T(8,128)S(1)} %pad_maximum_fusion.5.refs_0_), channel_id=1, source_target_pairs={{0,8},{8,0},{1,9},{9,1},{2,10},{10,2},{3,11},{11,3},{4,12},{12,4},... | collective-permute-start | bytes 1179656 | tf_op jit(solution)/shard_map/ppermute | solution.py:41
  213.8 8.2 %collective-permute-start.38 = (f32[4,16,1536]{2,1,0:T(8,128)S(1)}, f32[4,16,1536]{2,1,0:T(8,128)S(1)}, u32[]{:S(2)}, u32[]{:S(2)}) collective-permute-start(f32[4,16,1536]{2,1,0:T(8,128)S(1)} %collective-permute-done.36.refs_9_), channel_id=1, source_target_pairs={{0,64},{8,200},{16,80},{24,216},{32,96},{40,232},{48,112},{56,248}... | collective-permute-start | bytes 1179656 | tf_op jit(solution)/shard_map/ppermute | solution.py:53
  213.8 10.9 %collective-permute-start.40 = (f32[4,16,1536]{2,1,0:T(8,128)S(1)}, f32[4,16,1536]{2,1,0:T(8,128)S(1)}, u32[]{:S(2)}, u32[]{:S(2)}) collective-permute-start(f32[4,16,1536]{2,1,0:T(8,128)S(1)} %collective-permute-done.36.refs_9_), channel_id=1, source_target_pairs={{0,8},{8,0},{1,9},{9,1},{2,10},{10,2},{3,11},{11,3},{4,12},{12,4},... | collective-permute-start | bytes 1179656 | tf_op jit(solution)/shard_map/ppermute | solution.py:41
  217.0 7.8 %collective-permute-start.29 = (f32[4,16,1536]{2,1,0:T(8,128)S(1)}, f32[4,16,1536]{2,1,0:T(8,128)}, u32[]{:S(2)}, u32[]{:S(2)}) collective-permute-start(f32[4,16,1536]{2,1,0:T(8,128)S(1)} %collective-permute-done.27.refs_1_), channel_id=1, source_target_pairs={{0,48},{8,24},{16,32},{24,8},{32,16},{40,56},{48,0},{56,40},{64,11... | collective-permute-start | bytes 1179656 | tf_op jit(solution)/shard_map/ppermute | solution.py:53
  218.7 10.1 %collective-permute-start.31 = (f32[4,16,1536]{2,1,0:T(8,128)S(1)}, f32[4,16,1536]{2,1,0:T(8,128)}, u32[]{:S(2)}, u32[]{:S(2)}) collective-permute-start(f32[4,16,1536]{2,1,0:T(8,128)S(1)} %collective-permute-done.27.refs_1_), channel_id=1, source_target_pairs={{0,8},{8,0},{1,9},{9,1},{2,10},{10,2},{3,11},{11,3},{4,12},{12,4},... | collective-permute-start | bytes 1179656 | tf_op jit(solution)/shard_map/ppermute | solution.py:41
  220.0 8.8 %collective-permute-start.41 = (f32[4,16,1536]{2,1,0:T(8,128)S(1)}, f32[4,16,1536]{2,1,0:T(8,128)}, u32[]{:S(2)}, u32[]{:S(2)}) collective-permute-start(f32[4,16,1536]{2,1,0:T(8,128)S(1)} %collective-permute-done.37.refs_10_), channel_id=1, source_target_pairs={{0,8},{8,0},{1,9},{9,1},{2,10},{10,2},{3,11},{11,3},{4,12},{12,4},... | collective-permute-start | bytes 1179656 | tf_op jit(solution)/shard_map/ppermute | solution.py:41
  222.0 6.8 %collective-permute-start.32 = (f32[4,16,1536]{2,1,0:T(8,128)S(1)}, f32[4,16,1536]{2,1,0:T(8,128)}, u32[]{:S(2)}, u32[]{:S(2)}) collective-permute-start(f32[4,16,1536]{2,1,0:T(8,128)S(1)} %collective-permute-done.28.refs_2_), channel_id=1, source_target_pairs={{0,8},{8,0},{1,9},{9,1},{2,10},{10,2},{3,11},{11,3},{4,12},{12,4},... | collective-permute-start | bytes 1179656 | tf_op jit(solution)/shard_map/ppermute | solution.py:41
  224.7 4.2 %collective-permute-start.42 = (f32[4,16,1536]{2,1,0:T(8,128)S(1)}, f32[4,16,1536]{2,1,0:T(8,128)}, u32[]{:S(2)}, u32[]{:S(2)}) collective-permute-start(f32[4,16,1536]{2,1,0:T(8,128)S(1)} %collective-permute-done.38.refs_11_), channel_id=1, source_target_pairs={{0,8},{8,0},{1,9},{9,1},{2,10},{10,2},{3,11},{11,3},{4,12},{12,4},... | collective-permute-start | bytes 1179656 | tf_op jit(solution)/shard_map/ppermute | solution.py:41
  225.4 3.4 %collective-permute-start.33 = (f32[4,16,1536]{2,1,0:T(8,128)}, f32[4,16,1536]{2,1,0:T(8,128)}, u32[]{:S(2)}, u32[]{:S(2)}) collective-permute-start(f32[4,16,1536]{2,1,0:T(8,128)} %collective-permute-done.29.refs_3_), channel_id=1, source_target_pairs={{0,8},{8,0},{1,9},{9,1},{2,10},{10,2},{3,11},{11,3},{4,12},{12,4},... | collective-permute-start | bytes 1179656 | tf_op jit(solution)/shard_map/ppermute | solution.py:41
  (23 other events, 508.5 us)
Sparse Core Ops, SparseCore 0:
  9.1 218.1 all-gather.1

commit v4 on v3

--- a/solution.py
+++ b/solution.py
@@ -41,7 +41,7 @@
     return lax.ppermute(value, "col_2", [(0, 1), (1, 0)])
 
 
-def spread(streams):
+def spread(streams, beside=()):
     every = []
     for i, value in enumerate(streams):
         value = value[None]
@@ -51,7 +51,9 @@
     for stage in (2, 3):
         for i, parts in enumerate(every):
             parts += [lax.ppermute(part, COL, exchange(i, stage)) for part in parts]
-    return [parts + [other_core(part) for part in parts] for parts in every]
+            if beside and stage == 2 and i == 0:
+                parts[1], *beside = lax.optimization_barrier((parts[1], *beside))
+    return [parts + [other_core(part) for part in parts] for parts in every], beside
 
 
 def all_rows(value):
@@ -196,15 +198,12 @@
 
         lax.fori_loop(0, P_SIZE, divide, 0)
 
-    out[...] = weights[...]
-
-    def take(k, carry):
+    total = weights[...]
+    for k in range(P_SIZE):
         high, low = halves(factor[k])
         rows = jnp.concatenate([high, high, low], 0)
-        out[...] = out[...] - jnp.dot(split[k], rows, preferred_element_type=jnp.float32)
-        return carry
-
-    lax.fori_loop(0, P_SIZE, take, 0)
+        total = total - jnp.dot(split[k], rows, preferred_element_type=jnp.float32)
+    out[...] = total
     for part in range(NARROW // TILE):
         tile = n * (NARROW // TILE) + part - flags[0]
         inside = jnp.logical_and(tile >= 0, tile < PANEL_TILES)
@@ -245,9 +244,13 @@
     windows = windows.reshape(P_SIZE, 2, 4, 8, TILE).transpose(0, 1, 3, 2, 4)
     windows = windows.reshape(P_SIZE, MINE, PW)
     source = sources()
-    spread_parts = spread([picked[:EARLY], picked[EARLY:]])
 
     own_rows = lax.dynamic_slice(prune_mask, (0, me // 8, 0), (P_SIZE, 1, PANEL_TILES))[:, 0]
+    pruned = jnp.sum(jnp.where(mine[:, None, None], prune_mask, 0), 0).reshape(-1)
+    flags = jnp.concatenate([(shift // TILE)[None], pruned]).astype(jnp.int32)
+    spread_parts, (windows, source, own_rows, flags) = spread(
+        [picked[:EARLY], picked[EARLY:]], (windows, source, own_rows, flags)
+    )
     any_spec = pl.BlockSpec(memory_space=pl.ANY)
     vmem = pl.BlockSpec(memory_space=pltpu.VMEM)
     smem = pl.BlockSpec(memory_space=pltpu.SMEM)
@@ -265,9 +268,7 @@
         name="solve",
     )(source, own_rows, *spread_parts[0], *spread_parts[1], windows, diag_inverse)
 
-    spread_errors = spread(found)
-    pruned = jnp.sum(jnp.where(mine[:, None, None], prune_mask, 0), 0).reshape(-1)
-    flags = jnp.concatenate([(shift // TILE)[None], pruned]).astype(jnp.int32)
+    spread_errors, _ = spread(found)
     steps = pl.cdiv(width, NARROW)
     column = lambda i, *_: (0, i)
     return pl.pallas_call(

time: 270 us -> 262 us (0.970)
  Pallas kernels: 52 us -> 45.8 us
    pallas_call x1, Pallas kernels: 33.5 us -> 27.2 us  [shards(): pl.pallas_call(update_kernel, out_shape=jax.ShapeDtypeStruct(weights.shap...]
    ppermute x12, waiting for transfers between devices: 29.6 us -> 25.4 us  [spread(): parts += [lax.ppermute(part, COL, exchange(i, stage)) for part in parts]]
    ppermute x16, waiting for transfers between devices: 1.52 us -> 4.27 us  [other_core(): return lax.ppermute(value, 'col_2', [(0, 1), (1, 0)])]
  transfers between devices with their start and end apart: 45 -> 45, of which waited for: 17 -> 19; matrix products, arithmetic and copies ran while one was open for 6% -> 6% of each run, Pallas kernels for 7% -> 7%
where the time goes in v4:
time: 262 us; the launch traced here: 261 us
  waiting for transfers between devices  98.5 us (38%)
  starting transfers between devices  82.7 us (32%)
  Pallas kernels  45.8 us (17%)
  between operations  17.8 us (7%)
  local copies, waits for them, and re-layouts  10.7 us (4%)
  other arithmetic  5.98 us (2%)
    ppermute x16, starting transfers between devices, other_core(): return lax.ppermute(value, 'col_2', [(0, 1), (1, 0)])  41.2 us
    pallas_call x1, Pallas kernels, shards(): pl.pallas_call(update_kernel, out_shape=jax.ShapeDtypeStruct(weights.shap...  27.2 us
    ppermute x12, waiting for transfers between devices, spread(): parts += [lax.ppermute(part, COL, exchange(i, stage)) for part in parts]  25.4 us
    all_to_all x1, waiting for transfers between devices, shards(): lax.all_to_all(jnp.concatenate([pieces, wanted], 1), COL, 0, 0, tiled=True)  24.7 us
    ppermute x8, waiting for transfers between devices, spread(): lax.ppermute(value, COL, exchange(i, stage))  21 us
    pallas_call x1, Pallas kernels, shards(): pl.pallas_call(solve_kernel, out_shape=[jax.ShapeDtypeStruct((MINE, 3 * P...  18.5 us
    ppermute x4, waiting for transfers between devices, all_rows(): below.append(lax.ppermute(below[-1], 'row', up))  13.8 us
    ppermute x12, starting transfers between devices, spread(): parts += [lax.ppermute(part, COL, exchange(i, stage)) for part in parts]  12.9 us
  transfers between devices with their start and end apart: 45, of which 19 were waited for; matrix products, arithmetic and copies ran while one was open for 6% of the time, Pallas kernels for 7%

profile of v4, /device:TPU:1, one launch (start us, length us, event | category | flops | bytes accessed | tf_op | source)
XLA Modules:
  0.0 261.5 jit_solution(4997718738262437810)
XLA Ops:
  9.9 1.5 dynamic-slice_bitcast_fusion
  11.4 1.7 constant_dynamic-slice_fusion.1
  13.1 1.4 pad_maximum_fusion
  14.4 8.7 %all-to-all-start = ((f32[32,14,8,128]{3,2,1,0:T(8,128)}), f32[32,14,8,128]{3,2,1,0:T(8,128)S(1)}, u32[]{:S(2)}, u32[]{:S(2)}) async-start(f32[32,14,8,128]{3,2,1,0:T(8,128)} %pad_maximum_fusion), calls=%async_computation | async-start | bytes 3670016 | tf_op jit(solution)/shard_map/all_to_all | solution.py:236
  24.0 24.7 %all-to-all-done = f32[32,14,8,128]{3,2,1,0:T(8,128)S(1)} async-done(((f32[32,14,8,128]{3,2,1,0:T(8,128)}), f32[32,14,8,128]{3,2,1,0:T(8,128)S(1)}, u32[]{:S(2)}, u32[]{:S(2)}) %all-to-all-start) | async-done | bytes 1835040 | tf_op jit(solution)/shard_map/all_to_all | solution.py:236
  49.3 5.7 %collective-permute-start = (f32[21,8,128]{2,1,0:T(8,128)S(1)}, f32[21,8,128]{2,1,0:T(8,128)S(1)}, u32[]{:S(2)}, u32[]{:S(2)}) collective-permute-start(f32[21,8,128]{2,1,0:T(8,128)S(1)} %gather_fusion.1), channel_id=1, source_target_pairs={{0,7},{1,0},{2,1},{3,2},{4,3},{5,4},{6,5},{7,6},{8,15},{9,8},{10,9... | collective-permute-start | bytes 258056 | tf_op jit(solution)/shard_map/ppermute | solution.py:67
  55.0 3.9 %collective-permute-done = f32[21,8,128]{2,1,0:T(8,128)S(1)} collective-permute-done((f32[21,8,128]{2,1,0:T(8,128)S(1)}, f32[21,8,128]{2,1,0:T(8,128)S(1)}, u32[]{:S(2)}, u32[]{:S(2)}) %collective-permute-start) | collective-permute-done | bytes 86048 | tf_op jit(solution)/shard_map/ppermute | solution.py:67
  58.9 3.5 %collective-permute-start.1 = (f32[21,8,128]{2,1,0:T(8,128)S(1)}, f32[21,8,128]{2,1,0:T(8,128)S(1)}, u32[]{:S(2)}, u32[]{:S(2)}) collective-permute-start(f32[21,8,128]{2,1,0:T(8,128)S(1)} %collective-permute-done), channel_id=1, source_target_pairs={{0,7},{1,0},{2,1},{3,2},{4,3},{5,4},{6,5},{7,6},{8,15},{9,8},{10,9... | collective-permute-start | bytes 258056 | tf_op jit(solution)/shard_map/ppermute | solution.py:67
  62.4 3.7 %collective-permute-done.1 = f32[21,8,128]{2,1,0:T(8,128)S(1)} collective-permute-done((f32[21,8,128]{2,1,0:T(8,128)S(1)}, f32[21,8,128]{2,1,0:T(8,128)S(1)}, u32[]{:S(2)}, u32[]{:S(2)}) %collective-permute-start.1) | collective-permute-done | bytes 86048 | tf_op jit(solution)/shard_map/ppermute | solution.py:67
  66.1 3.5 %collective-permute-start.2 = (f32[21,8,128]{2,1,0:T(8,128)S(1)}, f32[21,8,128]{2,1,0:T(8,128)S(1)}, u32[]{:S(2)}, u32[]{:S(2)}) collective-permute-start(f32[21,8,128]{2,1,0:T(8,128)S(1)} %collective-permute-done.1), channel_id=1, source_target_pairs={{0,7},{1,0},{2,1},{3,2},{4,3},{5,4},{6,5},{7,6},{8,15},{9,8},{10,9... | collective-permute-start | bytes 258056 | tf_op jit(solution)/shard_map/ppermute | solution.py:67
  69.7 7.0 %collective-permute-done.5 = f32[21,8,128]{2,1,0:T(8,128)S(1)} collective-permute-done((f32[21,8,128]{2,1,0:T(8,128)S(1)}, f32[21,8,128]{2,1,0:T(8,128)S(1)}, u32[]{:S(2)}, u32[]{:S(2)}) %collective-permute-start.5) | collective-permute-done | bytes 86048 | tf_op jit(solution)/shard_map/ppermute | solution.py:65
  76.7 6.9 %collective-permute-done.6 = f32[21,8,128]{2,1,0:T(8,128)S(1)} collective-permute-done((f32[21,8,128]{2,1,0:T(8,128)S(1)}, f32[21,8,128]{2,1,0:T(8,128)S(1)}, u32[]{:S(2)}, u32[]{:S(2)}) %collective-permute-start.6) | collective-permute-done | bytes 86048 | tf_op jit(solution)/shard_map/ppermute | solution.py:65
  83.7 1.1 collective-permute-start.16
  85.4 6.2 %collective-permute-done.16 = f32[1,11,8,8,128]{4,3,2,1,0:T(8,128)S(1)} collective-permute-done((f32[1,11,8,8,128]{4,3,2,1,0:T(8,128)S(1)}, f32[1,11,8,8,128]{4,3,2,1,0:T(8,128)S(1)}, u32[]{:S(2)}, u32[]{:S(2)}) %collective-permute-start.16) | collective-permute-done | bytes 360480 | tf_op jit(solution)/shard_map/ppermute | solution.py:49
  92.5 1.7 collective-permute-start.8
  94.2 8.1 %collective-permute-done.17 = f32[2,11,8,8,128]{4,3,2,1,0:T(8,128)S(1)} collective-permute-done((f32[2,11,8,8,128]{4,3,2,1,0:T(8,128)S(1)}, f32[2,11,8,8,128]{4,3,2,1,0:T(8,128)S(1)}, u32[]{:S(2)}, u32[]{:S(2)}) %collective-permute-start.17) | collective-permute-done | bytes 720928 | tf_op jit(solution)/shard_map/ppermute | solution.py:49
  102.5 1.5 collective-permute-start.18
  106.7 7.8 %collective-permute-start.12 = (f32[4,10,8,8,128]{4,3,2,1,0:T(8,128)S(1)}, f32[4,10,8,8,128]{4,3,2,1,0:T(8,128)}, u32[]{:S(2)}, u32[]{:S(2)}) collective-permute-start(f32[4,10,8,8,128]{4,3,2,1,0:T(8,128)S(1)} %pad_maximum_fusion.2.refs_0_), channel_id=1, source_target_pairs={{0,8},{8,0},{1,9},{9,1},{2,10},{10,2},{3,11},{11,3},{4,12},{12,4},... | collective-permute-start | bytes 3932168 | tf_op jit(solution)/shard_map/ppermute | solution.py:41
  114.9 3.0 %collective-permute-start.19 = (f32[4,11,8,8,128]{4,3,2,1,0:T(8,128)S(1)}, f32[4,11,8,8,128]{4,3,2,1,0:T(8,128)}, u32[]{:S(2)}, u32[]{:S(2)}) collective-permute-start(f32[4,11,8,8,128]{4,3,2,1,0:T(8,128)S(1)} %pad_maximum_fusion.1.refs_8_), channel_id=1, source_target_pairs={{0,64},{8,200},{16,80},{24,216},{32,96},{40,232},{48,112},{56,248}... | collective-permute-start | bytes 4325384 | tf_op jit(solution)/shard_map/ppermute | solution.py:53
  117.9 5.9 %collective-permute-done.9.refs_1_ = f32[4,10,8,8,128]{4,3,2,1,0:T(8,128)} collective-permute-done((f32[4,10,8,8,128]{4,3,2,1,0:T(8,128)S(1)}, f32[4,10,8,8,128]{4,3,2,1,0:T(8,128)}, u32[]{:S(2)}, u32[]{:S(2)}) %collective-permute-start.9) | collective-permute-done | bytes 1310752 | tf_op jit(solution)/shard_map/ppermute | solution.py:53
  123.9 18.6 %collective-permute-start.21 = (f32[4,11,8,8,128]{4,3,2,1,0:T(8,128)S(1)}, f32[4,11,8,8,128]{4,3,2,1,0:T(8,128)}, u32[]{:S(2)}, u32[]{:S(2)}) collective-permute-start(f32[4,11,8,8,128]{4,3,2,1,0:T(8,128)S(1)} %pad_maximum_fusion.1.refs_8_), channel_id=1, source_target_pairs={{0,8},{8,0},{1,9},{9,1},{2,10},{10,2},{3,11},{11,3},{4,12},{12,4},... | collective-permute-start | bytes 4325384 | tf_op jit(solution)/shard_map/ppermute | solution.py:41
  143.7 2.8 %gather_fusion.2 = f32[48,8,128]{2,1,0:T(8,128)} fusion(f32[448,8,128]{2,1,0:T(8,128)} %bitcast.64, s32[1024]{0:T(1024)S(1)} %pad_clamp_fusion), kind=kCustom, calls=%fused_computation.2 | custom fusion | bytes 393408 | tf_op jit(solution)/shard_map/gather | solution.py:243
  146.5 2.0 collective-permute-start.11
  149.1 13.0 %collective-permute-done.20.refs_11_ = f32[4,11,8,8,128]{4,3,2,1,0:T(8,128)} collective-permute-done((f32[4,11,8,8,128]{4,3,2,1,0:T(8,128)}, f32[4,11,8,8,128]{4,3,2,1,0:T(8,128)}, u32[]{:S(2)}, u32[]{:S(2)}) %collective-permute-start.20) | collective-permute-done | bytes 1441824 | tf_op jit(solution)/shard_map/ppermute | solution.py:53
  162.1 2.0 collective-permute-done.11.refs_3_
  164.1 1.5 collective-permute-start.14
  166.3 2.3 collective-permute-done.14.refs_6_
  168.6 1.9 collective-permute-done.15.refs_7_
  170.5 18.5 %solve.1 = (f32[16,1536]{1,0:T(8,128)}, f32[16,1536]{1,0:T(8,128)}) custom-call(s32[64]{0:T(128)} %reshape.197.source, s32[6,4]{1,0:T(8,128)} %copy.38.flags, f32[4,10,8,8,128]{4,3,2,1,0:T(8,128)} %copy-done.1, f32[4,10,8,8,128]{4,3,2,1,0:T(8,128)} %collective-permute-done.9.refs_1_, f32[4,10,8,8,128]{4,3,2,1,0:T(8,128)} %collective-permute-done.10.refs_2_, ...), custom_call_target="tpu_custom_call" | custom-call | tf_op jit(solution)/shard_map/solve/pallas_call | solution.py:257
  189.2 1.6 collective-permute-start.25
  190.8 3.7 %collective-permute-done.34 = f32[1,16,1536]{2,1,0:T(8,128)S(1)} collective-permute-done((f32[1,16,1536]{2,1,0:T(8,128)}, f32[1,16,1536]{2,1,0:T(8,128)S(1)}, u32[]{:S(2)}, u32[]{:S(2)}) %collective-permute-start.34) | collective-permute-done | bytes 98336 | tf_op jit(solution)/shard_map/ppermute | solution.py:49
  194.4 0.9 pad_maximum_fusion.8
  195.4 1.8 collective-permute-start.35
  197.2 0.9 pad_maximum_fusion.7
  198.2 2.4 collective-permute-done.35
  200.7 0.9 pad_maximum_fusion.6.refs_8_
  201.9 1.5 collective-permute-start.37
  203.4 1.0 collective-permute-start.39
  204.4 1.0 collective-permute-start.27
  206.2 2.7 %collective-permute-done.36.refs_9_ = f32[4,16,1536]{2,1,0:T(8,128)S(1)} collective-permute-done((f32[4,16,1536]{2,1,0:T(8,128)S(1)}, f32[4,16,1536]{2,1,0:T(8,128)S(1)}, u32[]{:S(2)}, u32[]{:S(2)}) %collective-permute-start.36) | collective-permute-done | bytes 393248 | tf_op jit(solution)/shard_map/ppermute | solution.py:53
  208.9 3.5 %collective-permute-start.30 = (f32[4,16,1536]{2,1,0:T(8,128)S(1)}, f32[4,16,1536]{2,1,0:T(8,128)S(1)}, u32[]{:S(2)}, u32[]{:S(2)}) collective-permute-start(f32[4,16,1536]{2,1,0:T(8,128)S(1)} %pad_maximum_fusion.5.refs_0_), channel_id=1, source_target_pairs={{0,8},{8,0},{1,9},{9,1},{2,10},{10,2},{3,11},{11,3},{4,12},{12,4},... | collective-permute-start | bytes 1179656 | tf_op jit(solution)/shard_map/ppermute | solution.py:41
  212.4 1.3 collective-permute-start.38
  213.7 1.8 collective-permute-start.40
  216.3 2.4 collective-permute-start.31
  218.9 1.8 collective-permute-done.38.refs_11_
  220.7 2.1 collective-permute-start.32
  222.9 1.7 collective-permute-start.33
  227.4 27.2 %update.1 = f32[512,1664]{1,0:T(8,128)} custom-call(s32[64]{0:T(128)} %reshape.197.source, s32[17]{0:T(128)} %pad_add_fusion.1.flags, f32[4,16,1536]{2,1,0:T(8,128)} %copy-done.4, f32[4,16,1536]{2,1,0:T(8,128)} %copy-done.9, f32[4,16,1536]{2,1,0:T(8,128)} %copy-done.10, f32[4,16,1536]{2,1,0:T(8,128)} %copy-done.14, f32[4,16,1536]{2,1,0:T(8,128)} %copy-done.11, ...), custom_call_target="tpu_custom_call" | custom-call | tf_op jit(solution)/shard_map/update/pallas_call | solution.py:274
  (146 shorter events, 13.3 us)
Async XLA Ops:
  6.5 220.8 %all-gather.2.cloned.1.call-start = ((), (), s32[]{:S(2)}) async-start(), calls=%async_computation.1 | async-start | bytes 23003136 | tf_op jit(solution)/shard_map/all_gather | solution.py:228
  14.4 34.2 %all-to-all-start = ((f32[32,14,8,128]{3,2,1,0:T(8,128)}), f32[32,14,8,128]{3,2,1,0:T(8,128)S(1)}, u32[]{:S(2)}, u32[]{:S(2)}) async-start(f32[32,14,8,128]{3,2,1,0:T(8,128)} %pad_maximum_fusion), calls=%async_computation | async-start | bytes 3670016 | tf_op jit(solution)/shard_map/all_to_all | solution.py:236
  48.7 35.0 %copy-start.2 = (f32[32,14,8,128]{3,2,1,0:T(8,128)}, f32[32,14,8,128]{3,2,1,0:T(8,128)S(1)}, u32[]{:S(2)}) copy-start(f32[32,14,8,128]{3,2,1,0:T(8,128)S(1)} %all-to-all-done) | copy-start | bytes 5505028
  49.3 9.6 %collective-permute-start = (f32[21,8,128]{2,1,0:T(8,128)S(1)}, f32[21,8,128]{2,1,0:T(8,128)S(1)}, u32[]{:S(2)}, u32[]{:S(2)}) collective-permute-start(f32[21,8,128]{2,1,0:T(8,128)S(1)} %gather_fusion.1), channel_id=1, source_target_pairs={{0,7},{1,0},{2,1},{3,2},{4,3},{5,4},{6,5},{7,6},{8,15},{9,8},{10,9... | collective-permute-start | bytes 258056 | tf_op jit(solution)/shard_map/ppermute | solution.py:67
  54.9 7.5 %collective-permute-start.3 = (f32[21,8,128]{2,1,0:T(8,128)S(1)}, f32[21,8,128]{2,1,0:T(8,128)S(1)}, u32[]{:S(2)}, u32[]{:S(2)}) collective-permute-start(f32[21,8,128]{2,1,0:T(8,128)S(1)} %gather_fusion.1), channel_id=1, source_target_pairs={{0,1},{1,2},{2,3},{3,4},{4,5},{5,6},{6,7},{7,0},{8,9},{9,10},{10,1... | collective-permute-start | bytes 258056 | tf_op jit(solution)/shard_map/ppermute | solution.py:65
  58.9 7.3 %collective-permute-start.1 = (f32[21,8,128]{2,1,0:T(8,128)S(1)}, f32[21,8,128]{2,1,0:T(8,128)S(1)}, u32[]{:S(2)}, u32[]{:S(2)}) collective-permute-start(f32[21,8,128]{2,1,0:T(8,128)S(1)} %collective-permute-done), channel_id=1, source_target_pairs={{0,7},{1,0},{2,1},{3,2},{4,3},{5,4},{6,5},{7,6},{8,15},{9,8},{10,9... | collective-permute-start | bytes 258056 | tf_op jit(solution)/shard_map/ppermute | solution.py:67
  62.4 7.3 %collective-permute-start.4 = (f32[21,8,128]{2,1,0:T(8,128)S(1)}, f32[21,8,128]{2,1,0:T(8,128)S(1)}, u32[]{:S(2)}, u32[]{:S(2)}) collective-permute-start(f32[21,8,128]{2,1,0:T(8,128)S(1)} %collective-permute-done.3), channel_id=1, source_target_pairs={{0,1},{1,2},{2,3},{3,4},{4,5},{5,6},{6,7},{7,0},{8,9},{9,10},{10,1... | collective-permute-start | bytes 258056 | tf_op jit(solution)/shard_map/ppermute | solution.py:65
  66.1 10.5 %collective-permute-start.2 = (f32[21,8,128]{2,1,0:T(8,128)S(1)}, f32[21,8,128]{2,1,0:T(8,128)S(1)}, u32[]{:S(2)}, u32[]{:S(2)}) collective-permute-start(f32[21,8,128]{2,1,0:T(8,128)S(1)} %collective-permute-done.1), channel_id=1, source_target_pairs={{0,7},{1,0},{2,1},{3,2},{4,3},{5,4},{6,5},{7,6},{8,15},{9,8},{10,9... | collective-permute-start | bytes 258056 | tf_op jit(solution)/shard_map/ppermute | solution.py:67
  69.7 7.0 %collective-permute-start.5 = (f32[21,8,128]{2,1,0:T(8,128)S(1)}, f32[21,8,128]{2,1,0:T(8,128)S(1)}, u32[]{:S(2)}, u32[]{:S(2)}) collective-permute-start(f32[21,8,128]{2,1,0:T(8,128)S(1)} %collective-permute-done.4), channel_id=1, source_target_pairs={{0,1},{1,2},{2,3},{3,4},{4,5},{5,6},{6,7},{7,0},{8,9},{9,10},{10,1... | collective-permute-start | bytes 258056 | tf_op jit(solution)/shard_map/ppermute | solution.py:65
  76.6 6.9 %collective-permute-start.6 = (f32[21,8,128]{2,1,0:T(8,128)S(1)}, f32[21,8,128]{2,1,0:T(8,128)S(1)}, u32[]{:S(2)}, u32[]{:S(2)}) collective-permute-start(f32[21,8,128]{2,1,0:T(8,128)S(1)} %collective-permute-done.5), channel_id=1, source_target_pairs={{0,1},{1,2},{2,3},{3,4},{4,5},{5,6},{6,7},{7,0},{8,9},{9,10},{10,1... | collective-permute-start | bytes 258056 | tf_op jit(solution)/shard_map/ppermute | solution.py:65
  83.7 8.0 %collective-permute-start.16 = (f32[1,11,8,8,128]{4,3,2,1,0:T(8,128)S(1)}, f32[1,11,8,8,128]{4,3,2,1,0:T(8,128)S(1)}, u32[]{:S(2)}, u32[]{:S(2)}) collective-permute-start(f32[1,11,8,8,128]{4,3,2,1,0:T(8,128)S(1)} %slice_bitcast_fusion), channel_id=1, source_target_pairs={{0,16},{8,56},{16,0},{24,40},{32,48},{40,24},{48,32},{56,8},{64,80... | collective-permute-start | bytes 1081352 | tf_op jit(solution)/shard_map/ppermute | solution.py:49
  84.8 7.6 %collective-permute-start.7 = (f32[1,10,8,8,128]{4,3,2,1,0:T(8,128)S(1)}, f32[1,10,8,8,128]{4,3,2,1,0:T(8,128)S(1)}, u32[]{:S(2)}, u32[]{:S(2)}) collective-permute-start(f32[1,10,8,8,128]{4,3,2,1,0:T(8,128)S(1)} %slice_bitcast_fusion.1), channel_id=1, source_target_pairs={{0,64},{8,200},{16,80},{24,216},{32,96},{40,232},{48,112},{56,248}... | collective-permute-start | bytes 983048 | tf_op jit(solution)/shard_map/ppermute | solution.py:49
  91.7 10.6 %collective-permute-start.17 = (f32[2,11,8,8,128]{4,3,2,1,0:T(8,128)S(1)}, f32[2,11,8,8,128]{4,3,2,1,0:T(8,128)S(1)}, u32[]{:S(2)}, u32[]{:S(2)}) collective-permute-start(f32[2,11,8,8,128]{4,3,2,1,0:T(8,128)S(1)} %pad_maximum_fusion.3), channel_id=1, source_target_pairs={{0,192},{8,72},{16,208},{24,88},{32,224},{40,104},{48,240},{56,120... | collective-permute-start | bytes 2162696 | tf_op jit(solution)/shard_map/ppermute | solution.py:49
  92.5 11.5 %collective-permute-start.8 = (f32[2,10,8,8,128]{4,3,2,1,0:T(8,128)S(1)}, f32[2,10,8,8,128]{4,3,2,1,0:T(8,128)S(1)}, u32[]{:S(2)}, u32[]{:S(2)}) collective-permute-start(f32[2,10,8,8,128]{4,3,2,1,0:T(8,128)S(1)} %pad_maximum_fusion.4), channel_id=1, source_target_pairs={{0,16},{8,56},{16,0},{24,40},{32,48},{40,24},{48,32},{56,8},{64,80... | collective-permute-start | bytes 1966088 | tf_op jit(solution)/shard_map/ppermute | solution.py:49
  102.4 44.0 %copy-start = (f32[4,11,8,8,128]{4,3,2,1,0:T(8,128)}, f32[4,11,8,8,128]{4,3,2,1,0:T(8,128)S(1)}, u32[]{:S(2)}) copy-start(f32[4,11,8,8,128]{4,3,2,1,0:T(8,128)S(1)} %pad_maximum_fusion.1.refs_8_) | copy-start | bytes 4325380
  102.5 39.9 %collective-permute-start.18 = (f32[4,11,8,8,128]{4,3,2,1,0:T(8,128)S(1)}, f32[4,11,8,8,128]{4,3,2,1,0:T(8,128)}, u32[]{:S(2)}, u32[]{:S(2)}) collective-permute-start(f32[4,11,8,8,128]{4,3,2,1,0:T(8,128)S(1)} %pad_maximum_fusion.1.refs_8_), channel_id=1, source_target_pairs={{0,48},{8,24},{16,32},{24,8},{32,16},{40,56},{48,0},{56,40},{64,11... | collective-permute-start | bytes 4325384 | tf_op jit(solution)/shard_map/ppermute | solution.py:53
  104.1 66.4 %copy-start.1 = (f32[4,10,8,8,128]{4,3,2,1,0:T(8,128)}, f32[4,10,8,8,128]{4,3,2,1,0:T(8,128)S(1)}, u32[]{:S(2)}) copy-start(f32[4,10,8,8,128]{4,3,2,1,0:T(8,128)S(1)} %pad_maximum_fusion.2.refs_0_) | copy-start | bytes 3932164
  104.1 19.7 %collective-permute-start.9 = (f32[4,10,8,8,128]{4,3,2,1,0:T(8,128)S(1)}, f32[4,10,8,8,128]{4,3,2,1,0:T(8,128)}, u32[]{:S(2)}, u32[]{:S(2)}) collective-permute-start(f32[4,10,8,8,128]{4,3,2,1,0:T(8,128)S(1)} %pad_maximum_fusion.2.refs_0_), channel_id=1, source_target_pairs={{0,192},{8,72},{16,208},{24,88},{32,224},{40,104},{48,240},{56,120... | collective-permute-start | bytes 3932168 | tf_op jit(solution)/shard_map/ppermute | solution.py:53
  106.6 39.9 %collective-permute-start.10 = (f32[4,10,8,8,128]{4,3,2,1,0:T(8,128)S(1)}, f32[4,10,8,8,128]{4,3,2,1,0:T(8,128)}, u32[]{:S(2)}, u32[]{:S(2)}) collective-permute-start(f32[4,10,8,8,128]{4,3,2,1,0:T(8,128)S(1)} %pad_maximum_fusion.2.refs_0_), channel_id=1, source_target_pairs={{0,48},{8,24},{16,32},{24,8},{32,16},{40,56},{48,0},{56,40},{64,11... | collective-permute-start | bytes 3932168 | tf_op jit(solution)/shard_map/ppermute | solution.py:53
  106.7 41.9 %collective-permute-start.12 = (f32[4,10,8,8,128]{4,3,2,1,0:T(8,128)S(1)}, f32[4,10,8,8,128]{4,3,2,1,0:T(8,128)}, u32[]{:S(2)}, u32[]{:S(2)}) collective-permute-start(f32[4,10,8,8,128]{4,3,2,1,0:T(8,128)S(1)} %pad_maximum_fusion.2.refs_0_), channel_id=1, source_target_pairs={{0,8},{8,0},{1,9},{9,1},{2,10},{10,2},{3,11},{11,3},{4,12},{12,4},... | collective-permute-start | bytes 3932168 | tf_op jit(solution)/shard_map/ppermute | solution.py:41
  114.9 33.6 %collective-permute-start.19 = (f32[4,11,8,8,128]{4,3,2,1,0:T(8,128)S(1)}, f32[4,11,8,8,128]{4,3,2,1,0:T(8,128)}, u32[]{:S(2)}, u32[]{:S(2)}) collective-permute-start(f32[4,11,8,8,128]{4,3,2,1,0:T(8,128)S(1)} %pad_maximum_fusion.1.refs_8_), channel_id=1, source_target_pairs={{0,64},{8,200},{16,80},{24,216},{32,96},{40,232},{48,112},{56,248}... | collective-permute-start | bytes 4325384 | tf_op jit(solution)/shard_map/ppermute | solution.py:53
  123.9 25.2 %collective-permute-start.21 = (f32[4,11,8,8,128]{4,3,2,1,0:T(8,128)S(1)}, f32[4,11,8,8,128]{4,3,2,1,0:T(8,128)}, u32[]{:S(2)}, u32[]{:S(2)}) collective-permute-start(f32[4,11,8,8,128]{4,3,2,1,0:T(8,128)S(1)} %pad_maximum_fusion.1.refs_8_), channel_id=1, source_target_pairs={{0,8},{8,0},{1,9},{9,1},{2,10},{10,2},{3,11},{11,3},{4,12},{12,4},... | collective-permute-start | bytes 4325384 | tf_op jit(solution)/shard_map/ppermute | solution.py:41
  142.4 19.7 %collective-permute-start.20 = (f32[4,11,8,8,128]{4,3,2,1,0:T(8,128)}, f32[4,11,8,8,128]{4,3,2,1,0:T(8,128)}, u32[]{:S(2)}, u32[]{:S(2)}) collective-permute-start(f32[4,11,8,8,128]{4,3,2,1,0:T(8,128)} %collective-permute-done.18.refs_9_), channel_id=1, source_target_pairs={{0,64},{8,200},{16,80},{24,216},{32,96},{40,232},{48,112},{56,248}... | collective-permute-start | bytes 4325384 | tf_op jit(solution)/shard_map/ppermute | solution.py:53
  146.5 17.7 %collective-permute-start.11 = (f32[4,10,8,8,128]{4,3,2,1,0:T(8,128)}, f32[4,10,8,8,128]{4,3,2,1,0:T(8,128)}, u32[]{:S(2)}, u32[]{:S(2)}) collective-permute-start(f32[4,10,8,8,128]{4,3,2,1,0:T(8,128)} %collective-permute-done.9.refs_1_), channel_id=1, source_target_pairs={{0,48},{8,24},{16,32},{24,8},{32,16},{40,56},{48,0},{56,40},{64,11... | collective-permute-start | bytes 3932168 | tf_op jit(solution)/shard_map/ppermute | solution.py:53
  148.5 17.1 %collective-permute-start.13 = (f32[4,10,8,8,128]{4,3,2,1,0:T(8,128)}, f32[4,10,8,8,128]{4,3,2,1,0:T(8,128)}, u32[]{:S(2)}, u32[]{:S(2)}) collective-permute-start(f32[4,10,8,8,128]{4,3,2,1,0:T(8,128)} %collective-permute-done.9.refs_1_), channel_id=1, source_target_pairs={{0,8},{8,0},{1,9},{9,1},{2,10},{10,2},{3,11},{11,3},{4,12},{12,4},... | collective-permute-start | bytes 3932168 | tf_op jit(solution)/shard_map/ppermute | solution.py:41
  148.5 20.1 %collective-permute-start.22 = (f32[4,11,8,8,128]{4,3,2,1,0:T(8,128)}, f32[4,11,8,8,128]{4,3,2,1,0:T(8,128)}, u32[]{:S(2)}, u32[]{:S(2)}) collective-permute-start(f32[4,11,8,8,128]{4,3,2,1,0:T(8,128)} %collective-permute-done.18.refs_9_), channel_id=1, source_target_pairs={{0,8},{8,0},{1,9},{9,1},{2,10},{10,2},{3,11},{11,3},{4,12},{12,4},... | collective-permute-start | bytes 4325384 | tf_op jit(solution)/shard_map/ppermute | solution.py:41
  149.0 19.6 %collective-permute-start.23 = (f32[4,11,8,8,128]{4,3,2,1,0:T(8,128)}, f32[4,11,8,8,128]{4,3,2,1,0:T(8,128)S(1)}, u32[]{:S(2)}, u32[]{:S(2)}) collective-permute-start(f32[4,11,8,8,128]{4,3,2,1,0:T(8,128)} %collective-permute-done.19.refs_10_), channel_id=1, source_target_pairs={{0,8},{8,0},{1,9},{9,1},{2,10},{10,2},{3,11},{11,3},{4,12},{12,4},... | collective-permute-start | bytes 4325384 | tf_op jit(solution)/shard_map/ppermute | solution.py:41
  162.1 8.4 %collective-permute-start.24 = (f32[4,11,8,8,128]{4,3,2,1,0:T(8,128)}, f32[4,11,8,8,128]{4,3,2,1,0:T(8,128)}, u32[]{:S(2)}, u32[]{:S(2)}) collective-permute-start(f32[4,11,8,8,128]{4,3,2,1,0:T(8,128)} %collective-permute-done.20.refs_11_), channel_id=1, source_target_pairs={{0,8},{8,0},{1,9},{9,1},{2,10},{10,2},{3,11},{11,3},{4,12},{12,4},... | collective-permute-start | bytes 4325384 | tf_op jit(solution)/shard_map/ppermute | solution.py:41
  164.1 4.5 %collective-permute-start.14 = (f32[4,10,8,8,128]{4,3,2,1,0:T(8,128)}, f32[4,10,8,8,128]{4,3,2,1,0:T(8,128)}, u32[]{:S(2)}, u32[]{:S(2)}) collective-permute-start(f32[4,10,8,8,128]{4,3,2,1,0:T(8,128)} %collective-permute-done.10.refs_2_), channel_id=1, source_target_pairs={{0,8},{8,0},{1,9},{9,1},{2,10},{10,2},{3,11},{11,3},{4,12},{12,4},... | collective-permute-start | bytes 3932168 | tf_op jit(solution)/shard_map/ppermute | solution.py:41
  165.6 4.9 %collective-permute-start.15 = (f32[4,10,8,8,128]{4,3,2,1,0:T(8,128)}, f32[4,10,8,8,128]{4,3,2,1,0:T(8,128)}, u32[]{:S(2)}, u32[]{:S(2)}) collective-permute-start(f32[4,10,8,8,128]{4,3,2,1,0:T(8,128)} %collective-permute-done.11.refs_3_), channel_id=1, source_target_pairs={{0,8},{8,0},{1,9},{9,1},{2,10},{10,2},{3,11},{11,3},{4,12},{12,4},... | collective-permute-start | bytes 3932168 | tf_op jit(solution)/shard_map/ppermute | solution.py:41
  189.1 5.4 %collective-permute-start.34 = (f32[1,16,1536]{2,1,0:T(8,128)}, f32[1,16,1536]{2,1,0:T(8,128)S(1)}, u32[]{:S(2)}, u32[]{:S(2)}) collective-permute-start(f32[1,16,1536]{2,1,0:T(8,128)} %bitcast.69), channel_id=1, source_target_pairs={{0,16},{8,56},{16,0},{24,40},{32,48},{40,24},{48,32},{56,8},{64,80... | collective-permute-start | bytes 294920 | tf_op jit(solution)/shard_map/ppermute | solution.py:49
  189.2 8.0 %collective-permute-start.25 = (f32[1,16,1536]{2,1,0:T(8,128)}, f32[1,16,1536]{2,1,0:T(8,128)S(1)}, u32[]{:S(2)}, u32[]{:S(2)}) collective-permute-start(f32[1,16,1536]{2,1,0:T(8,128)} %bitcast.66), channel_id=1, source_target_pairs={{0,64},{8,200},{16,80},{24,216},{32,96},{40,232},{48,112},{56,248}... | collective-permute-start | bytes 294920 | tf_op jit(solution)/shard_map/ppermute | solution.py:49
  195.4 5.3 %collective-permute-start.35 = (f32[2,16,1536]{2,1,0:T(8,128)S(1)}, f32[2,16,1536]{2,1,0:T(8,128)S(1)}, u32[]{:S(2)}, u32[]{:S(2)}) collective-permute-start(f32[2,16,1536]{2,1,0:T(8,128)S(1)} %pad_maximum_fusion.8), channel_id=1, source_target_pairs={{0,192},{8,72},{16,208},{24,88},{32,224},{40,104},{48,240},{56,120... | collective-permute-start | bytes 589832 | tf_op jit(solution)/shard_map/ppermute | solution.py:49
  198.1 6.3 %collective-permute-start.26 = (f32[2,16,1536]{2,1,0:T(8,128)S(1)}, f32[2,16,1536]{2,1,0:T(8,128)S(1)}, u32[]{:S(2)}, u32[]{:S(2)}) collective-permute-start(f32[2,16,1536]{2,1,0:T(8,128)S(1)} %pad_maximum_fusion.7), channel_id=1, source_target_pairs={{0,16},{8,56},{16,0},{24,40},{32,48},{40,24},{48,32},{56,8},{64,80... | collective-permute-start | bytes 589832 | tf_op jit(solution)/shard_map/ppermute | solution.py:49
  201.6 7.3 %collective-permute-start.36 = (f32[4,16,1536]{2,1,0:T(8,128)S(1)}, f32[4,16,1536]{2,1,0:T(8,128)S(1)}, u32[]{:S(2)}, u32[]{:S(2)}) collective-permute-start(f32[4,16,1536]{2,1,0:T(8,128)S(1)} %pad_maximum_fusion.6.refs_8_), channel_id=1, source_target_pairs={{0,48},{8,24},{16,32},{24,8},{32,16},{40,56},{48,0},{56,40},{64,11... | collective-permute-start | bytes 1179656 | tf_op jit(solution)/shard_map/ppermute | solution.py:53
  201.9 10.5 %collective-permute-start.37 = (f32[4,16,1536]{2,1,0:T(8,128)S(1)}, f32[4,16,1536]{2,1,0:T(8,128)S(1)}, u32[]{:S(2)}, u32[]{:S(2)}) collective-permute-start(f32[4,16,1536]{2,1,0:T(8,128)S(1)} %pad_maximum_fusion.6.refs_8_), channel_id=1, source_target_pairs={{0,64},{8,200},{16,80},{24,216},{32,96},{40,232},{48,112},{56,248}... | collective-permute-start | bytes 1179656 | tf_op jit(solution)/shard_map/ppermute | solution.py:53
  203.4 10.3 %collective-permute-start.39 = (f32[4,16,1536]{2,1,0:T(8,128)S(1)}, f32[4,16,1536]{2,1,0:T(8,128)S(1)}, u32[]{:S(2)}, u32[]{:S(2)}) collective-permute-start(f32[4,16,1536]{2,1,0:T(8,128)S(1)} %pad_maximum_fusion.6.refs_8_), channel_id=1, source_target_pairs={{0,8},{8,0},{1,9},{9,1},{2,10},{10,2},{3,11},{11,3},{4,12},{12,4},... | collective-permute-start | bytes 1179656 | tf_op jit(solution)/shard_map/ppermute | solution.py:41
  204.4 11.1 %collective-permute-start.27 = (f32[4,16,1536]{2,1,0:T(8,128)S(1)}, f32[4,16,1536]{2,1,0:T(8,128)S(1)}, u32[]{:S(2)}, u32[]{:S(2)}) collective-permute-start(f32[4,16,1536]{2,1,0:T(8,128)S(1)} %pad_maximum_fusion.5.refs_0_), channel_id=1, source_target_pairs={{0,192},{8,72},{16,208},{24,88},{32,224},{40,104},{48,240},{56,120... | collective-permute-start | bytes 1179656 | tf_op jit(solution)/shard_map/ppermute | solution.py:53
  205.4 10.9 %collective-permute-start.28 = (f32[4,16,1536]{2,1,0:T(8,128)S(1)}, f32[4,16,1536]{2,1,0:T(8,128)S(1)}, u32[]{:S(2)}, u32[]{:S(2)}) collective-permute-start(f32[4,16,1536]{2,1,0:T(8,128)S(1)} %pad_maximum_fusion.5.refs_0_), channel_id=1, source_target_pairs={{0,48},{8,24},{16,32},{24,8},{32,16},{40,56},{48,0},{56,40},{64,11... | collective-permute-start | bytes 1179656 | tf_op jit(solution)/shard_map/ppermute | solution.py:53
  208.9 9.8 %collective-permute-start.30 = (f32[4,16,1536]{2,1,0:T(8,128)S(1)}, f32[4,16,1536]{2,1,0:T(8,128)S(1)}, u32[]{:S(2)}, u32[]{:S(2)}) collective-permute-start(f32[4,16,1536]{2,1,0:T(8,128)S(1)} %pad_maximum_fusion.5.refs_0_), channel_id=1, source_target_pairs={{0,8},{8,0},{1,9},{9,1},{2,10},{10,2},{3,11},{11,3},{4,12},{12,4},... | collective-permute-start | bytes 1179656 | tf_op jit(solution)/shard_map/ppermute | solution.py:41
  212.4 8.2 %collective-permute-start.38 = (f32[4,16,1536]{2,1,0:T(8,128)S(1)}, f32[4,16,1536]{2,1,0:T(8,128)S(1)}, u32[]{:S(2)}, u32[]{:S(2)}) collective-permute-start(f32[4,16,1536]{2,1,0:T(8,128)S(1)} %collective-permute-done.36.refs_9_), channel_id=1, source_target_pairs={{0,64},{8,200},{16,80},{24,216},{32,96},{40,232},{48,112},{56,248}... | collective-permute-start | bytes 1179656 | tf_op jit(solution)/shard_map/ppermute | solution.py:53
  213.7 9.1 %collective-permute-start.40 = (f32[4,16,1536]{2,1,0:T(8,128)S(1)}, f32[4,16,1536]{2,1,0:T(8,128)S(1)}, u32[]{:S(2)}, u32[]{:S(2)}) collective-permute-start(f32[4,16,1536]{2,1,0:T(8,128)S(1)} %collective-permute-done.36.refs_9_), channel_id=1, source_target_pairs={{0,8},{8,0},{1,9},{9,1},{2,10},{10,2},{3,11},{11,3},{4,12},{12,4},... | collective-permute-start | bytes 1179656 | tf_op jit(solution)/shard_map/ppermute | solution.py:41
  215.5 7.4 %collective-permute-start.29 = (f32[4,16,1536]{2,1,0:T(8,128)S(1)}, f32[4,16,1536]{2,1,0:T(8,128)S(1)}, u32[]{:S(2)}, u32[]{:S(2)}) collective-permute-start(f32[4,16,1536]{2,1,0:T(8,128)S(1)} %collective-permute-done.27.refs_1_), channel_id=1, source_target_pairs={{0,48},{8,24},{16,32},{24,8},{32,16},{40,56},{48,0},{56,40},{64,11... | collective-permute-start | bytes 1179656 | tf_op jit(solution)/shard_map/ppermute | solution.py:53
  216.3 8.3 %collective-permute-start.31 = (f32[4,16,1536]{2,1,0:T(8,128)S(1)}, f32[4,16,1536]{2,1,0:T(8,128)S(1)}, u32[]{:S(2)}, u32[]{:S(2)}) collective-permute-start(f32[4,16,1536]{2,1,0:T(8,128)S(1)} %collective-permute-done.27.refs_1_), channel_id=1, source_target_pairs={{0,8},{8,0},{1,9},{9,1},{2,10},{10,2},{3,11},{11,3},{4,12},{12,4},... | collective-permute-start | bytes 1179656 | tf_op jit(solution)/shard_map/ppermute | solution.py:41
  218.8 5.8 %collective-permute-start.41 = (f32[4,16,1536]{2,1,0:T(8,128)S(1)}, f32[4,16,1536]{2,1,0:T(8,128)S(1)}, u32[]{:S(2)}, u32[]{:S(2)}) collective-permute-start(f32[4,16,1536]{2,1,0:T(8,128)S(1)} %collective-permute-done.37.refs_10_), channel_id=1, source_target_pairs={{0,8},{8,0},{1,9},{9,1},{2,10},{10,2},{3,11},{11,3},{4,12},{12,4},... | collective-permute-start | bytes 1179656 | tf_op jit(solution)/shard_map/ppermute | solution.py:41
  220.7 4.0 %collective-permute-start.32 = (f32[4,16,1536]{2,1,0:T(8,128)S(1)}, f32[4,16,1536]{2,1,0:T(8,128)S(1)}, u32[]{:S(2)}, u32[]{:S(2)}) collective-permute-start(f32[4,16,1536]{2,1,0:T(8,128)S(1)} %collective-permute-done.28.refs_2_), channel_id=1, source_target_pairs={{0,8},{8,0},{1,9},{9,1},{2,10},{10,2},{3,11},{11,3},{4,12},{12,4},... | collective-permute-start | bytes 1179656 | tf_op jit(solution)/shard_map/ppermute | solution.py:41
  222.8 1.9 collective-permute-start.42
  222.9 3.5 %collective-permute-start.33 = (f32[4,16,1536]{2,1,0:T(8,128)S(1)}, f32[4,16,1536]{2,1,0:T(8,128)}, u32[]{:S(2)}, u32[]{:S(2)}) collective-permute-start(f32[4,16,1536]{2,1,0:T(8,128)S(1)} %collective-permute-done.29.refs_3_), channel_id=1, source_target_pairs={{0,8},{8,0},{1,9},{9,1},{2,10},{10,2},{3,11},{11,3},{4,12},{12,4},... | collective-permute-start | bytes 1179656 | tf_op jit(solution)/shard_map/ppermute | solution.py:41
  (25 other events, 238.7 us)
Sparse Core Ops, SparseCore 0:
  9.1 218.1 all-gather.1
